TPU v7x, 32 devices: a whole 2x2x4 slice. The times are simulated.
32 devices in a mesh: row: 8 (over z, x), col: 4 (over y, core).
Axes of the slice: x: 2, y: 2, z: 4, core: 2. Of those that a mesh axis runs over, the one named last changes fastest.
Arguments:
- fine_coeffs: float32 [512, 4096], P(('row', 'col')), may hold values from -6 to 6
- fine_slot: int32 [512], P(('row', 'col')), may hold values from 0 to 511, as said below
- neighbours: int32 [64, 6], P('row'), may hold values from -1 to 63, as said below
- filter_matrix: float32 [32, 32], replicated, may hold values from -1 to 1
- kernel_ops: float32 [20, 3, 3, 1024], replicated, may hold values from -0.625 to 0.625
Outputs:
- fine_result: float32 [512, 4096], P(('row', 'col'))
Inputs may be any that keep to these rules, and one draw needn't show every extreme that they name: `fine_slot`: every value appears once. Run r holds the parents r * 8 to (r + 1) * 8 - 1. A fine box on a device with col index c has its parent in the c-th block of 2 consecutive parents of the parent's run. Of the 16 fine boxes of one device, at most 4 have parents in one run, and some device has exactly 4 in some run. -1 where the grid of parents ends. neighbours[neighbours[p, d], d XOR 1] = p. For a parent of run r, the neighbours in directions 0, 2, 4 lie in run (r + 1) mod 8 and those in directions 1, 3, 5 in run (r - 1) mod 8.
All inputs are finite; a program needn't handle non-finite values.
Results may differ from a plain program's by a relative error of at most 0.0001.
Values sent between devices are 32-bit elements; how exact they have to be, the bound alone decides.
No kernel may reach another device: no remote copies, remote signals or barrier semaphores. Data moves between devices by JAX's collectives and lax.ppermute only.
A program may use at most 64 MiB of HBM per device.

v0:
```python
import jax
import jax.numpy as jnp
import numpy as np
from jax import lax
from jax.sharding import PartitionSpec as P

exact_mode = lax.Precision.HIGHEST
offset_order = np.array([1, 2, 0])


def shifted(array, axis, by):
    peers = lax.axis_size(axis)
    return lax.ppermute(array, axis, [(i, (i + by) % peers) for i in range(peers)])


def rotate_batch(blocks, matrices):
    breadth = matrices.shape[-1]
    viewed = blocks.reshape(blocks.shape[:2] + (-1, breadth))
    result = jnp.einsum("ekc,enmc->enkm", matrices, viewed, precision=exact_mode)
    return result.reshape(blocks.shape[:2] + (-1,))


def rotate_single(blocks, matrix):
    breadth = matrix.shape[-1]
    viewed = blocks.reshape(blocks.shape[:-1] + (-1, breadth))
    result = jnp.einsum("kc,...mc->...km", matrix, viewed, precision=exact_mode)
    return result.reshape(blocks.shape[:-1] + (-1,))


def rotate_many(blocks, matrices):
    breadth = matrices.shape[-1]
    viewed = blocks.reshape(blocks.shape[:1] + (-1, breadth))
    result = jnp.einsum("ekc,nmc->enkm", matrices, viewed, precision=exact_mode)
    return result.reshape((matrices.shape[0], blocks.shape[0], -1))


def octant_tables(pieces):
    octants = np.arange(8)
    return (pieces[octants % 2], pieces[octants // 2 % 2], pieces[octants // 4])


def filter_children(children, filter_matrix):
    breadth = filter_matrix.shape[0]
    pieces = jnp.transpose(filter_matrix.reshape(breadth, 2, breadth // 2), (1, 0, 2))
    along_z, along_y, along_x = octant_tables(pieces)
    sectioned = rotate_batch(children, along_z)
    sectioned = rotate_batch(sectioned, along_y)
    sectioned = rotate_batch(sectioned, along_x)
    return jnp.sum(sectioned, axis=0)


def unfilter_blocks(applied, filter_matrix):
    breadth = filter_matrix.shape[0]
    pieces = jnp.transpose(filter_matrix.reshape(breadth, 2, breadth // 2), (1, 2, 0))
    along_z, along_y, along_x = octant_tables(pieces)
    sectioned = rotate_many(applied, along_z)
    sectioned = rotate_batch(sectioned, along_y)
    return rotate_batch(sectioned, along_x)


def displaced(filtered, kernel_ops):
    amount = filtered.shape[0]
    volume = filtered.shape[1]

    def one_term(totals, factors):
        first_section = rotate_many(filtered, factors[2])
        mid_centre = rotate_many(first_section[1], factors[1][offset_order])
        mid_sides = rotate_single(first_section[np.array([2, 0])], factors[1, 1])
        last_centre = rotate_many(mid_centre[0], factors[0][offset_order])
        last_mid = rotate_single(mid_centre[1:], factors[0, 1])
        last_sides = rotate_single(mid_sides, factors[0, 1])
        return ((totals[0] + last_centre, totals[1] + last_mid, totals[2] + last_sides), None)

    initial = (
        jnp.zeros((3, amount, volume), jnp.float32),
        jnp.zeros((2, amount, volume), jnp.float32),
        jnp.zeros((2, amount, volume), jnp.float32),
    )
    totals, unused = lax.scan(one_term, initial, kernel_ops)
    return totals


def incoming_weights(neighbours, col_index, source_count, first_dir):
    par_row = neighbours.shape[0]
    slot_iota = jnp.arange(source_count)
    tables = []
    for axis_index in range(3):
        sender = neighbours[:, 2 * axis_index + first_dir]
        within = sender % par_row
        owned_here = (sender >= 0) & (within // source_count == col_index)
        picked = owned_here[:, None] & (
            (within - col_index * source_count)[:, None] == slot_iota[None, :]
        )
        tables.append(picked.astype(jnp.float32))
    return tables


def weighted_rows(tables, block_sets):
    summed = None
    for weight_table, block_set in zip(tables, block_sets):
        product = jnp.dot(weight_table, block_set, precision=exact_mode)
        summed = product if summed is None else summed + product
    return summed


def local(fine_coeffs, fine_slot, neighbours, filter_matrix, kernel_ops):
    breadth = filter_matrix.shape[0]
    factor_set = kernel_ops.reshape(kernel_ops.shape[:3] + (breadth, breadth))
    row_count = lax.axis_size("row")
    held_boxes = fine_coeffs.shape[0]
    volume = fine_coeffs.shape[1]
    par_row = neighbours.shape[0]
    source_count = held_boxes // 8
    capacity = 2 * (held_boxes // row_count)
    col_index = lax.axis_index("col")
    dest_row = fine_slot // (8 * par_row)
    row_hits = (dest_row[:, None] == jnp.arange(row_count)[None, :]).astype(jnp.int32)
    before = jnp.cumsum(row_hits, axis=0) - row_hits
    slot_index = dest_row * capacity + jnp.sum(before * row_hits, axis=1)
    packer = jnp.arange(row_count * capacity)[:, None] == slot_index[None, :]
    send_blocks = jnp.dot(packer.astype(jnp.float32), fine_coeffs, precision=exact_mode)
    send_ids = jnp.max(jnp.where(packer, fine_slot[None, :], -1), axis=1)
    got_blocks, got_ids = (
        lax.all_to_all(
            send_blocks.reshape(row_count, capacity, volume),
            "row",
            split_axis=0,
            concat_axis=0,
            tiled=True,
        ),
        lax.all_to_all(
            send_ids.reshape(row_count, capacity), "row", split_axis=0, concat_axis=0, tiled=True
        ),
    )
    got_ids = got_ids.reshape(-1)
    child_pos = got_ids % held_boxes
    position = child_pos % 8 * source_count + child_pos // 8
    picker = (
        (position[None, :] == jnp.arange(held_boxes)[:, None]) & (got_ids[None, :] >= 0)
    ).astype(jnp.float32)
    children = jnp.dot(picker, got_blocks.reshape(-1, volume), precision=exact_mode)
    filtered = filter_children(children.reshape(8, source_count, volume), filter_matrix)
    centre, middle, side_terms = displaced(filtered, factor_set)
    from_below = shifted((centre[1], middle[0], side_terms[0]), "row", 1)
    from_above = shifted((centre[2], middle[1], side_terms[1]), "row", -1)
    below_tables = incoming_weights(neighbours, col_index, source_count, 1)
    above_tables = incoming_weights(neighbours, col_index, source_count, 0)
    applied = centre[0] + lax.psum_scatter(
        weighted_rows(below_tables, from_below) + weighted_rows(above_tables, from_above),
        "col",
        scatter_dimension=0,
        tiled=True,
    )
    results = unfilter_blocks(applied, filter_matrix).reshape(held_boxes, volume)
    back_blocks = jnp.einsum("ab,ac->bc", picker, results, precision=exact_mode)
    returned = lax.all_to_all(
        back_blocks.reshape(row_count, capacity, volume),
        "row",
        split_axis=0,
        concat_axis=0,
        tiled=True,
    )
    return jnp.einsum(
        "ab,ac->bc", packer.astype(jnp.float32), returned.reshape(-1, volume), precision=exact_mode
    )


def solution(mesh):
    in_specs = (P(("row", "col"), None), P(("row", "col")), P("row", None), P(), P())
    out_specs = P(("row", "col"), None)
    return jax.shard_map(local, mesh=mesh, in_specs=in_specs, out_specs=out_specs, check_vma=False)
```

profile of v0, /device:TPU:0, one launch (start us, length us, event | category | flops | bytes accessed | tf_op | source)
XLA Modules:
  0.0 807.4 jit_solution(7139673797954579719)
XLA Ops:
  9.7 7.3 all-to-all-start
  19.1 4.3 all-to-all-done
  23.4 3.5 all-to-all-start.1
  32.3 2.6 reshape.230
  42.9 2.6 reshape_reshape.16
  45.6 6.7 convolution_bitcast_fusion.6
  52.3 4.9 reshape_reshape.17
  57.2 10.5 %convolution_bitcast_fusion.8 = f32[1,2,32,1024]{3,2,1,0:T(8,128)S(1)} fusion(f32[8,2,1024,16]{3,2,1,0:T(8,128)} %reshape_reshape.17, f32[8,32,16]{1,2,0:T(8,128)S(1)} %gather_fusion.5), kind=kOutput, calls=%fused_computation.45 | convolution fusion | flops 100663296 | bytes 1327104 | tf_op jit(solution)/shard_map/ekc,enmc->enkm/dot_general | solution.py:19
  68.6 618.9 %while.17 = (s32[]{:T(128)}, f32[3,2,32768]{2,1,0:T(2,128)}, f32[2,2,32768]{2,1,0:T(2,128)}, f32[2,2,32768]{2,1,0:T(2,128)}, f32[20,3,3,32,32]{4,3,0,2,1:T(8,128...) while((s32[]{:T(128)}, f32[3,2,32768]{2,1,0:T(2,128)}, ...), condition=%wide.region_4.5_spmd.clone.clone.clone, body=%wide.region_3.4_spmd.sunk.clone.clone.clone.sunk | while | flops 378406912 | bytes 42086876 | solution.py:79
  78.6 3.1 fusion.134
  88.9 2.3 convolution_bitcast_fusion.19
  107.9 3.1 fusion.134
  118.2 2.3 convolution_bitcast_fusion.19
  121.0 2.9 select_add_fusion.6
  138.4 3.1 fusion.134
  151.5 2.9 select_add_fusion.6
  168.9 3.1 fusion.134
  179.2 2.3 convolution_bitcast_fusion.19
  182.0 2.9 select_add_fusion.6
  199.4 3.1 fusion.134
  212.5 2.9 select_add_fusion.6
  229.9 3.1 fusion.134
  243.0 2.9 select_add_fusion.6
  260.4 3.1 fusion.134
  273.5 2.9 select_add_fusion.6
  290.9 3.1 fusion.134
  301.2 2.3 convolution_bitcast_fusion.19
  304.0 2.9 select_add_fusion.6
  321.4 3.1 fusion.134
  334.5 2.9 select_add_fusion.6
  351.9 3.1 fusion.134
  365.0 2.9 select_add_fusion.6
  382.4 3.1 fusion.134
  392.8 2.3 convolution_bitcast_fusion.19
  395.5 2.9 select_add_fusion.6
  413.0 3.1 fusion.134
  426.0 2.9 select_add_fusion.6
  443.5 3.1 fusion.134
  456.6 2.9 select_add_fusion.6
  474.0 3.1 fusion.134
  484.3 2.3 convolution_bitcast_fusion.19
  487.1 2.9 select_add_fusion.6
  504.5 3.1 fusion.134
  517.6 2.9 select_add_fusion.6
  535.0 3.1 fusion.134
  548.1 2.9 select_add_fusion.6
  565.5 3.1 fusion.134
  575.8 2.3 convolution_bitcast_fusion.19
  578.6 2.9 select_add_fusion.6
  596.0 3.1 fusion.134
  609.1 2.9 select_add_fusion.6
  626.5 3.1 fusion.134
  639.6 2.9 select_add_fusion.6
  657.0 3.1 fusion.134
  667.4 2.3 convolution_bitcast_fusion.19
  670.1 2.9 select_add_fusion.6
  688.7 4.3 collective-permute-start.4
  696.8 2.4 collective-permute-start.2
  701.1 19.1 %collective-permute-done.5 = f32[2,32768]{1,0:T(2,128)S(1)} collective-permute-done((f32[2,32768]{1,0:T(2,128)S(1)}, f32[2,32768]{1,0:T(2,128)S(1)}, u32[]{:S(2)}, u32[]{:S(2)}) %collective-permute-start.5) | collective-permute-done | bytes 262176 | tf_op jit(solution)/shard_map/ppermute | solution.py:13
  720.9 2.3 collective-permute-done.3
  727.2 37.9 %all-reduce.3.cloned.1.call-done = f32[8,32768]{1,0:T(8,128)} async-done(((f32[8,32768]{1,0:T(8,128)}), f32[8,32768]{1,0:T(8,128)}) %all-reduce.3.cloned.1.call-update) | async-done | bytes 1048592
  768.1 2.7 reshape.382
  770.8 5.9 fusion.15
  780.0 19.2 %all_to_all.19 = f32[8,4,4096]{2,1,0:T(4,128)S(1)} all-to-all(f32[8,4,4096]{2,1,0:T(4,128)S(1)} %fusion.30), channel_id=1, replica_groups=mesh['row'=8,'col'=4] {'row'}, dimensions={0} | all-to-all | bytes 1048576 | tf_op jit(solution)/shard_map/all_to_all | solution.py:156
  (957 shorter events, 506.3 us)
Async XLA Ops:
  6.5 10.5 %copy-start = (f32[16,4096]{1,0:T(8,128)S(1)}, f32[16,4096]{1,0:T(8,128)}, u32[]{:S(2)}) copy-start(f32[16,4096]{1,0:T(8,128)} %param.24) | copy-start | bytes 786436
  6.5 20.4 %copy-start.32 = (s32[8]{0:T(128)S(1)}, s32[8]{0:T(128)}, u32[]{:S(2)}) copy-start(s32[8]{0:T(128)} %constant.197) | copy-start | bytes 100
  6.5 24.0 %copy-start.31 = (s32[8]{0:T(128)S(1)}, s32[8]{0:T(128)}, u32[]{:S(2)}) copy-start(s32[8]{0:T(128)} %constant.198) | copy-start | bytes 100
  6.5 20.5 %copy-start.13 = (f32[32,32]{1,0:T(8,128)S(1)}, f32[32,32]{1,0:T(8,128)}, u32[]{:S(2)}) copy-start(f32[32,32]{1,0:T(8,128)} %param.27) | copy-start | bytes 12292
  6.5 25.8 %copy-start.6 = (f32[20,3,3,1024]{3,0,2,1:T(8,128)S(1)}, f32[20,3,3,1024]{3,0,2,1:T(8,128)}, u32[]{:S(2)}) copy-start(f32[20,3,3,1024]{3,0,2,1:T(8,128)} %param.28) | copy-start | bytes 2211844
  8.3 8.7 %copy-start.29 = (s32[16]{0:T(128)}, s32[16]{0:T(128)S(1)}, u32[]{:S(2)}) copy-start(s32[16]{0:T(128)S(1)} %multiply_add_fusion.1) | copy-start | bytes 196
  9.7 13.7 %all-to-all-start = ((s32[8,1,4]{2,1,0:T(1,128)}), s32[8,1,4]{2,1,0:T(1,128)S(1)}, u32[]{:S(2)}, u32[]{:S(2)}) async-start(s32[8,1,4]{2,1,0:T(1,128)} %bitcast), calls=%async_computation | async-start | bytes 8192 | tf_op jit(solution)/shard_map/all_to_all | solution.py:131
  23.4 16.8 %all-to-all-start.1 = ((f32[8,4,4096]{2,1,0:T(4,128)}), f32[8,4,4096]{2,1,0:T(4,128)S(1)}, u32[]{:S(2)}, u32[]{:S(2)}) async-start(f32[8,4,4096]{2,1,0:T(4,128)} %reshape.232), calls=%async_computation.1 | async-start | bytes 1048576 | tf_op jit(solution)/shard_map/all_to_all | solution.py:124
  26.9 738.2 %all-reduce.3.cloned.1.call-start = ((), (), s32[]{:S(2)}) async-start(), calls=%async_computation.3 | async-start | bytes 2097152
  30.6 4.4 copy-start.33
  30.6 5.6 copy-start.7
  57.2 11.4 %copy-start.14 = (s32[3]{0:T(128)S(1)}, s32[3]{0:T(128)}, u32[]{:S(2)}) copy-start(s32[3]{0:T(128)} %constant.421) | copy-start | bytes 40
  120.9 3.0 slice-start
  120.9 3.3 copy-start.5
  151.4 3.0 slice-start
  151.5 3.3 copy-start.5
  181.9 3.0 slice-start
  182.0 3.3 copy-start.5
  212.5 3.0 slice-start
  212.5 3.3 copy-start.5
  243.0 3.0 slice-start
  243.0 3.3 copy-start.5
  273.5 3.0 slice-start
  273.5 3.3 copy-start.5
  304.0 3.0 slice-start
  304.0 3.3 copy-start.5
  334.5 3.0 slice-start
  334.5 3.3 copy-start.5
  365.0 3.0 slice-start
  365.0 3.3 copy-start.5
  395.5 3.0 slice-start
  395.5 3.3 copy-start.5
  426.0 3.0 slice-start
  426.0 3.3 copy-start.5
  456.5 3.0 slice-start
  456.5 3.3 copy-start.5
  487.0 3.0 slice-start
  487.1 3.3 copy-start.5
  517.6 3.0 slice-start
  517.6 3.3 copy-start.5
  548.1 3.3 copy-start.5
  578.6 3.0 slice-start
  578.6 3.3 copy-start.5
  609.1 3.0 slice-start
  609.1 3.3 copy-start.5
  639.6 3.3 copy-start.5
  670.1 3.3 copy-start.5
  687.5 7.2 copy-start.4
  687.5 13.0 %copy-start.26 = (s32[8]{0:T(128)S(1)}, s32[8]{0:T(128)}, u32[]{:S(2)}) copy-start(s32[8]{0:T(128)} %get-tuple-element.174) | copy-start | bytes 100
  687.5 13.0 %copy-start.28 = (pred[8]{0:T(512)(128)(4,1)S(1)}, pred[8]{0:T(512)(128)(4,1)}, u32[]{:S(2)}) copy-start(pred[8]{0:T(512)(128)(4,1)} %get-tuple-element.169) | copy-start | bytes 28
  687.5 32.7 %copy-start.24 = (s32[8]{0:T(128)S(1)}, s32[8]{0:T(128)}, u32[]{:S(2)}) copy-start(s32[8]{0:T(128)} %get-tuple-element.175) | copy-start | bytes 100
  687.5 32.7 %copy-start.27 = (pred[8]{0:T(512)(128)(4,1)S(1)}, pred[8]{0:T(512)(128)(4,1)}, u32[]{:S(2)}) copy-start(pred[8]{0:T(512)(128)(4,1)} %get-tuple-element.168) | copy-start | bytes 28
  688.7 11.0 %collective-permute-start.4 = (f32[2,32768]{1,0:T(2,128)S(1)}, f32[2,32768]{1,0:T(2,128)S(1)}, u32[]{:S(2)}, u32[]{:S(2)}) collective-permute-start(f32[2,32768]{1,0:T(2,128)S(1)} %get-tuple-element.197), channel_id=1, source_target_pairs={{0,28},{4,0},{8,4},{12,8},{16,12},{20,16},{24,20},{28,24},{1,29},{... | collective-permute-start | bytes 786440 | tf_op jit(solution)/shard_map/ppermute | solution.py:13
  694.1 29.1 %copy-start.23 = (s32[8]{0:T(128)S(1)}, s32[8]{0:T(128)}, u32[]{:S(2)}) copy-start(s32[8]{0:T(128)} %get-tuple-element.173) | copy-start | bytes 100
  694.1 29.1 %copy-start.25 = (pred[8]{0:T(512)(128)(4,1)S(1)}, pred[8]{0:T(512)(128)(4,1)}, u32[]{:S(2)}) copy-start(pred[8]{0:T(512)(128)(4,1)} %get-tuple-element.165) | copy-start | bytes 28
  694.1 26.1 %collective-permute-start.5 = (f32[2,32768]{1,0:T(2,128)S(1)}, f32[2,32768]{1,0:T(2,128)S(1)}, u32[]{:S(2)}, u32[]{:S(2)}) collective-permute-start(f32[2,32768]{1,0:T(2,128)S(1)} %get-tuple-element.199), channel_id=1, source_target_pairs={{0,28},{4,0},{8,4},{12,8},{16,12},{20,16},{24,20},{28,24},{1,29},{... | collective-permute-start | bytes 786440 | tf_op jit(solution)/shard_map/ppermute | solution.py:13
  694.8 28.4 %collective-permute-start.3 = (f32[2,32768]{1,0:T(2,128)S(1)}, f32[2,32768]{1,0:T(2,128)S(1)}, u32[]{:S(2)}, u32[]{:S(2)}) collective-permute-start(f32[2,32768]{1,0:T(2,128)S(1)} %get-tuple-element.195), channel_id=1, source_target_pairs={{0,28},{4,0},{8,4},{12,8},{16,12},{20,16},{24,20},{28,24},{1,29},{... | collective-permute-start | bytes 786440 | tf_op jit(solution)/shard_map/ppermute | solution.py:13
  696.3 27.6 %collective-permute-start.1 = (f32[2,32768]{1,0:T(2,128)S(1)}, f32[2,32768]{1,0:T(2,128)S(1)}, u32[]{:S(2)}, u32[]{:S(2)}) collective-permute-start(f32[2,32768]{1,0:T(2,128)S(1)} %get-tuple-element.196), channel_id=1, source_target_pairs={{0,4},{4,8},{8,12},{12,16},{16,20},{20,24},{24,28},{28,0},{1,5},{5... | collective-permute-start | bytes 786440 | tf_op jit(solution)/shard_map/ppermute | solution.py:13
  696.8 27.7 %collective-permute-start.2 = (f32[2,32768]{1,0:T(2,128)S(1)}, f32[2,32768]{1,0:T(2,128)S(1)}, u32[]{:S(2)}, u32[]{:S(2)}) collective-permute-start(f32[2,32768]{1,0:T(2,128)S(1)} %get-tuple-element.198), channel_id=1, source_target_pairs={{0,4},{4,8},{8,12},{12,16},{16,20},{20,24},{24,28},{28,0},{1,5},{5... | collective-permute-start | bytes 786440 | tf_op jit(solution)/shard_map/ppermute | solution.py:13
  699.7 25.5 %collective-permute-start = (f32[2,32768]{1,0:T(2,128)S(1)}, f32[2,32768]{1,0:T(2,128)S(1)}, u32[]{:S(2)}, u32[]{:S(2)}) collective-permute-start(f32[2,32768]{1,0:T(2,128)S(1)} %get-tuple-element.194), channel_id=1, source_target_pairs={{0,4},{4,8},{8,12},{12,16},{16,20},{20,24},{24,28},{28,0},{1,5},{5... | collective-permute-start | bytes 786440 | tf_op jit(solution)/shard_map/ppermute | solution.py:13
  720.2 3.7 copy-start.20
  720.2 3.7 copy-start.22
  727.0 39.9 %copy-start.10 = (f32[8,16,32]{2,1,0:T(8,128)S(1)}, f32[8,16,32]{2,1,0:T(8,128)}, u32[]{:S(2)}) copy-start(f32[8,16,32]{2,1,0:T(8,128)} %gather_fusion.6) | copy-start | bytes 49156
  779.5 19.9 %copy-start.30 = (s32[16]{0:T(128)S(1)}, s32[16]{0:T(128)}, u32[]{:S(2)}) copy-start(s32[16]{0:T(128)} %copy-done.29) | copy-start | bytes 196
  (132 other events, 229.6 us)
Sparse Core Ops, SparseCore 0:
  727.2 37.8 all-reduce.2
where the time goes:
time: 820 us; the launch traced here: 807 us
  local copies, waits for them, and re-layouts  335 us (41%)
  matrix products  258 us (31%)
  other arithmetic  80.2 us (10%)
  waiting for transfers between devices  64.5 us (8%)
  starting transfers between devices  21 us (3%)
  blocking collectives  19.2 us (2%)
  loops' own time  14.9 us (2%)
  between operations  14.8 us (2%)
    dot_general x60, matrix products, rotate_single(): result = jnp.einsum('kc,...mc->...km', matrix, viewed, precision=exact_mode)  153 us
    dot_general x61, matrix products, rotate_many(): result = jnp.einsum('ekc,nmc->enkm', matrices, viewed, precision=exact_mode)  72.6 us
    reshape x60, local copies, waits for them, and re-layouts, rotate_single(): viewed = blocks.reshape(blocks.shape[:-1] + (-1, breadth))  68 us
    add x20, other arithmetic, one_term(): totals[2] + last_sides  57.3 us
    reshape x40, local copies, waits for them, and re-layouts, rotate_single(): return result.reshape(blocks.shape[:-1] + (-1,))  38.7 us
    unnamed x2, waiting for transfers between devices  37.9 us
    while x280, local copies, waits for them, and re-layouts  35.4 us
    reshape x21, local copies, waits for them, and re-layouts, rotate_many(): viewed = blocks.reshape(blocks.shape[:1] + (-1, breadth))  28.8 us
  transfers between devices with their start and end apart: 9, of which 6 were waited for; matrix products, arithmetic and copies ran while one was open for 2% of the time, Pallas kernels for 0%

commit v1 on v0

v1 whole, which is shorter than its diff:
```python
import functools

import jax
import jax.numpy as jnp
import numpy as np
from jax import lax
from jax.experimental import pallas as pl
from jax.experimental.pallas import tpu as pltpu
from jax.sharding import PartitionSpec as P

F32, BF16 = jnp.float32, jnp.bfloat16


def split_host(x):
    high = lax.reduce_precision(x, 8, 7)
    return high.astype(BF16), (x - high).astype(BF16)


def split_kernel(x):
    high = x.astype(BF16)
    return high, (x - high.astype(F32)).astype(BF16)


def triple(x, axis):
    high, low = split_host(x)
    return jnp.concatenate([high, high, low], axis=axis)


def apply_weights(factor_set, groups):
    terms, breadth = factor_set.shape[0], factor_set.shape[-1]
    lo_count = 128 // breadth
    hi_count = breadth // lo_count
    first = jnp.concatenate([triple(factor_set[:, 0, k].reshape(terms * breadth, breadth), 1) for k in (1, 2, 0)], axis=1)
    turned = jnp.tile(jnp.transpose(factor_set[:, 2], (0, 1, 3, 2)), (1, 1, 1, lo_count))
    second_high, second_low = split_host(turned)
    per = terms // groups
    third = factor_set[:, 1][:, np.array([1, 2, 0])].reshape(groups, per, 3, breadth, hi_count, lo_count)
    third = jnp.transpose(third, (0, 5, 3, 2, 1, 4)).reshape(groups, lo_count * breadth, 3, per * hi_count)
    third = triple(third, 3).reshape(groups, lo_count * breadth, -1)
    return first, second_high, second_low, third


def apply_kernel(where, own, *refs, parts, groups):
    sides = refs[: 2 * parts]
    first, second_high, second_low, third, out = refs[2 * parts : 2 * parts + 5]
    vols, xbuf, ubuf, lbuf, tbuf, rbuf, obuf, sems = refs[2 * parts + 5 :]
    count, breadth, width = own.shape
    lo_count = 128 // breadth
    hi_count = breadth // lo_count
    rows = first.shape[0]
    per = rows // breadth
    kgroup = per * hi_count
    group = pl.program_id(0)

    def copies(action):
        for n in range(count):
            for side in range(2):
                for axis in range(3):
                    slot = (n * 2 + side) * 3 + axis
                    at = where[n, side * 3 + axis]
                    target = vols.at[slot]
                    start = 0
                    for part in range(parts):
                        source = sides[side * parts + part]
                        size = source.shape[0]

                        @pl.when((at >= start) & (at < start + size))
                        def _(source=source, start=start):
                            action(pltpu.make_async_copy(source.at[at - start], target, sems.at[slot]))

                        start += size

    @pl.when(group == 0)
    def _():
        for n in range(count):
            for side in range(2):
                for axis in range(3):
                    slot = (n * 2 + side) * 3 + axis

                    @pl.when(where[n, side * 3 + axis] < 0)
                    def _(slot=slot):
                        vols[slot] = jnp.zeros((breadth, width), F32)

        copies(lambda c: c.start())
        tbuf[...] = jnp.zeros(tbuf.shape, BF16)
        obuf[...] = jnp.zeros(obuf.shape, F32)
        copies(lambda c: c.wait())

    for n in range(count):
        def fill(row, block):
            high, low = split_kernel(block)
            xbuf[row : row + breadth] = high
            xbuf[row + breadth : row + 2 * breadth] = low
            xbuf[row + 2 * breadth : row + 3 * breadth] = high

        def place(g, result):
            for h in range(hi_count):
                ubuf[g, n, h] = result[:, h * 128 : (h + 1) * 128]

        fill(0, own[n])
        fill(3 * breadth, vols[(n * 2 + 0) * 3])
        fill(6 * breadth, vols[(n * 2 + 1) * 3])
        place(0, jnp.dot(first[...], xbuf[...], preferred_element_type=F32))
        for g, (side, axis) in enumerate([(0, 2), (1, 2), (0, 1), (1, 1)]):
            fill(0, vols[(n * 2 + side) * 3 + axis])
            place(g + 1, jnp.dot(first[:, : 3 * breadth], xbuf[: 3 * breadth], preferred_element_type=F32))

    flat = ubuf.reshape(5 * count * hi_count * rows, 128)
    block_mask = (
        lax.broadcasted_iota(jnp.int32, (128, 128), 0) // breadth
        == lax.broadcasted_iota(jnp.int32, (128, 128), 1) // breadth
    )
    zero_block = jnp.zeros((128, 128), BF16)

    def pair_body(pair, carry):
        for k in range(3):
            for half in range(2):
                term = pair * 2 + half
                high = jnp.concatenate([second_high[term, k]] * lo_count, axis=0)
                low = jnp.concatenate([second_low[term, k]] * lo_count, axis=0)
                high = jnp.where(block_mask, high, zero_block)
                low = jnp.where(block_mask, low, zero_block)
                tbuf[half, k, :128, :128] = high
                tbuf[half, k, 128:, :128] = high
                tbuf[half, k, :128, 128:] = low
        for n in range(count):
            for half in range(2):
                term = pair * 2 + half
                for g in range(5):
                    base = (g * count + n) * hi_count * rows + term * breadth
                    for a in range(0, breadth, 2):
                        pieces = [flat[pl.ds(base + a + d, hi_count, stride=rows), :] for d in range(2)]
                        high, low = split_kernel(jnp.concatenate(pieces, axis=0))
                        at = a * hi_count
                        lbuf[half, g, at : at + 2 * hi_count, :128] = high
                        lbuf[half, g, at : at + 2 * hi_count, 128:] = low

            def mixed(half, g, k):
                return jnp.dot(lbuf[half, g], tbuf[half, k], preferred_element_type=F32)

            def folded(wide):
                return wide[:, :128] + wide[:, 128:]

            results = []
            for half in range(2):
                centre = folded(mixed(half, 0, 1) + mixed(half, 1, 2) + mixed(half, 2, 0))
                results.append((centre, folded(mixed(half, 3, 1)), folded(mixed(half, 4, 1))))
            for q in range(3):
                for a in range(breadth):
                    both = jnp.concatenate([results[half][q][a * hi_count : (a + 1) * hi_count] for half in range(2)], axis=0)
                    high, low = split_kernel(both)
                    tile = (n * breadth + a) // 2
                    lane = (a % 2) * 128
                    step = 2 * hi_count
                    row = pl.multiple_of(q * 3 * kgroup + pair * step, step)
                    rbuf[tile, pl.ds(row, step), lane : lane + 128] = high
                    rbuf[tile, pl.ds(row + kgroup, step), lane : lane + 128] = low
                    rbuf[tile, pl.ds(row + 2 * kgroup, step), lane : lane + 128] = high
        return carry

    lax.fori_loop(0, per // 2, pair_body, 0)

    lane_block = lax.broadcasted_iota(jnp.int32, (breadth, 256), 1) % 128 // breadth

    def tile_body(tile, carry):
        wide = jnp.dot(third[0], rbuf[tile], preferred_element_type=F32)
        total = wide[:breadth]
        for low in range(1, lo_count):
            total = jnp.where(lane_block == low, wide[low * breadth : (low + 1) * breadth], total)
        for d in range(2):
            row = pl.multiple_of((tile * 2 + d) * breadth, breadth)
            obuf[pl.ds(row, breadth), :] = obuf[pl.ds(row, breadth), :] + total[:, d * 128 : (d + 1) * 128]
        return carry

    lax.fori_loop(0, count * breadth // 2, tile_body, 0)

    @pl.when(group == groups - 1)
    def _():
        lane_of = lax.broadcasted_iota(jnp.int32, (8, 128), 1) // breadth
        for n in range(count):
            for a in range(0, breadth, 8):
                for high in range(hi_count):
                    total = None
                    for low in range(lo_count):
                        b = high * lo_count + low
                        piece = obuf[pl.ds((n * breadth + a) * breadth + b, 8, stride=breadth), :]
                        shift = 64
                        while shift >= breadth:
                            piece = piece + pltpu.roll(piece, shift, 1)
                            shift //= 2
                        total = piece if total is None else jnp.where(lane_of == low, piece, total)
                    out[n, a : a + 8, high * 128 : (high + 1) * 128] = total


def apply_call(where, own, below, above, weights, groups):
    first, second_high, second_low, third = weights
    count, breadth, width = own.shape
    lo_count = 128 // breadth
    hi_count = breadth // lo_count
    rows = first.shape[0] // groups
    per = rows // breadth
    parts = len(below)
    tiles = count * breadth // 2
    anywhere = pl.BlockSpec(memory_space=pl.ANY)
    return pl.pallas_call(
        functools.partial(apply_kernel, parts=parts, groups=groups),
        out_shape=jax.ShapeDtypeStruct(own.shape, F32),
        grid_spec=pltpu.PrefetchScalarGridSpec(
            num_scalar_prefetch=1,
            grid=(groups,),
            in_specs=[pl.BlockSpec(own.shape, lambda g, w: (0, 0, 0))]
            + [anywhere] * (2 * parts)
            + [
                pl.BlockSpec((rows, first.shape[1]), lambda g, w: (g, 0)),
                pl.BlockSpec((per,) + second_high.shape[1:], lambda g, w: (g, 0, 0, 0)),
                pl.BlockSpec((per,) + second_low.shape[1:], lambda g, w: (g, 0, 0, 0)),
                pl.BlockSpec((1,) + third.shape[1:], lambda g, w: (g, 0, 0)),
            ],
            out_specs=pl.BlockSpec(own.shape, lambda g, w: (0, 0, 0)),
            scratch_shapes=[
                pltpu.VMEM((count * 6, breadth, width), F32),
                pltpu.VMEM((9 * breadth, width), BF16),
                pltpu.VMEM((5, count, hi_count, rows, 128), F32),
                pltpu.VMEM((2, 5, breadth * hi_count, 256), BF16),
                pltpu.VMEM((2, 3, 256, 256), BF16),
                pltpu.VMEM((tiles, third.shape[2], 256), BF16),
                pltpu.VMEM((count * breadth * breadth, 128), F32),
                pltpu.SemaphoreType.DMA((count * 6,)),
            ],
        ),
        compiler_params=pltpu.CompilerParams(dimension_semantics=("arbitrary",), vmem_limit_bytes=60 << 20),
        name="apply",
    )(where, own, *below, *above, first, second_high, second_low, third)


def iota(shape, axis):
    return lax.broadcasted_iota(jnp.int32, shape, axis)


def to_row(column):
    size = column.shape[0]
    diagonal = iota((size, size), 0) == iota((size, size), 1)
    return jnp.sum(jnp.where(diagonal, column, 0.0), axis=0, keepdims=True)


def to_column(row):
    size = row.shape[1]
    diagonal = iota((size, size), 0) == iota((size, size), 1)
    return jnp.sum(jnp.where(diagonal, row, 0.0), axis=1, keepdims=True)


def run_of(slots, runs, run_size):
    run = jnp.zeros(slots.shape, F32)
    for r in range(1, runs):
        run = run + jnp.where(slots >= r * run_size, 1.0, 0.0)
    return run


def place_row(slot_row, runs, run_size, capacity):
    held = slot_row.shape[1]
    run_row = run_of(slot_row, runs, run_size)
    same = to_column(run_row) == run_row
    earlier = iota((held, held), 0) < iota((held, held), 1)
    before = jnp.sum(jnp.where(same & earlier, 1.0, 0.0), axis=0, keepdims=True)
    return run_row * capacity + before


def pack_kernel(slot_row, fine, out, stack, *, runs, run_size, capacity):
    held, volume = fine.shape
    places = runs * capacity
    slots = slot_row[...]
    place = place_row(slots, runs, run_size, capacity)
    hit = iota((places, held), 0).astype(F32) == place
    ids = jnp.sum(jnp.where(hit, slots.astype(F32) + 1.0, 0.0), axis=1, keepdims=True)
    out[:, volume:] = jnp.broadcast_to(ids, (places, 128))
    one = jnp.where(hit, 1.0, 0.0).astype(BF16)
    rest = fine[...]
    for part in range(3):
        head = rest.astype(BF16)
        stack[part * held : (part + 1) * held] = head
        rest = rest - head.astype(F32)
    out[:, :volume] = jnp.dot(jnp.concatenate([one] * 3, axis=1), stack[...], preferred_element_type=F32)


def unpack_kernel(slot_row, back, out, stack, *, runs, run_size, capacity):
    held, volume = out.shape
    places = runs * capacity
    place = to_column(place_row(slot_row[...], runs, run_size, capacity))
    hit = iota((held, places), 1).astype(F32) == place
    one = jnp.where(hit, 1.0, 0.0).astype(BF16)
    rest = back[...]
    for part in range(3):
        head = rest.astype(BF16)
        stack[part * places : (part + 1) * places] = head
        rest = rest - head.astype(F32)
    out[...] = jnp.dot(jnp.concatenate([one] * 3, axis=1), stack[...], preferred_element_type=F32)


def child_code(ids, held):
    at = ids - 1.0
    return jnp.where(at < 0.0, -1.0, at - held * jnp.floor(at / held))


def row_code(index, count):
    inner = index & 7
    code = (inner >> 1) * 8 + (inner & 1) * 4 + (index >> 3)
    return jnp.where(inner < 2 * count, code.astype(F32), -2.0)


def filter_kernel(got, across_z, across_y, rows, out, stack, lines, cross, weave, *, count):
    places = got.shape[0]
    width = out.shape[1]
    volume = got.shape[1] - 128
    face = width // 4
    span = volume // face
    held = 8 * count
    code = to_row(child_code(got[:, volume : volume + 1], held))
    hit = row_code(iota((32, places), 0), count) == code
    one = jnp.where(hit, 1.0, 0.0).astype(BF16)
    high, low = split_kernel(got[:, :volume])
    stack[:places] = high
    stack[places:] = low
    boxes = jnp.dot(jnp.concatenate([one, one], axis=1), stack[...], preferred_element_type=F32)
    for g in range(4):
        for i in range(0, span, 2):
            both = jnp.concatenate([boxes[g * 8 : g * 8 + 8, (i + d) * face : (i + d + 1) * face] for d in range(2)], axis=0)
            high, low = split_kernel(both)
            lines[0, i * 8 : i * 8 + 16, g * face : (g + 1) * face] = high
            lines[1, i * 8 : i * 8 + 16, g * face : (g + 1) * face] = low
    half = across_z.shape[0] // 2
    for g in range(4):
        zs = across_z[(g & 1) * half : (g & 1) * half + half]
        for j in range(half):
            row = (g >> 1) * half + j
            high, low = split_kernel(zs * across_y[row : row + 1])
            at = (g * half + j) * half
            cross[0, at : at + half] = high
            cross[1, at : at + half] = low
    total = jnp.dot(lines[0], cross[0], preferred_element_type=F32)
    total = total + jnp.dot(lines[1], cross[0], preferred_element_type=F32)
    total = total + jnp.dot(lines[0], cross[1], preferred_element_type=F32)
    high, low = split_kernel(total)
    size = total.shape[0]
    weave[:size] = high
    weave[size : 2 * size] = low
    weave[2 * size :] = high
    out[...] = jnp.dot(rows[...], weave[...], preferred_element_type=F32)


def unfilter_kernel(applied, ids, across_c, across_b, rows, out, weave, cross, stack, *, count):
    places = out.shape[0]
    size, width = applied.shape
    breadth = across_c.shape[0]
    face = width // 4
    held = 8 * count
    high, low = split_kernel(applied[...])
    weave[:size] = high
    weave[size : 2 * size] = low
    weave[2 * size :] = high
    lines = jnp.dot(rows[...], weave[...], preferred_element_type=F32)
    for b in range(breadth):
        high, low = split_kernel(across_c[...] * across_b[b : b + 1])
        cross[0, b * breadth : (b + 1) * breadth] = high
        cross[1, b * breadth : (b + 1) * breadth] = low
    high, low = split_kernel(lines)
    total = jnp.dot(high, cross[0], preferred_element_type=F32)
    total = total + jnp.dot(low, cross[0], preferred_element_type=F32)
    total = total + jnp.dot(high, cross[1], preferred_element_type=F32)
    for g in range(0, 4, 2):
        for i in range(total.shape[0] // 8):
            both = jnp.concatenate([total[i * 8 : i * 8 + 8, (g + d) * face : (g + d + 1) * face] for d in range(2)], axis=0)
            high, low = split_kernel(both)
            stack[g * 8 : g * 8 + 16, i * face : (i + 1) * face] = high
            stack[32 + g * 8 : 32 + g * 8 + 16, i * face : (i + 1) * face] = low
    code = child_code(ids[:, :1], held)
    hit = row_code(iota((places, 32), 1), count) == code
    one = jnp.where(hit, 1.0, 0.0).astype(BF16)
    out[...] = jnp.dot(jnp.concatenate([one, one], axis=1), stack[...], preferred_element_type=F32)


def shifted(array, axis, by):
    peers = lax.axis_size(axis)
    return lax.ppermute(array, axis, [(i, (i + by) % peers) for i in range(peers)])


def swapped(array, axis, bit):
    peers = lax.axis_size(axis)
    return lax.ppermute(array, axis, [(i, i ^ bit) for i in range(peers)])


def vmem_call(kernel, out_shape, scratch, name, **settings):
    return pl.pallas_call(
        functools.partial(kernel, **settings),
        out_shape=jax.ShapeDtypeStruct(out_shape, F32),
        scratch_shapes=[pltpu.VMEM(shape, dtype) for shape, dtype in scratch],
        compiler_params=pltpu.CompilerParams(vmem_limit_bytes=60 << 20),
        name=name,
    )


def local(fine_coeffs, fine_slot, neighbours, filter_matrix, kernel_ops):
    breadth = filter_matrix.shape[0]
    half = breadth // 2
    factor_set = kernel_ops.reshape(kernel_ops.shape[:3] + (breadth, breadth))
    runs = lax.axis_size("row")
    cols = lax.axis_size("col")
    held, volume = fine_coeffs.shape
    par_row = neighbours.shape[0]
    count = held // 8
    capacity = 2 * (held // runs)
    places = runs * capacity
    width = breadth * breadth
    routing = dict(runs=runs, run_size=8 * par_row, capacity=capacity)
    groups = 2

    slot_row = fine_slot.reshape(1, held)
    sent = vmem_call(pack_kernel, (places, volume + 128), [((3 * held, volume), BF16)], "pack", **routing)(slot_row, fine_coeffs)
    got = lax.all_to_all(sent, "row", split_axis=0, concat_axis=0, tiled=True)

    turned = filter_matrix.T
    across_z = jnp.tile(turned, (1, breadth))
    across_y = jnp.repeat(turned, breadth, axis=1)
    tall = filter_matrix.reshape(breadth, 2, half)
    same = np.eye(count, dtype=np.float32)
    mix = jnp.einsum("nm,aoi->naimo", same, tall, precision=lax.Precision.HIGHEST).reshape(count * breadth, half, 2 * count)
    mix = jnp.pad(mix, ((0, 0), (0, 0), (0, 8 - 2 * count))).reshape(count * breadth, half * 8)
    filtered = vmem_call(
        filter_kernel,
        (count * breadth, width),
        [
            ((2 * places, volume), BF16),
            ((2, half * 8, width), BF16),
            ((2, width, width), BF16),
            ((3 * half * 8, width), BF16),
        ],
        "filter",
        count=count,
    )(got, across_z, across_y, triple(mix, 1)).reshape(count, breadth, width)

    col_index = lax.axis_index("col")
    bits = [1 << k for k in reversed(range(cols.bit_length() - 1))]
    below = [shifted(filtered, "row", 1)]
    above = [shifted(filtered, "row", -1)]
    for bit in bits:
        below = below + [swapped(part, "col", bit) for part in below]
        above = above + [swapped(part, "col", bit) for part in above]
    mine = lax.dynamic_slice_in_dim(neighbours, col_index * count, count, 0)
    within = mine % par_row
    relation = (within // count) ^ col_index
    part = jnp.zeros_like(relation)
    for order, bit in enumerate(bits):
        part = part + ((relation // bit) % 2) * (1 << order)
    at = jnp.where(mine >= 0, part * count + within % count, -1)
    where = jnp.concatenate([at[:, 1::2], at[:, 0::2]], axis=1)
    weights = apply_weights(factor_set, groups)
    applied = apply_call(where, filtered, below, above, weights, groups).reshape(count * breadth, width)

    across_c = jnp.broadcast_to(filter_matrix.reshape(breadth, 1, 2, 1, half), (breadth, 2, 2, half, half)).reshape(breadth, width)
    across_b = jnp.broadcast_to(filter_matrix.reshape(breadth, 2, 1, half, 1), (breadth, 2, 2, half, half)).reshape(breadth, width)
    results = vmem_call(
        unfilter_kernel,
        (places, volume),
        [
            ((3 * count * breadth, width), BF16),
            ((2, width, width), BF16),
            ((64, volume), BF16),
        ],
        "unfilter",
        count=count,
    )(applied, got[:, volume:], across_c, across_b, triple(mix.T, 1))
    back = lax.all_to_all(results, "row", split_axis=0, concat_axis=0, tiled=True)
    return vmem_call(unpack_kernel, (held, volume), [((3 * places, volume), BF16)], "unpack", **routing)(slot_row, back)


def solution(mesh):
    in_specs = (P(("row", "col"), None), P(("row", "col")), P("row", None), P(), P())
    out_specs = P(("row", "col"), None)
    return jax.shard_map(local, mesh=mesh, in_specs=in_specs, out_specs=out_specs, check_vma=False)
```

time: 820 us -> 141 us (0.17); the launches traced: 807 us -> 140 us
  local copies, waits for them, and re-layouts: 335 us -> 35.9 us
  matrix products: 258 us -> 0 us
  other arithmetic: 80.2 us -> 5.23 us
  waiting for transfers between devices: 64.5 us -> 7.67 us
  Pallas kernels: 0 us -> 55.9 us
  loops' own time: 14.9 us -> 0 us
  between operations: 14.8 us -> 0.22 us
    dot_general x136 -> x0, matrix products: 258 us -> none  [the longest x60 153 us: rotate_single(): result = jnp.einsum('kc,...mc->...km', matrix, viewed, precision=exact_mode)]
    reshape x165 -> x7, local copies, waits for them, and re-layouts: 163 us -> 5.95 us  [the longest x1 2.33 us: apply_weights(): jnp.transpose(third, (0, 5, 3, 2, 1, 4))]
    add x44 -> x0, other arithmetic: 75.2 us -> none  [the longest x20 57.3 us: one_term(): totals[2] + last_sides]
    pallas_call x0 -> x5, Pallas kernels: none -> 55.9 us  [the longest x1 44.3 us: apply_call(): pl.pallas_call(functools.partial(apply_kernel, parts=parts, groups=groups...]
    squeeze x83 -> x0, local copies, waits for them, and re-layouts: 46.9 us -> none  [the longest x20 18.6 us: displaced(): totals, unused = lax.scan(one_term, initial, kernel_ops)]
    gather x66 -> x2, local copies, waits for them, and re-layouts: 51.8 us -> 5.23 us  [apply_weights(): factor_set[:, 1][:, np.array([1, 2, 0])]]
    unnamed x2 -> x0, waiting for transfers between devices: 37.9 us -> none
    while x280 -> x0, local copies, waits for them, and re-layouts: 35.4 us -> none
  transfers between devices with their start and end apart: 9 -> 9, of which waited for: 6 -> 2; matrix products, arithmetic and copies ran while one was open for 2% -> 25% of each run, Pallas kernels for 0% -> 0%
where the time goes in v1:
time: 141 us; the launch traced here: 140 us
  Pallas kernels  55.9 us (40%)
  local copies, waits for them, and re-layouts  35.9 us (25%)
  blocking collectives  19.3 us (14%)
  starting transfers between devices  16.1 us (11%)
  waiting for transfers between devices  7.67 us (5%)
  other arithmetic  5.23 us (4%)
    pallas_call x1, Pallas kernels, apply_call(): pl.pallas_call(functools.partial(apply_kernel, parts=parts, groups=groups...  44.3 us
    all_to_all x1, blocking collectives, local(): lax.all_to_all(results, 'row', split_axis=0, concat_axis=0, tiled=True)  19.3 us
    ppermute x2, waiting for transfers between devices, shifted(): lax.ppermute(array, axis, [(i, (i + by) % peers) for i in range(peers)])  7.66 us
    all_to_all x1, starting transfers between devices, local(): got = lax.all_to_all(sent, 'row', split_axis=0, concat_axis=0, tiled=True)  7.28 us
    another operation x2, local copies, waits for them, and re-layouts, apply_weights(): jnp.tile(jnp.transpose(factor_set[:, 2], (0, 1, 3, 2)), (1, 1, 1, lo_count))  6.11 us
    gather x2, local copies, waits for them, and re-layouts, apply_weights(): factor_set[:, 1][:, np.array([1, 2, 0])]  5.23 us
    ppermute x2, starting transfers between devices, shifted(): lax.ppermute(array, axis, [(i, (i + by) % peers) for i in range(peers)])  4.71 us
    ppermute x6, starting transfers between devices, swapped(): return lax.ppermute(array, axis, [(i, i ^ bit) for i in range(peers)])  4.06 us
  transfers between devices with their start and end apart: 9, of which 2 were waited for; matrix products, arithmetic and copies ran while one was open for 25% of the time, Pallas kernels for 0%

profile of v1, /device:TPU:0, one launch (start us, length us, event | category | flops | bytes accessed | tf_op | source)
XLA Modules:
  0.0 140.2 jit_solution(16733685937342454473)
XLA Ops:
  0.0 2.2 %pack.1 = f32[32,4224]{1,0:T(8,128)} custom-call(s32[1,16]{1,0:T(1,128)} %bitcast.67, f32[16,4096]{1,0:T(8,128)} %fine.1), custom_call_target="tpu_custom_call" | custom-call | tf_op jit(solution)/shard_map/pack/pallas_call | solution.py:417
  2.2 2.0 %all_to_all.14 = f32[8,4,4224]{2,1,0:T(4,128)} reshape(f32[32,4224]{1,0:T(8,128)} %pack.1) | data formatting | bytes 1081344 | tf_op jit(solution)/shard_map/all_to_all | solution.py:418
  4.2 7.3 %all-to-all-start = ((f32[8,4,4224]{2,1,0:T(4,128)}), f32[8,4,4224]{2,1,0:T(4,128)S(1)}, u32[]{:S(2)}, u32[]{:S(2)}) async-start(f32[8,4,4224]{2,1,0:T(4,128)} %all_to_all.14), calls=%async_computation | async-start | bytes 1081344 | tf_op jit(solution)/shard_map/all_to_all | solution.py:418
  11.5 0.1 copy.39
  11.6 0.1 copy.37
  11.7 0.1 multiply_bitcast_fusion
  11.7 0.1 reshape.58
  11.9 0.7 copy.41.rows
  12.6 0.2 broadcast_in_dim.18
  12.8 0.9 reshape.56.across_y
  13.7 0.9 tile.9.across_z
  14.6 2.0 %reshape.61 = f32[20,3,3,32,32]{4,3,0,2,1:T(8,128)S(1)} reshape(f32[20,3,3,1024]{3,0,2,1:T(8,128)} %param.12) | data formatting | bytes 1474560 | tf_op jit(solution)/shard_map/reshape | solution.py:404
  16.7 0.0 copy-start.11
  16.7 1.2 fusion.12
  17.8 1.0 copy.51
  18.9 2.8 %gather_fusion = f32[3,20,32,32]{3,2,1,0:T(8,128)} fusion(f32[20,3,32,32]{3,2,1,0:T(8,128)} %bitcast.53, s32[1024]{0:T(1024)S(1)} %pad_clamp_fusion), kind=kCustom, calls=%fused_computation | custom fusion | bytes 491532 | tf_op jit(solution)/shard_map/gather | solution.py:37
  21.6 2.5 %copy.44 = f32[20,3,32,32]{2,3,1,0:T(8,128)} copy(f32[20,3,32,32]{3,2,0,1:T(8,128)} %bitcast.54) | data formatting | bytes 491520 | tf_op jit(solution)/shard_map/gather | solution.py:37
  24.1 2.2 %copy.45 = f32[2,4,32,3,10,8]{2,1,5,4,3,0:T(4,128)} copy(f32[2,4,32,3,10,8]{2,1,5,3,4,0:T(4,128)} %bitcast.55) | data formatting | bytes 491520 | tf_op jit(solution)/shard_map/transpose | solution.py:38
  26.3 2.3 %reshape.63 = f32[2,128,3,80]{1,3,2,0:T(8,128)} reshape(f32[2,4,32,3,10,8]{2,1,5,4,3,0:T(4,128)} %copy.45) | data formatting | bytes 491520 | tf_op jit(solution)/shard_map/reshape | solution.py:38
  28.7 1.0 reduce-precision_convert_fusion.4
  29.7 0.8 pad_maximum_fusion
  30.4 0.9 fusion.13
  31.4 0.1 fusion.3
  31.4 0.0 all-to-all-done
  31.4 1.0 all_to_all.16.got
  32.4 3.7 %filter.1 = f32[64,1024]{1,0:T(8,128)} custom-call(f32[32,4224]{1,0:T(8,128)} %all_to_all.16.got, f32[32,1024]{1,0:T(8,128)} %tile.9.across_z, f32[32,1024]{1,0:T(8,128)} %reshape.56.across_y, bf16[64,384]{1,0:T(8,128)(2,1)} %copy.41.rows), custom_call_target="tpu_custom_call" | custom-call | tf_op jit(solution)/shard_map/filter/pallas_call | solution.py:427
  36.1 4.7 %collective-permute-start.4 = (f32[2,32,1024]{2,1,0:T(8,128)}, f32[2,32,1024]{2,1,0:T(8,128)}, u32[]{:S(2)}, u32[]{:S(2)}) collective-permute-start(f32[2,32,1024]{2,1,0:T(8,128)} %bitcast.59), channel_id=1, source_target_pairs={{0,28},{4,0},{8,4},{12,8},{16,12},{20,16},{24,20},{28,24},{1,29},{... | collective-permute-start | bytes 786440 | tf_op jit(solution)/shard_map/ppermute | solution.py:383
  40.8 0.0 collective-permute-start
  40.8 0.7 compare_select_fusion.4
  41.6 0.1 slice.25
  41.7 0.1 slice.24
  41.8 0.1 fusion.1
  41.9 4.3 %collective-permute-done.4.refs_4_ = f32[2,32,1024]{2,1,0:T(8,128)} collective-permute-done((f32[2,32,1024]{2,1,0:T(8,128)}, f32[2,32,1024]{2,1,0:T(8,128)}, u32[]{:S(2)}, u32[]{:S(2)}) %collective-permute-start.4) | collective-permute-done | bytes 262176 | tf_op jit(solution)/shard_map/ppermute | solution.py:383
  46.2 1.5 %collective-permute-start.5 = (f32[2,32,1024]{2,1,0:T(8,128)}, f32[2,32,1024]{2,1,0:T(8,128)S(1)}, u32[]{:S(2)}, u32[]{:S(2)}) collective-permute-start(f32[2,32,1024]{2,1,0:T(8,128)} %collective-permute-done.4.refs_4_), channel_id=1, source_target_pairs={{0,2},{1,3},{2,0},{3,1},{4,6},{5,7},{6,4},{7,5},{8,10},{9,11},{10,... | collective-permute-start | bytes 786440 | tf_op jit(solution)/shard_map/ppermute | solution.py:388
  47.7 3.4 %collective-permute-done.refs_0_ = f32[2,32,1024]{2,1,0:T(8,128)} collective-permute-done((f32[2,32,1024]{2,1,0:T(8,128)}, f32[2,32,1024]{2,1,0:T(8,128)}, u32[]{:S(2)}, u32[]{:S(2)}) %collective-permute-start) | collective-permute-done | bytes 262176 | tf_op jit(solution)/shard_map/ppermute | solution.py:383
  51.1 1.5 %collective-permute-start.1 = (f32[2,32,1024]{2,1,0:T(8,128)}, f32[2,32,1024]{2,1,0:T(8,128)}, u32[]{:S(2)}, u32[]{:S(2)}) collective-permute-start(f32[2,32,1024]{2,1,0:T(8,128)} %collective-permute-done.refs_0_), channel_id=1, source_target_pairs={{0,2},{1,3},{2,0},{3,1},{4,6},{5,7},{6,4},{7,5},{8,10},{9,11},{10,... | collective-permute-start | bytes 786440 | tf_op jit(solution)/shard_map/ppermute | solution.py:388
  52.6 0.6 pad_add_fusion.where
  53.2 0.8 copy.48.across_b
  54.1 0.8 copy.47.across_c
  54.9 0.9 copy.46.refs_11_
  55.9 0.3 copy.42
  56.2 2.6 %tile.20 = f32[20,3,32,4,32]{4,3,2,1,0:T(4,128)} broadcast(f32[20,3,32,32]{3,2,1,0:T(8,128)S(1)} %copy.42), dimensions={0,1,2,4} | broadcast | bytes 1228800 | tf_op jit(solution)/shard_map/tile | solution.py:34
  58.8 3.5 %tile.21 = f32[20,3,32,128]{3,2,1,0:T(8,128)S(1)} reshape(f32[20,3,32,4,32]{4,3,2,1,0:T(4,128)} %tile.20) | data formatting | bytes 1966080 | tf_op jit(solution)/shard_map/tile | solution.py:34
  62.3 1.3 concatenate.17.refs_8_
  63.6 0.7 pad_maximum_fusion.2.rows
  64.3 0.0 collective-permute-start.6
  64.3 0.5 collective-permute-start.2
  64.8 0.0 collective-permute-done.5.refs_5_
  64.8 0.1 collective-permute-start.7
  64.9 0.4 collective-permute-start.3
  65.3 1.1 fusion
  66.5 1.3 slice.39.ids
  67.8 0.0 collective-permute-done.6.refs_6_
  67.8 0.0 collective-permute-done.2.refs_2_
  67.8 0.6 copy-done.5
  68.5 0.1 copy-done.6
  68.6 0.1 copy-done.7
  68.7 0.1 copy-done.8
  68.7 44.3 %apply.1 = f32[2,32,1024]{2,1,0:T(8,128)} custom-call(s32[2,6]{1,0:T(2,128)} %pad_add_fusion.where, f32[2,32,1024]{2,1,0:T(8,128)} %bitcast.61, f32[2,32,1024]{2,1,0:T(8,128)} %collective-permute-done.refs_0_, f32[2,32,1024]{2,1,0:T(8,128)} %collective-permute-done.1.refs_1_, f32[2,32,1024]{2,1,0:T(8,128)} %copy-done.6, f32[2,32,1024]{2,1,0:T(8,128)} %copy-done.8, ...), custom_call_target="tpu_custom_call" | custom-call | tf_op jit(solution)/shard_map/apply/pallas_call | solution.py:205
  113.0 3.5 %unfilter.1 = f32[32,4096]{1,0:T(8,128)} custom-call(f32[64,1024]{1,0:T(8,128)} %bitcast.62, f32[32,128]{1,0:T(8,128)} %slice.39.ids, f32[32,1024]{1,0:T(8,128)} %copy.47.across_c, f32[32,1024]{1,0:T(8,128)} %copy.48.across_b, bf16[128,192]{1,0:T(8,128)(2,1)} %pad_maximum_fusion.2.rows), custom_call_target="tpu_custom_call" | custom-call | tf_op jit(solution)/shard_map/unfilter/pallas_call | solution.py:460
  116.5 1.2 all_to_all.17
  117.7 19.3 %all_to_all.22 = f32[8,4,4096]{2,1,0:T(4,128)S(1)} all-to-all(f32[8,4,4096]{2,1,0:T(4,128)S(1)} %all_to_all.17), channel_id=1, replica_groups=mesh['row'=8,'col'=4] {'row'}, dimensions={0} | all-to-all | bytes 1048576 | tf_op jit(solution)/shard_map/all_to_all | solution.py:471
  137.0 1.0 all_to_all.19.back
  138.0 2.2 %unpack.1 = f32[16,4096]{1,0:T(8,128)} custom-call(s32[1,16]{1,0:T(1,128)} %bitcast.68, f32[32,4096]{1,0:T(8,128)} %all_to_all.19.back), custom_call_target="tpu_custom_call" | custom-call | tf_op jit(solution)/shard_map/unpack/pallas_call | solution.py:472
  (30 shorter events, 0.2 us)
Async XLA Ops:
  0.0 11.6 %copy-start.10 = (f32[2,2]{0,1:T(2,128)S(1)}, f32[2,2]{0,1:T(2,128)}, u32[]{:S(2)}) copy-start(f32[2,2]{0,1:T(2,128)} %constant.81.clone) | copy-start | bytes 52
  0.0 11.5 %copy-start.9 = (f32[32,32]{1,0:T(8,128)S(1)}, f32[32,32]{1,0:T(8,128)}, u32[]{:S(2)}) copy-start(f32[32,32]{1,0:T(8,128)} %param.11) | copy-start | bytes 12292
  4.2 27.2 %all-to-all-start = ((f32[8,4,4224]{2,1,0:T(4,128)}), f32[8,4,4224]{2,1,0:T(4,128)S(1)}, u32[]{:S(2)}, u32[]{:S(2)}) async-start(f32[8,4,4224]{2,1,0:T(4,128)} %all_to_all.14), calls=%async_computation | async-start | bytes 1081344 | tf_op jit(solution)/shard_map/all_to_all | solution.py:418
  16.7 2.2 %copy-start.11 = (s32[3]{0:T(128)S(1)}, s32[3]{0:T(128)}, u32[]{:S(2)}) copy-start(s32[3]{0:T(128)} %constant.89) | copy-start | bytes 40
  31.4 10.4 %copy-start.2 = (f32[20,1,1,32,32]{4,3,0,2,1:T(8,128)S(1)}, f32[20,1,1,32,32]{4,3,0,2,1:T(8,128)}, u32[]{:S(2)}) copy-start(f32[20,1,1,32,32]{4,3,0,2,1:T(8,128)} %get-tuple-element.8) | copy-start | bytes 245764
  31.4 10.4 %copy-start.3 = (f32[20,1,1,32,32]{4,3,0,2,1:T(8,128)S(1)}, f32[20,1,1,32,32]{4,3,0,2,1:T(8,128)}, u32[]{:S(2)}) copy-start(f32[20,1,1,32,32]{4,3,0,2,1:T(8,128)} %get-tuple-element.9) | copy-start | bytes 245764
  31.4 23.5 %copy-start.1 = (bf16[2,128,3,240]{1,3,2,0:T(8,128)(2,1)S(1)}, bf16[2,128,3,240]{1,3,2,0:T(8,128)(2,1)}, u32[]{:S(2)}) copy-start(bf16[2,128,3,240]{1,3,2,0:T(8,128)(2,1)} %pad_maximum_fusion) | copy-start | bytes 1105924
  32.4 23.4 %copy-start = (f32[20,3,32,32]{2,3,0,1:T(8,128)S(1)}, f32[20,3,32,32]{2,3,0,1:T(8,128)}, u32[]{:S(2)}) copy-start(f32[20,3,32,32]{2,3,0,1:T(8,128)} %get-tuple-element.6) | copy-start | bytes 737284
  36.1 10.0 %collective-permute-start.4 = (f32[2,32,1024]{2,1,0:T(8,128)}, f32[2,32,1024]{2,1,0:T(8,128)}, u32[]{:S(2)}, u32[]{:S(2)}) collective-permute-start(f32[2,32,1024]{2,1,0:T(8,128)} %bitcast.59), channel_id=1, source_target_pairs={{0,28},{4,0},{8,4},{12,8},{16,12},{20,16},{24,20},{28,24},{1,29},{... | collective-permute-start | bytes 786440 | tf_op jit(solution)/shard_map/ppermute | solution.py:383
  40.8 10.2 %collective-permute-start = (f32[2,32,1024]{2,1,0:T(8,128)}, f32[2,32,1024]{2,1,0:T(8,128)}, u32[]{:S(2)}, u32[]{:S(2)}) collective-permute-start(f32[2,32,1024]{2,1,0:T(8,128)} %bitcast.60), channel_id=1, source_target_pairs={{0,4},{4,8},{8,12},{12,16},{16,20},{20,24},{24,28},{28,0},{1,5},{5... | collective-permute-start | bytes 786440 | tf_op jit(solution)/shard_map/ppermute | solution.py:383
  46.2 18.7 %collective-permute-start.5 = (f32[2,32,1024]{2,1,0:T(8,128)}, f32[2,32,1024]{2,1,0:T(8,128)S(1)}, u32[]{:S(2)}, u32[]{:S(2)}) collective-permute-start(f32[2,32,1024]{2,1,0:T(8,128)} %collective-permute-done.4.refs_4_), channel_id=1, source_target_pairs={{0,2},{1,3},{2,0},{3,1},{4,6},{5,7},{6,4},{7,5},{8,10},{9,11},{10,... | collective-permute-start | bytes 786440 | tf_op jit(solution)/shard_map/ppermute | solution.py:388
  51.1 13.8 %collective-permute-start.1 = (f32[2,32,1024]{2,1,0:T(8,128)}, f32[2,32,1024]{2,1,0:T(8,128)}, u32[]{:S(2)}, u32[]{:S(2)}) collective-permute-start(f32[2,32,1024]{2,1,0:T(8,128)} %collective-permute-done.refs_0_), channel_id=1, source_target_pairs={{0,2},{1,3},{2,0},{3,1},{4,6},{5,7},{6,4},{7,5},{8,10},{9,11},{10,... | collective-permute-start | bytes 786440 | tf_op jit(solution)/shard_map/ppermute | solution.py:388
  64.3 3.5 %collective-permute-start.6 = (f32[2,32,1024]{2,1,0:T(8,128)}, f32[2,32,1024]{2,1,0:T(8,128)S(1)}, u32[]{:S(2)}, u32[]{:S(2)}) collective-permute-start(f32[2,32,1024]{2,1,0:T(8,128)} %collective-permute-done.4.refs_4_), channel_id=1, source_target_pairs={{0,1},{1,0},{2,3},{3,2},{4,5},{5,4},{6,7},{7,6},{8,9},{9,8},{10,11... | collective-permute-start | bytes 786440 | tf_op jit(solution)/shard_map/ppermute | solution.py:388
  64.3 3.5 %collective-permute-start.2 = (f32[2,32,1024]{2,1,0:T(8,128)}, f32[2,32,1024]{2,1,0:T(8,128)S(1)}, u32[]{:S(2)}, u32[]{:S(2)}) collective-permute-start(f32[2,32,1024]{2,1,0:T(8,128)} %collective-permute-done.refs_0_), channel_id=1, source_target_pairs={{0,1},{1,0},{2,3},{3,2},{4,5},{5,4},{6,7},{7,6},{8,9},{9,8},{10,11... | collective-permute-start | bytes 786440 | tf_op jit(solution)/shard_map/ppermute | solution.py:388
  64.8 3.0 %copy-start.4 = (f32[2,32,1024]{2,1,0:T(8,128)}, f32[2,32,1024]{2,1,0:T(8,128)S(1)}, u32[]{:S(2)}) copy-start(f32[2,32,1024]{2,1,0:T(8,128)S(1)} %collective-permute-done.5.refs_5_) | copy-start | bytes 786436
  64.8 3.0 %collective-permute-start.7 = (f32[2,32,1024]{2,1,0:T(8,128)S(1)}, f32[2,32,1024]{2,1,0:T(8,128)S(1)}, u32[]{:S(2)}, u32[]{:S(2)}) collective-permute-start(f32[2,32,1024]{2,1,0:T(8,128)S(1)} %collective-permute-done.5.refs_5_), channel_id=1, source_target_pairs={{0,1},{1,0},{2,3},{3,2},{4,5},{5,4},{6,7},{7,6},{8,9},{9,8},{10,11... | collective-permute-start | bytes 786440 | tf_op jit(solution)/shard_map/ppermute | solution.py:388
  64.9 2.9 %collective-permute-start.3 = (f32[2,32,1024]{2,1,0:T(8,128)}, f32[2,32,1024]{2,1,0:T(8,128)S(1)}, u32[]{:S(2)}, u32[]{:S(2)}) collective-permute-start(f32[2,32,1024]{2,1,0:T(8,128)} %collective-permute-done.1.refs_1_), channel_id=1, source_target_pairs={{0,1},{1,0},{2,3},{3,2},{4,5},{5,4},{6,7},{7,6},{8,9},{9,8},{10,11... | collective-permute-start | bytes 786440 | tf_op jit(solution)/shard_map/ppermute | solution.py:388
  67.8 0.7 copy-start.5
  67.8 0.8 copy-start.6
  67.8 0.9 copy-start.7
  67.8 0.9 copy-start.8

commit v2 on v1

v2 whole, which is shorter than its diff:
```python
import functools

import jax
import jax.numpy as jnp
import numpy as np
from jax import lax
from jax.experimental import pallas as pl
from jax.experimental.pallas import tpu as pltpu
from jax.sharding import PartitionSpec as P

F32, BF16 = jnp.float32, jnp.bfloat16
LANES = 128
PAD = 8


def iota(shape, axis):
    return lax.broadcasted_iota(jnp.int32, shape, axis)


def split(x):
    high = x.astype(BF16)
    return high, (x - high.astype(F32)).astype(BF16)


def product(a, b):
    return jnp.dot(a, b, preferred_element_type=F32)


def exact_expand(x, hot):
    one = jnp.where(hot, 1.0, 0.0).astype(BF16)
    total = None
    for part in range(3):
        head = x.astype(BF16)
        piece = product(head, one)
        total = piece if total is None else total + piece
        x = x - head.astype(F32)
    return total


def prepare_kernel(ops, first, second_high, second_low, merge, spread, *, groups):
    breadth = ops.shape[1]
    terms = ops.shape[0] // (9 * breadth)
    lo_count = LANES // breadth
    hi_count = breadth // lo_count
    per = terms // groups

    def factor(term, axis, k):
        at = ((term * 3 + axis) * 3 + k) * breadth
        return ops[at : at + breadth]

    blank = jnp.zeros((breadth, LANES - 3 * breadth), F32)
    for term in range(terms):
        for k in range(3):
            value = factor(term, 0, k)
            high = value.astype(BF16).astype(F32)
            line = jnp.concatenate([high, high, value - high, blank], axis=1)
            first[term * breadth : (term + 1) * breadth, k * LANES : (k + 1) * LANES] = line.astype(BF16)
        at = (term * 9 + 6) * breadth
        turned = ops[at : at + 3 * breadth].T
        for k in range(3):
            high, low = split(jnp.concatenate([turned[:, k * breadth : (k + 1) * breadth]] * lo_count, axis=1))
            second_high[term, k] = high
            second_low[term, k] = low
    for g in range(groups):
        for inner in range(lo_count):
            strip = [
                jnp.concatenate(
                    [factor(g * per + t, 1, k)[:, inner * hi_count : (inner + 1) * hi_count] for t in range(per)], axis=1
                )
                for k in range(3)
            ]
            high, low = split(jnp.concatenate([strip[1], strip[0]], axis=1))
            merge[g, inner * breadth : (inner + 1) * breadth] = high
            merge[g, LANES + inner * breadth : LANES + (inner + 1) * breadth] = low
            for s, k in enumerate((1, 2)):
                high = strip[k].astype(BF16).astype(F32)
                line = jnp.concatenate([high, high, strip[k] - high], axis=1)
                spread[g, s, inner * breadth : (inner + 1) * breadth] = line.astype(BF16)


def fill(xbuf, slot, block):
    breadth = block.shape[0]
    high, low = split(block)
    base = slot * LANES
    xbuf[base : base + breadth] = high
    xbuf[base + breadth : base + 2 * breadth] = low
    xbuf[base + 2 * breadth : base + 3 * breadth] = high


def place(ubuf, g, n, result):
    rows = result.shape[0]
    for h in range(result.shape[1] // LANES):
        ubuf[g, n, h, :rows] = result[:, h * LANES : (h + 1) * LANES]


def second_stage(ubuf, lbuf, tbuf, second_high, second_low, per, breadth, offsets, recipes, emit):
    volumes, count, hi_count, stride = ubuf.shape[:4]
    lo_count = LANES // breadth
    flat = ubuf.reshape(volumes * count * hi_count * stride, LANES)
    block_mask = iota((LANES, LANES), 0) // breadth == iota((LANES, LANES), 1) // breadth
    zero_block = jnp.zeros((LANES, LANES), BF16)

    def pair_body(pair, carry):
        for spot, k in enumerate(offsets):
            for half in range(2):
                term = pair * 2 + half
                high = jnp.concatenate([second_high[term, k]] * lo_count, axis=0)
                low = jnp.concatenate([second_low[term, k]] * lo_count, axis=0)
                high = jnp.where(block_mask, high, zero_block)
                low = jnp.where(block_mask, low, zero_block)
                tbuf[half, spot, :LANES, :LANES] = high
                tbuf[half, spot, LANES:, :LANES] = high
                tbuf[half, spot, :LANES, LANES:] = low
        for n in range(count):
            for half in range(2):
                term = pair * 2 + half
                for g in range(volumes):
                    base = (g * count + n) * hi_count * stride + term * breadth
                    for a in range(0, breadth, 2):
                        pieces = [flat[pl.ds(base + a + d, hi_count, stride=stride), :] for d in range(2)]
                        high, low = split(jnp.concatenate(pieces, axis=0))
                        at = a * hi_count
                        lbuf[half, g, at : at + 2 * hi_count, :LANES] = high
                        lbuf[half, g, at : at + 2 * hi_count, LANES:] = low
            results = []
            for half in range(2):
                line = []
                for recipe in recipes:
                    wide = None
                    for g, spot in recipe:
                        piece = product(lbuf[half, g], tbuf[half, spot])
                        wide = piece if wide is None else wide + piece
                    line.append(wide[:, :LANES] + wide[:, LANES:])
                results.append(line)
            for q in range(len(recipes)):
                for a in range(breadth):
                    both = jnp.concatenate(
                        [results[half][q][a * hi_count : (a + 1) * hi_count] for half in range(2)], axis=0
                    )
                    high, low = split(both)
                    emit(q, pair, (n * breadth + a) // 2, (a % 2) * LANES, high, low)
        return carry

    lax.fori_loop(0, per // 2, pair_body, 0)


def pick_diagonal(wide, breadth):
    lane_block = iota((breadth, wide.shape[1]), 1) % LANES // breadth
    total = wide[:breadth]
    for low in range(1, LANES // breadth):
        total = jnp.where(lane_block == low, wide[low * breadth : (low + 1) * breadth], total)
    return total


def turn_block(obuf, base, breadth, store):
    lo_count = LANES // breadth
    lane_of = iota((8, LANES), 1) // breadth
    for a in range(0, breadth, 8):
        for high in range(breadth // lo_count):
            total = None
            for low in range(lo_count):
                b = high * lo_count + low
                piece = obuf[pl.ds(base + a * breadth + b, 8, stride=breadth), :]
                shift = LANES // 2
                while shift >= breadth:
                    piece = piece + pltpu.roll(piece, shift, 1)
                    shift //= 2
                total = piece if total is None else jnp.where(lane_of == low, piece, total)
            store(a, high * LANES, total)


def merge_kernel(where, own, *refs, parts):
    sources = refs[:parts]
    first, second_high, second_low, third, out = refs[parts : parts + 5]
    vols, xbuf, ubuf, lbuf, tbuf, rbuf, obuf, sems = refs[parts + 5 :]
    count, breadth, width = own.shape
    per = first.shape[0] // breadth
    kgroup = per * breadth * breadth // LANES

    def copies(action):
        for n in range(count):
            for axis in range(3):
                slot = n * 3 + axis
                at = where[n, axis]
                start = 0
                for source in sources:
                    size = source.shape[0]

                    @pl.when((at >= start) & (at < start + size))
                    def _(source=source, start=start, slot=slot, at=at):
                        action(pltpu.make_async_copy(source.at[at - start], vols.at[slot], sems.at[slot]))

                    start += size

    copies(lambda c: c.start())
    for n in range(count):
        for axis in range(3):

            @pl.when(where[n, axis] < 0)
            def _(slot=n * 3 + axis):
                vols[slot] = jnp.zeros((breadth, width), F32)

    tbuf[...] = jnp.zeros(tbuf.shape, BF16)
    xbuf[...] = jnp.zeros(xbuf.shape, BF16)
    copies(lambda c: c.wait())
    for n in range(count):
        fill(xbuf, 0, vols[n * 3])
        fill(xbuf, 1, own[n])
        place(ubuf, 0, n, product(first[:, : 2 * LANES], xbuf[...]))
        for g, axis in ((1, 2), (2, 1)):
            fill(xbuf, 0, vols[n * 3 + axis])
            place(ubuf, g, n, product(first[:, LANES : 2 * LANES], xbuf[:LANES]))

    def emit(q, pair, tile, lane, high, low):
        step = high.shape[0]
        row = pl.multiple_of(q * kgroup + pair * step, step)
        rbuf[tile, pl.ds(row, step), lane : lane + LANES] = high
        rbuf[tile, pl.ds(row + 2 * kgroup, step), lane : lane + LANES] = low

    second_stage(ubuf, lbuf, tbuf, second_high, second_low, per, breadth, (1, 0), (((0, 0), (1, 1)), ((2, 0),)), emit)

    def tile_body(tile, carry):
        wide = product(third[0], rbuf[tile, : 2 * kgroup])
        wide = wide[:LANES] + wide[LANES:] + product(third[0, :LANES], rbuf[tile, 2 * kgroup :])
        total = pick_diagonal(wide, breadth)
        for d in range(2):
            row = pl.multiple_of((tile * 2 + d) * breadth, breadth)
            obuf[pl.ds(row, breadth), :] = total[:, d * LANES : (d + 1) * LANES]
        return carry

    lax.fori_loop(0, count * breadth // 2, tile_body, 0)
    for n in range(count):

        def store(a, lane, value, n=n):
            out[n, a : a + 8, lane : lane + LANES] = value

        turn_block(obuf, n * breadth * breadth, breadth, store)


def spread_kernel(where, own, *refs, resumed):
    if resumed:
        old_keep, old_send = refs[:2]
        refs = refs[2:]
    first, second_high, second_low, third, keep, send = refs[:6]
    xbuf, ubuf, lbuf, tbuf, rbuf, obuf, block = refs[6:]
    count, breadth, width = own.shape
    per = first.shape[0] // breadth
    kgroup = per * breadth * breadth // LANES
    half_slots = keep.shape[0]
    if resumed:
        keep[...] = old_keep[...]
        send[...] = old_send[...]
    else:
        keep[...] = jnp.zeros(keep.shape, F32)
        send[...] = jnp.zeros(send.shape, F32)
    tbuf[...] = jnp.zeros(tbuf.shape, BF16)
    xbuf[...] = jnp.zeros(xbuf.shape, BF16)
    for n in range(count):
        fill(xbuf, 0, own[n])
        for g in range(2):
            place(ubuf, g, n, product(first[:, (1 + g) * LANES : (2 + g) * LANES], xbuf[...]))

    def emit(q, pair, tile, lane, high, low):
        step = high.shape[0]
        row = pl.multiple_of(q * 3 * kgroup + pair * step, step)
        rbuf[tile, pl.ds(row, step), lane : lane + LANES] = high
        rbuf[tile, pl.ds(row + kgroup, step), lane : lane + LANES] = low
        rbuf[tile, pl.ds(row + 2 * kgroup, step), lane : lane + LANES] = high

    recipes = (((1, 0),), ((0, 0),), ((0, 1),))
    second_stage(ubuf, lbuf, tbuf, second_high, second_low, per, breadth, (1, 2), recipes, emit)

    def tile_body(tile, carry):
        for q in range(3):
            wide = product(third[0, 1 if q == 1 else 0], rbuf[tile, q * 3 * kgroup : (q + 1) * 3 * kgroup])
            total = pick_diagonal(wide, breadth)
            for d in range(2):
                row = pl.multiple_of((tile * 2 + d) * breadth, breadth)
                obuf[q, pl.ds(row, breadth), :] = total[:, d * LANES : (d + 1) * LANES]
        return carry

    lax.fori_loop(0, count * breadth // 2, tile_body, 0)
    for n in range(count):
        for q in range(3):

            def store(a, lane, value):
                block[a : a + 8, lane : lane + LANES] = value

            turn_block(obuf.at[q], n * breadth * breadth, breadth, store)
            slot = where[n, q]

            @pl.when((slot >= 0) & (slot < half_slots))
            def _(slot=slot):
                keep[slot] = keep[slot] + block[...]

            @pl.when(slot >= half_slots)
            def _(slot=slot):
                send[slot - half_slots] = send[slot - half_slots] + block[...]


def whole_spec(array):
    return pl.BlockSpec(array.shape, lambda i, w, rank=len(array.shape): (0,) * rank)


def group_spec(array, g, size):
    rank = len(array.shape)
    return pl.BlockSpec((size,) + array.shape[1:], lambda i, w: (g,) + (0,) * (rank - 1))


def stage_scratch(volumes, recipes, thick, count, breadth, width, per):
    hi_count = breadth * breadth // LANES
    return [
        pltpu.VMEM((volumes, count, hi_count, per * breadth + PAD, LANES), F32),
        pltpu.VMEM((2, volumes, breadth * hi_count, 2 * LANES), BF16),
        pltpu.VMEM((2, 2, 2 * LANES, 2 * LANES), BF16),
        pltpu.VMEM((count * breadth // 2, recipes * thick * per * hi_count, 2 * LANES), BF16),
    ]


def cost(count, breadth, per, units):
    return pl.CostEstimate(flops=units * per * 2 * count * breadth**4 * 200, transcendentals=0, bytes_accessed=1 << 22)


def stage_call(kernel, name, where, own, extra, extra_specs, weights, third, g, groups, out_shapes, scratch, units):
    first, second_high, second_low = weights
    breadth = own.shape[1]
    terms = second_high.shape[0]
    per = terms // groups
    return pl.pallas_call(
        kernel,
        out_shape=out_shapes,
        grid_spec=pltpu.PrefetchScalarGridSpec(
            num_scalar_prefetch=1,
            grid=(1,),
            in_specs=[whole_spec(own)]
            + extra_specs
            + [
                group_spec(first, g, per * breadth),
                group_spec(second_high, g, per),
                group_spec(second_low, g, per),
                group_spec(third, g, 1),
            ],
            out_specs=[whole_spec(shape) for shape in out_shapes],
            scratch_shapes=scratch,
        ),
        compiler_params=pltpu.CompilerParams(dimension_semantics=("arbitrary",), vmem_limit_bytes=60 << 20),
        cost_estimate=cost(own.shape[0], breadth, per, units),
        name=name,
    )(where, own, *extra, first, second_high, second_low, third)


def merge_call(where, own, parts, weights, third, g, groups):
    count, breadth, width = own.shape
    per = weights[1].shape[0] // groups
    scratch = stage_scratch(3, 2, 2, count, breadth, width, per)
    scratch = (
        [pltpu.VMEM((count * 3, breadth, width), F32), pltpu.VMEM((2 * LANES, width), BF16)]
        + scratch
        + [pltpu.VMEM((count * breadth * breadth, LANES), F32), pltpu.SemaphoreType.DMA((count * 3,))]
    )
    return stage_call(
        functools.partial(merge_kernel, parts=len(parts)),
        "merge",
        where,
        own,
        list(parts),
        [pl.BlockSpec(memory_space=pl.ANY)] * len(parts),
        weights,
        third,
        g,
        groups,
        [jax.ShapeDtypeStruct(own.shape, F32)],
        scratch,
        9,
    )[0]


def spread_call(where, own, old, slots, weights, third, g, groups):
    count, breadth, width = own.shape
    per = weights[1].shape[0] // groups
    scratch = stage_scratch(2, 3, 3, count, breadth, width, per)
    scratch = (
        [pltpu.VMEM((LANES, width), BF16)]
        + scratch
        + [pltpu.VMEM((3, count * breadth * breadth, LANES), F32), pltpu.VMEM((breadth, width), F32)]
    )
    shape = jax.ShapeDtypeStruct((slots // 2, breadth, width), F32)
    return stage_call(
        functools.partial(spread_kernel, resumed=len(old) > 0),
        "spread",
        where,
        own,
        list(old),
        [whole_spec(shape)] * len(old),
        weights,
        third,
        g,
        groups,
        [shape, shape],
        scratch,
        8,
    )


def to_row(column):
    size = column.shape[0]
    diagonal = iota((size, size), 0) == iota((size, size), 1)
    return jnp.sum(jnp.where(diagonal, column, 0.0), axis=0, keepdims=True)


def to_column(row):
    size = row.shape[1]
    diagonal = iota((size, size), 0) == iota((size, size), 1)
    return jnp.sum(jnp.where(diagonal, row, 0.0), axis=1, keepdims=True)


def place_row(slot_row, runs, run_size, capacity):
    held = slot_row.shape[1]
    run_row = jnp.zeros(slot_row.shape, F32)
    for r in range(1, runs):
        run_row = run_row + jnp.where(slot_row >= r * run_size, 1.0, 0.0)
    same = to_column(run_row) == run_row
    earlier = iota((held, held), 0) < iota((held, held), 1)
    before = jnp.sum(jnp.where(same & earlier, 1.0, 0.0), axis=0, keepdims=True)
    return run_row * capacity + before


def pack_kernel(slot_row, fine, out, stack, *, runs, run_size):
    held, volume = fine.shape
    capacity = out.shape[1]
    places = runs * capacity
    slots = slot_row[...]
    place = place_row(slots, runs, run_size, capacity)
    hit = iota((places, held), 0).astype(F32) == place
    ids = jnp.sum(jnp.where(hit, slots.astype(F32) + 1.0, 0.0), axis=1, keepdims=True)
    ids = jnp.broadcast_to(ids, (places, LANES))
    one = jnp.where(hit, 1.0, 0.0).astype(BF16)
    rest = fine[...]
    for part in range(3):
        head = rest.astype(BF16)
        stack[part * held : (part + 1) * held] = head
        rest = rest - head.astype(F32)
    packed = product(jnp.concatenate([one] * 3, axis=1), stack[...])
    for r in range(runs):
        out[r, :, :volume] = packed[r * capacity : (r + 1) * capacity]
        out[r, :, volume:] = ids[r * capacity : (r + 1) * capacity]


def unpack_kernel(slot_row, back, out, stack, *, run_size):
    held, volume = out.shape
    runs, capacity = back.shape[:2]
    places = runs * capacity
    place = to_column(place_row(slot_row[...], runs, run_size, capacity))
    hit = iota((held, places), 1).astype(F32) == place
    one = jnp.where(hit, 1.0, 0.0).astype(BF16)
    rest = jnp.concatenate([back[r] for r in range(runs)], axis=0)
    for part in range(3):
        head = rest.astype(BF16)
        stack[part * places : (part + 1) * places] = head
        rest = rest - head.astype(F32)
    out[...] = product(jnp.concatenate([one] * 3, axis=1), stack[...])


def child_code(ids, held):
    at = ids - 1.0
    return jnp.where(at < 0.0, -1.0, at - held * jnp.floor(at / held))


def row_code(index, count):
    inner = index & 7
    code = (inner >> 1) * 8 + (inner & 1) * 4 + (index >> 3)
    return jnp.where(inner < 2 * count, code.astype(F32), -2.0)


def child_rows(filter_matrix, count):
    breadth = filter_matrix.shape[0]
    half = breadth // 2
    lane = iota((breadth, half * 8), 1)
    inner = lane & 7
    hot = iota((breadth, half * 8), 0) == (inner & 1) * half + (lane >> 3)
    spread = exact_expand(filter_matrix, hot)
    return jnp.concatenate([jnp.where(inner >> 1 == n, spread, 0.0) for n in range(count)], axis=0)


def triple_lanes(x):
    high, low = split(x)
    return jnp.concatenate([high, high, low], axis=1)


def filter_kernel(got, filter_ref, out, stack, lines, cross, weave, *, count):
    runs, capacity, volume = got.shape
    volume = volume - LANES
    places = runs * capacity
    breadth = filter_ref.shape[0]
    half = breadth // 2
    width = out.shape[2]
    face = width // 4
    span = volume // face
    lo_count = LANES // breadth
    hi_count = breadth // lo_count
    matrix = filter_ref[...]
    turned = matrix.T
    lane = iota((breadth, width), 1)
    outer = lane // breadth
    across_z = exact_expand(turned, iota((breadth, width), 0) == lane % breadth)
    across_y = exact_expand(turned, iota((breadth, width), 0) == (outer % lo_count) * hi_count + outer // lo_count)
    for g in range(4):
        zs = across_z[(g & 1) * half : (g & 1) * half + half]
        for j in range(half):
            row = (g >> 1) * half + j
            high, low = split(zs * across_y[row : row + 1])
            at = (g * half + j) * half
            cross[0, at : at + half] = high
            cross[1, at : at + half] = low
    joined = jnp.concatenate([got[r] for r in range(runs)], axis=0)
    code = to_row(child_code(joined[:, volume : volume + 1], 8 * count))
    hit = row_code(iota((32, places), 0), count) == code
    one = jnp.where(hit, 1.0, 0.0).astype(BF16)
    high, low = split(joined[:, :volume])
    stack[:places] = high
    stack[places:] = low
    boxes = product(jnp.concatenate([one, one], axis=1), stack[...])
    for g in range(4):
        for i in range(0, span, 2):
            both = jnp.concatenate(
                [boxes[g * 8 : g * 8 + 8, (i + d) * face : (i + d + 1) * face] for d in range(2)], axis=0
            )
            high, low = split(both)
            lines[0, i * 8 : i * 8 + 16, g * face : (g + 1) * face] = high
            lines[1, i * 8 : i * 8 + 16, g * face : (g + 1) * face] = low
    total = product(lines[0], cross[0]) + product(lines[1], cross[0]) + product(lines[0], cross[1])
    high, low = split(total)
    size = total.shape[0]
    weave[:size] = high
    weave[size : 2 * size] = low
    weave[2 * size :] = high
    result = product(triple_lanes(child_rows(matrix, count)), weave[...])
    for n in range(count):
        out[n] = result[n * breadth : (n + 1) * breadth]


def unfilter_kernel(got, filter_ref, *refs, count, pieces):
    applied = refs[:pieces]
    out, weave, cross, stack = refs[pieces:]
    runs, capacity, volume = out.shape
    places = runs * capacity
    breadth = filter_ref.shape[0]
    half = breadth // 2
    width = applied[0].shape[2]
    face = width // 4
    size = count * breadth
    matrix = filter_ref[...]
    lane = iota((breadth, width), 1)
    octant = lane // face
    across_c = exact_expand(matrix, iota((breadth, width), 0) == octant % 2 * half + lane % half)
    across_b = exact_expand(matrix, iota((breadth, width), 0) == octant // 2 * half + lane // half % half)
    for b in range(breadth):
        high, low = split(across_c * across_b[b : b + 1])
        cross[0, b * breadth : (b + 1) * breadth] = high
        cross[1, b * breadth : (b + 1) * breadth] = low
    for n in range(count):
        total = applied[0][n]
        for piece in applied[1:]:
            total = total + piece[n]
        high, low = split(total)
        at = n * breadth
        weave[at : at + breadth] = high
        weave[size + at : size + at + breadth] = low
        weave[2 * size + at : 2 * size + at + breadth] = high
    lines = product(triple_lanes(child_rows(matrix, count).T), weave[...])
    high, low = split(lines)
    total = product(high, cross[0]) + product(low, cross[0]) + product(high, cross[1])
    for g in range(0, 4, 2):
        for i in range(total.shape[0] // 8):
            both = jnp.concatenate(
                [total[i * 8 : i * 8 + 8, (g + d) * face : (g + d + 1) * face] for d in range(2)], axis=0
            )
            high, low = split(both)
            stack[g * 8 : g * 8 + 16, i * face : (i + 1) * face] = high
            stack[32 + g * 8 : 32 + g * 8 + 16, i * face : (i + 1) * face] = low
    ids = jnp.concatenate([got[r] for r in range(runs)], axis=0)
    code = child_code(ids[:, :1], 8 * count)
    hit = row_code(iota((places, 32), 1), count) == code
    one = jnp.where(hit, 1.0, 0.0).astype(BF16)
    packed = product(jnp.concatenate([one, one], axis=1), stack[...])
    for r in range(runs):
        out[r] = packed[r * capacity : (r + 1) * capacity]


def vmem_call(kernel, out_shape, scratch, name, in_specs=None, **settings):
    extra = {} if in_specs is None else dict(grid=(1,), in_specs=in_specs)
    if in_specs is not None:
        rank = len(out_shape)
        extra["out_specs"] = pl.BlockSpec(out_shape, lambda i: (0,) * rank)
    return pl.pallas_call(
        functools.partial(kernel, **settings),
        out_shape=jax.ShapeDtypeStruct(out_shape, F32),
        scratch_shapes=[pltpu.VMEM(shape, dtype) for shape, dtype in scratch],
        compiler_params=pltpu.CompilerParams(vmem_limit_bytes=60 << 20),
        name=name,
        **extra,
    )


def moved(array, row_step, bit):
    rows = lax.axis_size("row")
    cols = lax.axis_size("col")
    pairs = [
        (r * cols + c, (r + row_step) % rows * cols + (c ^ bit)) for r in range(rows) for c in range(cols)
    ]
    return lax.ppermute(array, ("row", "col"), pairs)


def local(fine_coeffs, fine_slot, neighbours, filter_matrix, kernel_ops):
    breadth = filter_matrix.shape[0]
    terms = kernel_ops.shape[0]
    runs = lax.axis_size("row")
    cols = lax.axis_size("col")
    held, volume = fine_coeffs.shape
    par_row = neighbours.shape[0]
    count = held // 8
    capacity = 2 * (held // runs)
    places = runs * capacity
    width = breadth * breadth
    hi_count = width // LANES
    groups = 2
    per = terms // groups
    uppers = range(0, cols, 2)

    slot_row = fine_slot.reshape(1, held)
    routing = dict(run_size=8 * par_row)
    sent = vmem_call(
        pack_kernel, (runs, capacity, volume + LANES), [((3 * held, volume), BF16)], "pack", runs=runs, **routing
    )(slot_row, fine_coeffs)
    got = lax.all_to_all(sent, "row", split_axis=0, concat_axis=0, tiled=True)

    first, second_high, second_low, merge_third, spread_third = pl.pallas_call(
        functools.partial(prepare_kernel, groups=groups),
        out_shape=[
            jax.ShapeDtypeStruct((terms * breadth, 3 * LANES), BF16),
            jax.ShapeDtypeStruct((terms, 3, breadth, LANES), BF16),
            jax.ShapeDtypeStruct((terms, 3, breadth, LANES), BF16),
            jax.ShapeDtypeStruct((groups, 2 * LANES, 2 * per * hi_count), BF16),
            jax.ShapeDtypeStruct((groups, 2, LANES, 3 * per * hi_count), BF16),
        ],
        compiler_params=pltpu.CompilerParams(vmem_limit_bytes=60 << 20),
        name="prepare",
    )(kernel_ops.reshape(terms * 9 * breadth, breadth))
    weights = (first, second_high, second_low)

    col_index = lax.axis_index("col")
    mine = lax.dynamic_slice_in_dim(neighbours, col_index * count, count, 0)[:, ::2]
    within = mine % par_row
    relation = (within // count) ^ col_index
    spot = (relation % 2) * (len(uppers) * count) + relation // 2 * count + within % count
    where = jnp.where(mine >= 0, spot, -1)

    filtered = vmem_call(
        filter_kernel,
        (count, breadth, width),
        [
            ((2 * places, volume), BF16),
            ((2, breadth * 4, width), BF16),
            ((2, width, width), BF16),
            ((12 * breadth, width), BF16),
        ],
        "filter",
        count=count,
    )(got, filter_matrix)

    parts = [moved(filtered, -1, u) for u in uppers]
    spread = spread_call(where, filtered, (), par_row, weights, spread_third, 0, groups)
    parts, spread = lax.optimization_barrier((parts, spread))
    parts = parts + [moved(part, 0, 1) for part in parts]
    keep, send = spread_call(where, filtered, spread, par_row, weights, spread_third, 1, groups)
    parts, keep, send = lax.optimization_barrier((parts, keep, send))

    came = moved(send, 0, 1)
    early = merge_call(where, filtered, parts, weights, merge_third, 0, groups)
    came, early = lax.optimization_barrier((came, early))
    terms_out = [moved(keep[u // 2 * count : (u // 2 + 1) * count] + came[u // 2 * count : (u // 2 + 1) * count], 1, u) for u in uppers]
    late = merge_call(where, filtered, parts, weights, merge_third, 1, groups)

    pieces = [early, late] + terms_out
    tail = volume // LANES
    results = vmem_call(
        unfilter_kernel,
        (runs, capacity, volume),
        [
            ((3 * count * breadth, width), BF16),
            ((2, width, width), BF16),
            ((64, volume), BF16),
        ],
        "unfilter",
        in_specs=[
            pl.BlockSpec((runs, capacity, LANES), lambda i: (0, 0, tail)),
            pl.BlockSpec((breadth, breadth), lambda i: (0, 0)),
        ]
        + [pl.BlockSpec((count, breadth, width), lambda i: (0, 0, 0))] * len(pieces),
        count=count,
        pieces=len(pieces),
    )(got, filter_matrix, *pieces)
    back = lax.all_to_all(results, "row", split_axis=0, concat_axis=0, tiled=True)
    return vmem_call(unpack_kernel, (held, volume), [((3 * places, volume), BF16)], "unpack", **routing)(slot_row, back)


def solution(mesh):
    in_specs = (P(("row", "col"), None), P(("row", "col")), P("row", None), P(), P())
    out_specs = P(("row", "col"), None)
    return jax.shard_map(local, mesh=mesh, in_specs=in_specs, out_specs=out_specs, check_vma=False)
```

time: 141 us -> 132 us (0.936)
  local copies, waits for them, and re-layouts: 35.9 us -> 6.82 us
  Pallas kernels: 55.9 us -> 84.6 us
  other arithmetic: 5.23 us -> 0.63 us
  waiting for transfers between devices: 7.67 us -> 5.11 us
  starting transfers between devices: 16.1 us -> 13.9 us
    pallas_call x4 -> x8, Pallas kernels: 53.6 us -> 82.3 us  [the longest x4 67.4 us: stage_call(): pl.pallas_call(kernel, out_shape=out_shapes, grid_spec=pltpu.PrefetchScal...]
    ppermute x8 -> x7, waiting for transfers between devices: 7.67 us -> 0.02 us  [moved(): return lax.ppermute(array, ('row', 'col'), pairs)]
    another operation x4 -> x0, local copies, waits for them, and re-layouts: 7.04 us -> none  [the longest x2 6.11 us: apply_weights(): jnp.tile(jnp.transpose(factor_set[:, 2], (0, 1, 3, 2)), (1, 1, 1, lo_count))]
    reshape x8 -> x1, local copies, waits for them, and re-layouts: 7.97 us -> 2.2 us  [local(): kernel_ops.reshape(terms * 9 * breadth, breadth)]
    gather x2 -> x0, local copies, waits for them, and re-layouts: 5.23 us -> none  [apply_weights(): factor_set[:, 1][:, np.array([1, 2, 0])]]
    all_to_all x4 -> x0, local copies, waits for them, and re-layouts: 5.17 us -> none  [the longest x2 2.99 us: local(): got = lax.all_to_all(sent, 'row', split_axis=0, concat_axis=0, tiled=True)]
    all_to_all x1, waiting for transfers between devices: 0.01 us -> 5.09 us  [local(): got = lax.all_to_all(sent, 'row', split_axis=0, concat_axis=0, tiled=True)]
    slice x5 -> x1, local copies, waits for them, and re-layouts: 3.58 us -> 0.09 us  [local(): lax.dynamic_slice_in_dim(neighbours, col_index * count, count, 0)[:, ::2]]
  transfers between devices with their start and end apart: 9 -> 8, of which waited for: 2 -> 1; matrix products, arithmetic and copies ran while one was open for 25% -> 3% of each run, Pallas kernels for 0% -> 55%
where the time goes in v2:
time: 132 us; the launch traced here: 131 us
  Pallas kernels  84.6 us (64%)
  blocking collectives  19.9 us (15%)
  starting transfers between devices  13.9 us (11%)
  local copies, waits for them, and re-layouts  6.82 us (5%)
  waiting for transfers between devices  5.11 us (4%)
    pallas_call x4, Pallas kernels, stage_call(): pl.pallas_call(kernel, out_shape=out_shapes, grid_spec=pltpu.PrefetchScal...  67.4 us
    all_to_all x1, blocking collectives, local(): lax.all_to_all(results, 'row', split_axis=0, concat_axis=0, tiled=True)  19.9 us
    all_to_all x1, starting transfers between devices, local(): got = lax.all_to_all(sent, 'row', split_axis=0, concat_axis=0, tiled=True)  7.28 us
    ppermute x7, starting transfers between devices, moved(): return lax.ppermute(array, ('row', 'col'), pairs)  6.63 us
    pallas_call x1, Pallas kernels, local(): pl.pallas_call(functools.partial(prepare_kernel, groups=groups), out_shap...  5.18 us
    all_to_all x1, waiting for transfers between devices, local(): got = lax.all_to_all(sent, 'row', split_axis=0, concat_axis=0, tiled=True)  5.09 us
    unnamed x19, local copies, waits for them, and re-layouts  4.52 us
    pallas_call x1, Pallas kernels, local(): vmem_call(unfilter_kernel, (runs, capacity, volume), [((3 * count * bread...  3.91 us
  transfers between devices with their start and end apart: 8, of which 1 were waited for; matrix products, arithmetic and copies ran while one was open for 3% of the time, Pallas kernels for 55%

profile of v2, /device:TPU:0, one launch (start us, length us, event | category | flops | bytes accessed | tf_op | source)
XLA Modules:
  0.0 131.0 jit_solution(15038185603132438834)
XLA Ops:
  0.0 0.0 copy-start
  0.0 2.2 %pack.1 = f32[8,4,4224]{2,1,0:T(4,128)} custom-call(s32[1,16]{1,0:T(1,128)} %bitcast.1, f32[16,4096]{1,0:T(8,128)} %fine.1), custom_call_target="tpu_custom_call" | custom-call | tf_op jit(solution)/shard_map/pack/pallas_call | solution.py:632
  2.2 7.3 %all-to-all-start = ((f32[8,4,4224]{2,1,0:T(4,128)}), f32[8,4,4224]{2,1,0:T(4,128)S(1)}, u32[]{:S(2)}, u32[]{:S(2)}) async-start(f32[8,4,4224]{2,1,0:T(4,128)} %pack.1), calls=%async_computation | async-start | bytes 1081344 | tf_op jit(solution)/shard_map/all_to_all | solution.py:635
  9.4 0.0 copy-done
  9.5 0.1 slice.15
  9.6 1.7 %copy.7 = f32[20,3,3,1024]{3,2,1,0:T(4,128)S(1)} copy(f32[20,3,3,1024]{3,0,2,1:T(8,128)} %param.9) | data formatting | bytes 1474560 | tf_op args[4]
  11.2 2.2 %reshape.7.ops = f32[5760,32]{1,0:T(8,128)} reshape(f32[20,3,3,1024]{3,2,1,0:T(4,128)S(1)} %copy.7) | data formatting | bytes 1474560 | tf_op jit(solution)/shard_map/reshape | solution.py:648
  13.4 5.2 %prepare.1 = (bf16[640,384]{1,0:T(8,128)(2,1)}, bf16[20,3,32,128]{3,2,1,0:T(8,128)(2,1)}, bf16[20,3,32,128]{3,2,1,0:T(8,128)(2,1)}, bf16[2,256,160]{2,1,0:T(8,128)(2,1)}, bf16[2,2,128,240]{3,2,1,0:T(8,128)(2,1)}) custom-call(f32[5760,32]{1,0:T(8,128)} %reshape.7.ops), custom_call_target="tpu_custom_call" | custom-call | tf_op jit(solution)/shard_map/prepare/pallas_call | solution.py:637
  18.6 0.6 compare_select_fusion.2.where
  19.2 5.1 %all-to-all-done.got = f32[8,4,4224]{2,1,0:T(4,128)S(1)} async-done(((f32[8,4,4224]{2,1,0:T(4,128)}), f32[8,4,4224]{2,1,0:T(4,128)S(1)}, u32[]{:S(2)}, u32[]{:S(2)}) %all-to-all-start) | async-done | bytes 540704 | tf_op jit(solution)/shard_map/all_to_all | solution.py:635
  24.3 0.0 copy-start.1
  24.3 0.8 copy-done.1
  25.1 3.7 %filter.1.own = f32[2,32,1024]{2,1,0:T(8,128)} custom-call(f32[8,4,4224]{2,1,0:T(4,128)} %copy-done.1, f32[32,32]{1,0:T(8,128)} %filter_ref.3), custom_call_target="tpu_custom_call" | custom-call | tf_op jit(solution)/shard_map/filter/pallas_call | solution.py:658
  28.8 2.4 %collective-permute-start = (f32[2,32,1024]{2,1,0:T(8,128)}, f32[2,32,1024]{2,1,0:T(8,128)S(1)}, u32[]{:S(2)}, u32[]{:S(2)}) collective-permute-start(f32[2,32,1024]{2,1,0:T(8,128)} %filter.1.own), channel_id=1, source_target_pairs={{0,28},{1,29},{2,30},{3,31},{4,0},{5,1},{6,2},{7,3},{8,4},{9,5},{1... | collective-permute-start | bytes 786440 | tf_op jit(solution)/shard_map/ppermute | solution.py:611
  31.2 1.2 collective-permute-start.1
  32.4 17.6 %spread.2 = (f32[4,32,1024]{2,1,0:T(8,128)}, f32[4,32,1024]{2,1,0:T(8,128)}) custom-call(s32[2,3]{1,0:T(2,128)} %compare_select_fusion.2.where, f32[2,32,1024]{2,1,0:T(8,128)} %filter.1.own, bf16[640,384]{1,0:T(8,128)(2,1)} %get-tuple-element.26.refs_0_.refs_2_.refs_4_, bf16[20,3,32,128]{3,2,1,0:T(8,128)(2,1)} %get-tuple-element.27.refs_1_.refs_3_.refs_5_, ...), custom_call_target="tpu_custom_call" | custom-call | flops 67108864000 | bytes 4194304 | tf_op jit(solution)/shard_map/spread/pallas_call | solution.py:329
  50.0 0.0 collective-permute-done.refs_0_
  50.0 0.0 copy-start.5
  50.0 0.0 collective-permute-done.1.refs_1_
  50.0 0.0 copy-start.6
  50.0 0.1 collective-permute-start.2
  50.1 0.5 collective-permute-start.3
  50.6 17.7 %spread.3 = (f32[4,32,1024]{2,1,0:T(8,128)}, f32[4,32,1024]{2,1,0:T(8,128)}) custom-call(s32[2,3]{1,0:T(2,128)} %compare_select_fusion.2.where, f32[2,32,1024]{2,1,0:T(8,128)} %filter.1.own, f32[4,32,1024]{2,1,0:T(8,128)} %get-tuple-element.34.refs_0_, f32[4,32,1024]{2,1,0:T(8,128)} %get-tuple-element.35.refs_1_, ...), custom_call_target="tpu_custom_call" | custom-call | flops 67108864000 | bytes 4194304 | tf_op jit(solution)/shard_map/spread/pallas_call | solution.py:329
  68.2 0.0 copy-done.5
  68.2 0.0 copy-done.6
  68.3 0.0 collective-permute-done.2.refs_2_
  68.3 0.0 copy-start.7
  68.3 0.0 collective-permute-done.3.refs_3_
  68.3 0.0 copy-start.8
  68.3 0.1 collective-permute-start.4
  68.4 0.5 copy-done.7
  69.0 0.1 copy-done.8
  69.1 0.0 copy-start.2
  69.1 16.1 %merge.2.refs_0_ = f32[2,32,1024]{2,1,0:T(8,128)} custom-call(s32[2,3]{1,0:T(2,128)} %compare_select_fusion.2.where, f32[2,32,1024]{2,1,0:T(8,128)} %filter.1.own, f32[2,32,1024]{2,1,0:T(8,128)} %copy-done.5, f32[2,32,1024]{2,1,0:T(8,128)} %copy-done.6, f32[2,32,1024]{2,1,0:T(8,128)} %copy-done.7, f32[2,32,1024]{2,1,0:T(8,128)} %copy-done.8, ...), custom_call_target="tpu_custom_call" | custom-call | flops 75497472000 | bytes 4194304 | tf_op jit(solution)/shard_map/merge/pallas_call | solution.py:329
  85.2 0.0 collective-permute-done.4
  85.2 0.0 copy-done.2
  85.2 0.1 slice_add_fusion
  85.3 1.9 %collective-permute-start.5 = (f32[2,32,1024]{2,1,0:T(8,128)S(1)}, f32[2,32,1024]{2,1,0:T(8,128)S(1)}, u32[]{:S(2)}, u32[]{:S(2)}) collective-permute-start(f32[2,32,1024]{2,1,0:T(8,128)S(1)} %get-tuple-element.48), channel_id=1, source_target_pairs={{0,4},{1,5},{2,6},{3,7},{4,8},{5,9},{6,10},{7,11},{8,12},{9,13},{1... | collective-permute-start | bytes 786440 | tf_op jit(solution)/shard_map/ppermute | solution.py:611
  87.2 0.4 collective-permute-start.6
  87.6 16.0 %merge.3.refs_1_ = f32[2,32,1024]{2,1,0:T(8,128)} custom-call(s32[2,3]{1,0:T(2,128)} %compare_select_fusion.2.where, f32[2,32,1024]{2,1,0:T(8,128)} %filter.1.own, f32[2,32,1024]{2,1,0:T(8,128)} %copy-done.5, f32[2,32,1024]{2,1,0:T(8,128)} %copy-done.6, f32[2,32,1024]{2,1,0:T(8,128)} %copy-done.7, f32[2,32,1024]{2,1,0:T(8,128)} %copy-done.8, ...), custom_call_target="tpu_custom_call" | custom-call | flops 75497472000 | bytes 4194304 | tf_op jit(solution)/shard_map/merge/pallas_call | solution.py:329
  103.6 0.0 collective-permute-done.5.refs_2_
  103.6 0.0 copy-start.3
  103.7 0.0 collective-permute-done.6.refs_3_
  103.7 0.7 copy-done.3
  104.4 0.0 copy-start.4
  104.4 0.7 copy-done.4
  105.0 3.9 %unfilter.1 = f32[8,4,4096]{2,1,0:T(4,128)} custom-call(f32[8,4,4224]{2,1,0:T(4,128)} %copy-done.1, f32[32,32]{1,0:T(8,128)} %filter_ref.3, f32[2,32,1024]{2,1,0:T(8,128)} %merge.2.refs_0_, f32[2,32,1024]{2,1,0:T(8,128)} %merge.3.refs_1_, f32[2,32,1024]{2,1,0:T(8,128)} %copy-done.3, f32[2,32,1024]{2,1,0:T(8,128)} %copy-done.4), custom_call_target="tpu_custom_call" | custom-call | tf_op jit(solution)/shard_map/unfilter/pallas_call | solution.py:686
  109.0 19.9 %all_to_all.10.back = f32[8,4,4096]{2,1,0:T(4,128)} all-to-all(f32[8,4,4096]{2,1,0:T(4,128)} %unfilter.1), channel_id=1, replica_groups=mesh['row'=8,'col'=4] {'row'}, dimensions={0} | all-to-all | bytes 1048576 | tf_op jit(solution)/shard_map/all_to_all | solution.py:703
  128.8 2.2 %unpack.1 = f32[16,4096]{1,0:T(8,128)} custom-call(s32[1,16]{1,0:T(1,128)} %bitcast.2, f32[8,4,4096]{2,1,0:T(4,128)} %all_to_all.10.back), custom_call_target="tpu_custom_call" | custom-call | tf_op jit(solution)/shard_map/unpack/pallas_call | solution.py:704
  (1 shorter events, 0.0 us)
Async XLA Ops:
  0.0 9.5 %copy-start = (s32[8,6]{1,0:T(8,128)S(1)}, s32[8,6]{1,0:T(8,128)}, u32[]{:S(2)}) copy-start(s32[8,6]{1,0:T(8,128)} %param.7) | copy-start | bytes 580
  2.2 22.1 %all-to-all-start = ((f32[8,4,4224]{2,1,0:T(4,128)}), f32[8,4,4224]{2,1,0:T(4,128)S(1)}, u32[]{:S(2)}, u32[]{:S(2)}) async-start(f32[8,4,4224]{2,1,0:T(4,128)} %pack.1), calls=%async_computation | async-start | bytes 1081344 | tf_op jit(solution)/shard_map/all_to_all | solution.py:635
  24.3 0.8 copy-start.1
  28.8 21.2 %collective-permute-start = (f32[2,32,1024]{2,1,0:T(8,128)}, f32[2,32,1024]{2,1,0:T(8,128)S(1)}, u32[]{:S(2)}, u32[]{:S(2)}) collective-permute-start(f32[2,32,1024]{2,1,0:T(8,128)} %filter.1.own), channel_id=1, source_target_pairs={{0,28},{1,29},{2,30},{3,31},{4,0},{5,1},{6,2},{7,3},{8,4},{9,5},{1... | collective-permute-start | bytes 786440 | tf_op jit(solution)/shard_map/ppermute | solution.py:611
  31.2 18.8 %collective-permute-start.1 = (f32[2,32,1024]{2,1,0:T(8,128)}, f32[2,32,1024]{2,1,0:T(8,128)S(1)}, u32[]{:S(2)}, u32[]{:S(2)}) collective-permute-start(f32[2,32,1024]{2,1,0:T(8,128)} %filter.1.own), channel_id=1, source_target_pairs={{0,30},{1,31},{2,28},{3,29},{4,2},{5,3},{6,0},{7,1},{8,6},{9,7},{1... | collective-permute-start | bytes 786440 | tf_op jit(solution)/shard_map/ppermute | solution.py:611
  50.0 18.3 %copy-start.5 = (f32[2,32,1024]{2,1,0:T(8,128)}, f32[2,32,1024]{2,1,0:T(8,128)S(1)}, u32[]{:S(2)}) copy-start(f32[2,32,1024]{2,1,0:T(8,128)S(1)} %collective-permute-done.refs_0_) | copy-start | bytes 786436
  50.0 18.3 %copy-start.6 = (f32[2,32,1024]{2,1,0:T(8,128)}, f32[2,32,1024]{2,1,0:T(8,128)S(1)}, u32[]{:S(2)}) copy-start(f32[2,32,1024]{2,1,0:T(8,128)S(1)} %collective-permute-done.1.refs_1_) | copy-start | bytes 786436
  50.0 18.2 %collective-permute-start.2 = (f32[2,32,1024]{2,1,0:T(8,128)S(1)}, f32[2,32,1024]{2,1,0:T(8,128)S(1)}, u32[]{:S(2)}, u32[]{:S(2)}) collective-permute-start(f32[2,32,1024]{2,1,0:T(8,128)S(1)} %collective-permute-done.refs_0_), channel_id=1, source_target_pairs={{0,1},{1,0},{2,3},{3,2},{4,5},{5,4},{6,7},{7,6},{8,9},{9,8},{10,11... | collective-permute-start | bytes 786440 | tf_op jit(solution)/shard_map/ppermute | solution.py:611
  50.1 18.2 %collective-permute-start.3 = (f32[2,32,1024]{2,1,0:T(8,128)S(1)}, f32[2,32,1024]{2,1,0:T(8,128)S(1)}, u32[]{:S(2)}, u32[]{:S(2)}) collective-permute-start(f32[2,32,1024]{2,1,0:T(8,128)S(1)} %collective-permute-done.1.refs_1_), channel_id=1, source_target_pairs={{0,1},{1,0},{2,3},{3,2},{4,5},{5,4},{6,7},{7,6},{8,9},{9,8},{10,11... | collective-permute-start | bytes 786440 | tf_op jit(solution)/shard_map/ppermute | solution.py:611
  68.3 0.7 copy-start.7
  68.3 0.8 copy-start.8
  68.3 16.9 %collective-permute-start.4 = (f32[4,32,1024]{2,1,0:T(8,128)}, f32[4,32,1024]{2,1,0:T(8,128)S(1)}, u32[]{:S(2)}, u32[]{:S(2)}) collective-permute-start(f32[4,32,1024]{2,1,0:T(8,128)} %get-tuple-element.38), channel_id=1, source_target_pairs={{0,1},{1,0},{2,3},{3,2},{4,5},{5,4},{6,7},{7,6},{8,9},{9,8},{10,11... | collective-permute-start | bytes 1572872 | tf_op jit(solution)/shard_map/ppermute | solution.py:611
  69.1 16.1 %copy-start.2 = (f32[4,32,1024]{2,1,0:T(8,128)S(1)}, f32[4,32,1024]{2,1,0:T(8,128)}, u32[]{:S(2)}) copy-start(f32[4,32,1024]{2,1,0:T(8,128)} %get-tuple-element.45) | copy-start | bytes 1572868
  85.3 18.3 %collective-permute-start.5 = (f32[2,32,1024]{2,1,0:T(8,128)S(1)}, f32[2,32,1024]{2,1,0:T(8,128)S(1)}, u32[]{:S(2)}, u32[]{:S(2)}) collective-permute-start(f32[2,32,1024]{2,1,0:T(8,128)S(1)} %get-tuple-element.48), channel_id=1, source_target_pairs={{0,4},{1,5},{2,6},{3,7},{4,8},{5,9},{6,10},{7,11},{8,12},{9,13},{1... | collective-permute-start | bytes 786440 | tf_op jit(solution)/shard_map/ppermute | solution.py:611
  87.2 16.5 %collective-permute-start.6 = (f32[2,32,1024]{2,1,0:T(8,128)S(1)}, f32[2,32,1024]{2,1,0:T(8,128)S(1)}, u32[]{:S(2)}, u32[]{:S(2)}) collective-permute-start(f32[2,32,1024]{2,1,0:T(8,128)S(1)} %get-tuple-element.47), channel_id=1, source_target_pairs={{0,6},{1,7},{2,4},{3,5},{4,10},{5,11},{6,8},{7,9},{8,14},{9,15},{1... | collective-permute-start | bytes 786440 | tf_op jit(solution)/shard_map/ppermute | solution.py:611
  103.6 0.7 copy-start.3
  104.4 0.7 copy-start.4

commit v3 on v2

--- a/solution.py
+++ b/solution.py
@@ -157,16 +157,18 @@
     lane_of = iota((8, LANES), 1) // breadth
     for a in range(0, breadth, 8):
         for high in range(breadth // lo_count):
-            total = None
-            for low in range(lo_count):
-                b = high * lo_count + low
-                piece = obuf[pl.ds(base + a * breadth + b, 8, stride=breadth), :]
-                shift = LANES // 2
-                while shift >= breadth:
-                    piece = piece + pltpu.roll(piece, shift, 1)
-                    shift //= 2
-                total = piece if total is None else jnp.where(lane_of == low, piece, total)
-            store(a, high * LANES, total)
+            level = [
+                obuf[pl.ds(base + a * breadth + high * lo_count + low, 8, stride=breadth), :] for low in range(lo_count)
+            ]
+            step = 1
+            while step < lo_count:
+                own_side = (lane_of // step) % 2 == 0
+                level = [
+                    jnp.where(own_side, p, q) + pltpu.roll(jnp.where(own_side, q, p), step * breadth, 1)
+                    for p, q in zip(level[::2], level[1::2])
+                ]
+                step *= 2
+            store(a, high * LANES, level[0])
 
 
 def merge_kernel(where, own, *refs, parts):
@@ -192,17 +194,23 @@
 
                     start += size
 
-    copies(lambda c: c.start())
-    for n in range(count):
-        for axis in range(3):
-
-            @pl.when(where[n, axis] < 0)
-            def _(slot=n * 3 + axis):
-                vols[slot] = jnp.zeros((breadth, width), F32)
-
-    tbuf[...] = jnp.zeros(tbuf.shape, BF16)
-    xbuf[...] = jnp.zeros(xbuf.shape, BF16)
-    copies(lambda c: c.wait())
+    group = pl.program_id(0)
+
+    @pl.when(group == 0)
+    def _():
+        copies(lambda c: c.start())
+        for n in range(count):
+            for axis in range(3):
+
+                @pl.when(where[n, axis] < 0)
+                def _(slot=n * 3 + axis):
+                    vols[slot] = jnp.zeros((breadth, width), F32)
+
+        tbuf[...] = jnp.zeros(tbuf.shape, BF16)
+        xbuf[...] = jnp.zeros(xbuf.shape, BF16)
+        obuf[...] = jnp.zeros(obuf.shape, F32)
+        copies(lambda c: c.wait())
+
     for n in range(count):
         fill(xbuf, 0, vols[n * 3])
         fill(xbuf, 1, own[n])
@@ -225,36 +233,37 @@
         total = pick_diagonal(wide, breadth)
         for d in range(2):
             row = pl.multiple_of((tile * 2 + d) * breadth, breadth)
-            obuf[pl.ds(row, breadth), :] = total[:, d * LANES : (d + 1) * LANES]
+            obuf[pl.ds(row, breadth), :] = obuf[pl.ds(row, breadth), :] + total[:, d * LANES : (d + 1) * LANES]
         return carry
 
-    lax.fori_loop(0, count * breadth // 2, tile_body, 0)
-    for n in range(count):
-
-        def store(a, lane, value, n=n):
-            out[n, a : a + 8, lane : lane + LANES] = value
-
-        turn_block(obuf, n * breadth * breadth, breadth, store)
-
-
-def spread_kernel(where, own, *refs, resumed):
-    if resumed:
-        old_keep, old_send = refs[:2]
-        refs = refs[2:]
-    first, second_high, second_low, third, keep, send = refs[:6]
-    xbuf, ubuf, lbuf, tbuf, rbuf, obuf, block = refs[6:]
+    lax.fori_loop(0, count * breadth // 2, tile_body, 0, unroll=True)
+
+    @pl.when(group == pl.num_programs(0) - 1)
+    def _():
+        for n in range(count):
+
+            def store(a, lane, value, n=n):
+                out[n, a : a + 8, lane : lane + LANES] = value
+
+            turn_block(obuf, n * breadth * breadth, breadth, store)
+
+
+def spread_kernel(where, own, first, second_high, second_low, third, keep, send, *refs):
+    xbuf, ubuf, lbuf, tbuf, rbuf, obuf, block = refs
     count, breadth, width = own.shape
     per = first.shape[0] // breadth
     kgroup = per * breadth * breadth // LANES
     half_slots = keep.shape[0]
-    if resumed:
-        keep[...] = old_keep[...]
-        send[...] = old_send[...]
-    else:
+    group = pl.program_id(0)
+
+    @pl.when(group == 0)
+    def _():
         keep[...] = jnp.zeros(keep.shape, F32)
         send[...] = jnp.zeros(send.shape, F32)
-    tbuf[...] = jnp.zeros(tbuf.shape, BF16)
-    xbuf[...] = jnp.zeros(xbuf.shape, BF16)
+        tbuf[...] = jnp.zeros(tbuf.shape, BF16)
+        xbuf[...] = jnp.zeros(xbuf.shape, BF16)
+        obuf[...] = jnp.zeros(obuf.shape, F32)
+
     for n in range(count):
         fill(xbuf, 0, own[n])
         for g in range(2):
@@ -276,35 +285,40 @@
             total = pick_diagonal(wide, breadth)
             for d in range(2):
                 row = pl.multiple_of((tile * 2 + d) * breadth, breadth)
-                obuf[q, pl.ds(row, breadth), :] = total[:, d * LANES : (d + 1) * LANES]
+                obuf[q, pl.ds(row, breadth), :] = (
+                    obuf[q, pl.ds(row, breadth), :] + total[:, d * LANES : (d + 1) * LANES]
+                )
         return carry
 
-    lax.fori_loop(0, count * breadth // 2, tile_body, 0)
-    for n in range(count):
-        for q in range(3):
-
-            def store(a, lane, value):
-                block[a : a + 8, lane : lane + LANES] = value
-
-            turn_block(obuf.at[q], n * breadth * breadth, breadth, store)
-            slot = where[n, q]
-
-            @pl.when((slot >= 0) & (slot < half_slots))
-            def _(slot=slot):
-                keep[slot] = keep[slot] + block[...]
-
-            @pl.when(slot >= half_slots)
-            def _(slot=slot):
-                send[slot - half_slots] = send[slot - half_slots] + block[...]
+    lax.fori_loop(0, count * breadth // 2, tile_body, 0, unroll=True)
+
+    @pl.when(group == pl.num_programs(0) - 1)
+    def _():
+        for n in range(count):
+            for q in range(3):
+
+                def store(a, lane, value):
+                    block[a : a + 8, lane : lane + LANES] = value
+
+                turn_block(obuf.at[q], n * breadth * breadth, breadth, store)
+                slot = where[n, q]
+
+                @pl.when((slot >= 0) & (slot < half_slots))
+                def _(slot=slot):
+                    keep[slot] = keep[slot] + block[...]
+
+                @pl.when(slot >= half_slots)
+                def _(slot=slot):
+                    send[slot - half_slots] = send[slot - half_slots] + block[...]
 
 
 def whole_spec(array):
     return pl.BlockSpec(array.shape, lambda i, w, rank=len(array.shape): (0,) * rank)
 
 
-def group_spec(array, g, size):
+def group_spec(array, size):
     rank = len(array.shape)
-    return pl.BlockSpec((size,) + array.shape[1:], lambda i, w: (g,) + (0,) * (rank - 1))
+    return pl.BlockSpec((size,) + array.shape[1:], lambda i, w: (i,) + (0,) * (rank - 1))
 
 
 def stage_scratch(volumes, recipes, thick, count, breadth, width, per):
@@ -321,7 +335,7 @@
     return pl.CostEstimate(flops=units * per * 2 * count * breadth**4 * 200, transcendentals=0, bytes_accessed=1 << 22)
 
 
-def stage_call(kernel, name, where, own, extra, extra_specs, weights, third, g, groups, out_shapes, scratch, units):
+def stage_call(kernel, name, where, own, extra, extra_specs, weights, third, groups, out_shapes, scratch, units):
     first, second_high, second_low = weights
     breadth = own.shape[1]
     terms = second_high.shape[0]
@@ -331,25 +345,25 @@
         out_shape=out_shapes,
         grid_spec=pltpu.PrefetchScalarGridSpec(
             num_scalar_prefetch=1,
-            grid=(1,),
+            grid=(groups,),
             in_specs=[whole_spec(own)]
             + extra_specs
             + [
-                group_spec(first, g, per * breadth),
-                group_spec(second_high, g, per),
-                group_spec(second_low, g, per),
-                group_spec(third, g, 1),
+                group_spec(first, per * breadth),
+                group_spec(second_high, per),
+                group_spec(second_low, per),
+                group_spec(third, 1),
             ],
             out_specs=[whole_spec(shape) for shape in out_shapes],
             scratch_shapes=scratch,
         ),
         compiler_params=pltpu.CompilerParams(dimension_semantics=("arbitrary",), vmem_limit_bytes=60 << 20),
-        cost_estimate=cost(own.shape[0], breadth, per, units),
+        cost_estimate=cost(own.shape[0], breadth, terms, units),
         name=name,
     )(where, own, *extra, first, second_high, second_low, third)
 
 
-def merge_call(where, own, parts, weights, third, g, groups):
+def merge_call(where, own, parts, weights, third, groups):
     count, breadth, width = own.shape
     per = weights[1].shape[0] // groups
     scratch = stage_scratch(3, 2, 2, count, breadth, width, per)
@@ -367,7 +381,6 @@
         [pl.BlockSpec(memory_space=pl.ANY)] * len(parts),
         weights,
         third,
-        g,
         groups,
         [jax.ShapeDtypeStruct(own.shape, F32)],
         scratch,
@@ -375,7 +388,7 @@
     )[0]
 
 
-def spread_call(where, own, old, slots, weights, third, g, groups):
+def spread_call(where, own, slots, weights, third, groups):
     count, breadth, width = own.shape
     per = weights[1].shape[0] // groups
     scratch = stage_scratch(2, 3, 3, count, breadth, width, per)
@@ -386,15 +399,14 @@
     )
     shape = jax.ShapeDtypeStruct((slots // 2, breadth, width), F32)
     return stage_call(
-        functools.partial(spread_kernel, resumed=len(old) > 0),
+        spread_kernel,
         "spread",
         where,
         own,
-        list(old),
-        [whole_spec(shape)] * len(old),
+        [],
+        [],
         weights,
         third,
-        g,
         groups,
         [shape, shape],
         scratch,
@@ -669,19 +681,16 @@
     )(got, filter_matrix)
 
     parts = [moved(filtered, -1, u) for u in uppers]
-    spread = spread_call(where, filtered, (), par_row, weights, spread_third, 0, groups)
-    parts, spread = lax.optimization_barrier((parts, spread))
+    keep, send = spread_call(where, filtered, par_row, weights, spread_third, groups)
+    parts, keep, send = lax.optimization_barrier((parts, keep, send))
     parts = parts + [moved(part, 0, 1) for part in parts]
-    keep, send = spread_call(where, filtered, spread, par_row, weights, spread_third, 1, groups)
-    parts, keep, send = lax.optimization_barrier((parts, keep, send))
-
     came = moved(send, 0, 1)
-    early = merge_call(where, filtered, parts, weights, merge_third, 0, groups)
-    came, early = lax.optimization_barrier((came, early))
-    terms_out = [moved(keep[u // 2 * count : (u // 2 + 1) * count] + came[u // 2 * count : (u // 2 + 1) * count], 1, u) for u in uppers]
-    late = merge_call(where, filtered, parts, weights, merge_third, 1, groups)
-
-    pieces = [early, late] + terms_out
+
+    terms_out = []
+    for u in uppers:
+        at = u // 2 * count
+        terms_out.append(moved(keep[at : at + count] + came[at : at + count], 1, u))
+    pieces = [merge_call(where, filtered, parts, weights, merge_third, groups)] + terms_out
     tail = volume // LANES
     results = vmem_call(
         unfilter_kernel,

time: 132 us -> 104 us (0.79)
  Pallas kernels: 84.6 us -> 55.4 us
  other arithmetic: 0.63 us -> 2.48 us
  waiting for transfers between devices: 5.11 us -> 6.63 us
    pallas_call x4 -> x2, Pallas kernels: 67.4 us -> 38.2 us  [stage_call(): pl.pallas_call(kernel, out_shape=out_shapes, grid_spec=pltpu.PrefetchScal...]
    add x1, other arithmetic: 0.07 us -> 1.94 us  [local(): terms_out.append(moved(keep[at:at + count] + came[at:at + count], 1, u))]
    ppermute x7, waiting for transfers between devices: 0.02 us -> 1.55 us  [moved(): return lax.ppermute(array, ('row', 'col'), pairs)]
    unnamed x19 -> x13, local copies, waits for them, and re-layouts: 4.52 us -> 3.26 us
  transfers between devices with their start and end apart: 8 -> 8, of which waited for: 1 -> 2; matrix products, arithmetic and copies ran while one was open for 3% -> 6% of each run, Pallas kernels for 55% -> 42%
where the time goes in v3:
time: 104 us
  Pallas kernels  55.4 us (53%)
  blocking collectives  19.8 us (19%)
  starting transfers between devices  13.8 us (13%)
  waiting for transfers between devices  6.63 us (6%)
  local copies, waits for them, and re-layouts  5.57 us (5%)
  other arithmetic  2.48 us (2%)
    pallas_call x2, Pallas kernels, stage_call(): pl.pallas_call(kernel, out_shape=out_shapes, grid_spec=pltpu.PrefetchScal...  38.2 us
    all_to_all x1, blocking collectives, local(): lax.all_to_all(results, 'row', split_axis=0, concat_axis=0, tiled=True)  19.8 us
    all_to_all x1, starting transfers between devices, local(): got = lax.all_to_all(sent, 'row', split_axis=0, concat_axis=0, tiled=True)  7.28 us
    ppermute x7, starting transfers between devices, moved(): return lax.ppermute(array, ('row', 'col'), pairs)  6.51 us
    pallas_call x1, Pallas kernels, local(): pl.pallas_call(functools.partial(prepare_kernel, groups=groups), out_shap...  5.22 us
    all_to_all x1, waiting for transfers between devices, local(): got = lax.all_to_all(sent, 'row', split_axis=0, concat_axis=0, tiled=True)  5.08 us
    pallas_call x1, Pallas kernels, local(): vmem_call(unfilter_kernel, (runs, capacity, volume), [((3 * count * bread...  3.83 us
    pallas_call x1, Pallas kernels, local(): vmem_call(filter_kernel, (count, breadth, width), [((2 * places, volume),...  3.71 us
  transfers between devices with their start and end apart: 8, of which 2 were waited for; matrix products, arithmetic and copies ran while one was open for 6% of the time, Pallas kernels for 42%

profile of v3, /device:TPU:0, one launch (start us, length us, event | category | flops | bytes accessed | tf_op | source)
XLA Modules:
  0.0 103.7 jit_solution(7892023861708576005)
XLA Ops:
  0.0 0.0 copy-start
  0.0 2.1 %pack.1 = f32[8,4,4224]{2,1,0:T(4,128)} custom-call(s32[1,16]{1,0:T(1,128)} %bitcast.1, f32[16,4096]{1,0:T(8,128)} %fine.1), custom_call_target="tpu_custom_call" | custom-call | tf_op jit(solution)/shard_map/pack/pallas_call | solution.py:644
  2.2 7.3 %all-to-all-start = ((f32[8,4,4224]{2,1,0:T(4,128)}), f32[8,4,4224]{2,1,0:T(4,128)S(1)}, u32[]{:S(2)}, u32[]{:S(2)}) async-start(f32[8,4,4224]{2,1,0:T(4,128)} %pack.1), calls=%async_computation | async-start | bytes 1081344 | tf_op jit(solution)/shard_map/all_to_all | solution.py:647
  9.4 0.0 copy-done
  9.5 0.1 slice.15
  9.5 1.7 %copy.7 = f32[20,3,3,1024]{3,2,1,0:T(4,128)S(1)} copy(f32[20,3,3,1024]{3,0,2,1:T(8,128)} %param.9) | data formatting | bytes 1474560 | tf_op args[4]
  11.2 2.2 %reshape.7.ops = f32[5760,32]{1,0:T(8,128)} reshape(f32[20,3,3,1024]{3,2,1,0:T(4,128)S(1)} %copy.7) | data formatting | bytes 1474560 | tf_op jit(solution)/shard_map/reshape | solution.py:660
  13.4 5.2 %prepare.1 = (bf16[640,384]{1,0:T(8,128)(2,1)}, bf16[20,3,32,128]{3,2,1,0:T(8,128)(2,1)}, bf16[20,3,32,128]{3,2,1,0:T(8,128)(2,1)}, bf16[2,256,160]{2,1,0:T(8,128)(2,1)}, bf16[2,2,128,240]{3,2,1,0:T(8,128)(2,1)}) custom-call(f32[5760,32]{1,0:T(8,128)} %reshape.7.ops), custom_call_target="tpu_custom_call" | custom-call | tf_op jit(solution)/shard_map/prepare/pallas_call | solution.py:649
  18.6 0.5 compare_select_fusion.2.where
  19.2 5.1 %all-to-all-done.got = f32[8,4,4224]{2,1,0:T(4,128)S(1)} async-done(((f32[8,4,4224]{2,1,0:T(4,128)}), f32[8,4,4224]{2,1,0:T(4,128)S(1)}, u32[]{:S(2)}, u32[]{:S(2)}) %all-to-all-start) | async-done | bytes 540704 | tf_op jit(solution)/shard_map/all_to_all | solution.py:647
  24.3 0.0 copy-start.1
  24.3 0.8 copy-done.1
  25.1 3.7 %filter.1.own = f32[2,32,1024]{2,1,0:T(8,128)} custom-call(f32[8,4,4224]{2,1,0:T(4,128)} %copy-done.1, f32[32,32]{1,0:T(8,128)} %filter_ref.3), custom_call_target="tpu_custom_call" | custom-call | tf_op jit(solution)/shard_map/filter/pallas_call | solution.py:670
  28.8 2.4 %collective-permute-start = (f32[2,32,1024]{2,1,0:T(8,128)}, f32[2,32,1024]{2,1,0:T(8,128)S(1)}, u32[]{:S(2)}, u32[]{:S(2)}) collective-permute-start(f32[2,32,1024]{2,1,0:T(8,128)} %filter.1.own), channel_id=1, source_target_pairs={{0,28},{1,29},{2,30},{3,31},{4,0},{5,1},{6,2},{7,3},{8,4},{9,5},{1... | collective-permute-start | bytes 786440 | tf_op jit(solution)/shard_map/ppermute | solution.py:623
  31.2 1.2 %collective-permute-start.1 = (f32[2,32,1024]{2,1,0:T(8,128)}, f32[2,32,1024]{2,1,0:T(8,128)S(1)}, u32[]{:S(2)}, u32[]{:S(2)}) collective-permute-start(f32[2,32,1024]{2,1,0:T(8,128)} %filter.1.own), channel_id=1, source_target_pairs={{0,30},{1,31},{2,28},{3,29},{4,2},{5,3},{6,0},{7,1},{8,6},{9,7},{1... | collective-permute-start | bytes 786440 | tf_op jit(solution)/shard_map/ppermute | solution.py:623
  32.4 19.0 %spread.1 = (f32[4,32,1024]{2,1,0:T(8,128)}, f32[4,32,1024]{2,1,0:T(8,128)}) custom-call(s32[2,3]{1,0:T(2,128)} %compare_select_fusion.2.where, f32[2,32,1024]{2,1,0:T(8,128)} %filter.1.own, bf16[640,384]{1,0:T(8,128)(2,1)} %get-tuple-element.16.first.refs_4_, bf16[20,3,32,128]{3,2,1,0:T(8,128)(2,1)} %get-tuple-element.17.second_high.refs_5_, ...), custom_call_target="tpu_custom_call" | custom-call | flops 134217728000 | bytes 4194304 | tf_op jit(solution)/shard_map/spread/pallas_call | solution.py:343
  51.4 0.0 collective-permute-done.refs_0_
  51.4 0.0 copy-start.2
  51.4 0.0 collective-permute-done.1.refs_1_
  51.4 0.0 copy-start.3
  51.4 0.1 collective-permute-start.4
  51.5 0.5 collective-permute-start.2
  52.0 0.1 collective-permute-start.3
  52.1 1.5 %collective-permute-done.4 = f32[4,32,1024]{2,1,0:T(8,128)S(1)} collective-permute-done((f32[4,32,1024]{2,1,0:T(8,128)}, f32[4,32,1024]{2,1,0:T(8,128)S(1)}, u32[]{:S(2)}, u32[]{:S(2)}) %collective-permute-start.4) | collective-permute-done | bytes 524320 | tf_op jit(solution)/shard_map/ppermute | solution.py:623
  53.6 1.9 %slice_add_fusion = (f32[2,32,1024]{2,1,0:T(8,128)}, f32[2,32,1024]{2,1,0:T(8,128)}) fusion(f32[4,32,1024]{2,1,0:T(8,128)S(1)} %collective-permute-done.4, f32[4,32,1024]{2,1,0:T(8,128)} %get-tuple-element.25), kind=kLoop, calls=%fused_computation | loop fusion | flops 131072 | bytes 1572864 | tf_op jit(solution)/shard_map/add | solution.py:692
  55.5 1.8 %collective-permute-start.5 = (f32[2,32,1024]{2,1,0:T(8,128)}, f32[2,32,1024]{2,1,0:T(8,128)}, u32[]{:S(2)}, u32[]{:S(2)}) collective-permute-start(f32[2,32,1024]{2,1,0:T(8,128)} %get-tuple-element.28), channel_id=1, source_target_pairs={{0,4},{1,5},{2,6},{3,7},{4,8},{5,9},{6,10},{7,11},{8,12},{9,13},{1... | collective-permute-start | bytes 786440 | tf_op jit(solution)/shard_map/ppermute | solution.py:623
  57.3 0.5 collective-permute-start.6
  57.8 0.0 collective-permute-done.2.refs_2_
  57.8 0.0 copy-start.4
  57.8 0.0 collective-permute-done.3.refs_3_
  57.8 0.0 copy-start.5
  57.8 0.0 copy-done.2
  57.8 0.0 copy-done.3
  57.8 0.7 copy-done.4
  58.5 0.1 copy-done.5
  58.6 19.3 %merge.1.refs_0_ = f32[2,32,1024]{2,1,0:T(8,128)} custom-call(s32[2,3]{1,0:T(2,128)} %compare_select_fusion.2.where, f32[2,32,1024]{2,1,0:T(8,128)} %filter.1.own, f32[2,32,1024]{2,1,0:T(8,128)} %copy-done.2, f32[2,32,1024]{2,1,0:T(8,128)} %copy-done.3, f32[2,32,1024]{2,1,0:T(8,128)} %copy-done.4, f32[2,32,1024]{2,1,0:T(8,128)} %copy-done.5, ...), custom_call_target="tpu_custom_call" | custom-call | flops 150994944000 | bytes 4194304 | tf_op jit(solution)/shard_map/merge/pallas_call | solution.py:343
  77.9 0.0 collective-permute-done.5.refs_1_
  77.9 0.0 collective-permute-done.6.refs_2_
  77.9 3.8 %unfilter.1 = f32[8,4,4096]{2,1,0:T(4,128)} custom-call(f32[8,4,4224]{2,1,0:T(4,128)} %copy-done.1, f32[32,32]{1,0:T(8,128)} %filter_ref.3, f32[2,32,1024]{2,1,0:T(8,128)} %merge.1.refs_0_, f32[2,32,1024]{2,1,0:T(8,128)} %collective-permute-done.5.refs_1_, f32[2,32,1024]{2,1,0:T(8,128)} %collective-permute-done.6.refs_2_), custom_call_target="tpu_custom_call" | custom-call | tf_op jit(solution)/shard_map/unfilter/pallas_call | solution.py:695
  81.7 19.8 %all_to_all.10.back = f32[8,4,4096]{2,1,0:T(4,128)} all-to-all(f32[8,4,4096]{2,1,0:T(4,128)} %unfilter.1), channel_id=1, replica_groups=mesh['row'=8,'col'=4] {'row'}, dimensions={0} | all-to-all | bytes 1048576 | tf_op jit(solution)/shard_map/all_to_all | solution.py:712
  101.5 2.2 %unpack.1 = f32[16,4096]{1,0:T(8,128)} custom-call(s32[1,16]{1,0:T(1,128)} %bitcast.2, f32[8,4,4096]{2,1,0:T(4,128)} %all_to_all.10.back), custom_call_target="tpu_custom_call" | custom-call | tf_op jit(solution)/shard_map/unpack/pallas_call | solution.py:713
  (1 shorter events, 0.0 us)
Async XLA Ops:
  0.0 9.4 %copy-start = (s32[8,6]{1,0:T(8,128)S(1)}, s32[8,6]{1,0:T(8,128)}, u32[]{:S(2)}) copy-start(s32[8,6]{1,0:T(8,128)} %param.7) | copy-start | bytes 580
  2.2 22.1 %all-to-all-start = ((f32[8,4,4224]{2,1,0:T(4,128)}), f32[8,4,4224]{2,1,0:T(4,128)S(1)}, u32[]{:S(2)}, u32[]{:S(2)}) async-start(f32[8,4,4224]{2,1,0:T(4,128)} %pack.1), calls=%async_computation | async-start | bytes 1081344 | tf_op jit(solution)/shard_map/all_to_all | solution.py:647
  24.3 0.8 copy-start.1
  28.8 22.6 %collective-permute-start = (f32[2,32,1024]{2,1,0:T(8,128)}, f32[2,32,1024]{2,1,0:T(8,128)S(1)}, u32[]{:S(2)}, u32[]{:S(2)}) collective-permute-start(f32[2,32,1024]{2,1,0:T(8,128)} %filter.1.own), channel_id=1, source_target_pairs={{0,28},{1,29},{2,30},{3,31},{4,0},{5,1},{6,2},{7,3},{8,4},{9,5},{1... | collective-permute-start | bytes 786440 | tf_op jit(solution)/shard_map/ppermute | solution.py:623
  31.2 20.2 %collective-permute-start.1 = (f32[2,32,1024]{2,1,0:T(8,128)}, f32[2,32,1024]{2,1,0:T(8,128)S(1)}, u32[]{:S(2)}, u32[]{:S(2)}) collective-permute-start(f32[2,32,1024]{2,1,0:T(8,128)} %filter.1.own), channel_id=1, source_target_pairs={{0,30},{1,31},{2,28},{3,29},{4,2},{5,3},{6,0},{7,1},{8,6},{9,7},{1... | collective-permute-start | bytes 786440 | tf_op jit(solution)/shard_map/ppermute | solution.py:623
  51.4 6.4 %copy-start.2 = (f32[2,32,1024]{2,1,0:T(8,128)}, f32[2,32,1024]{2,1,0:T(8,128)S(1)}, u32[]{:S(2)}) copy-start(f32[2,32,1024]{2,1,0:T(8,128)S(1)} %collective-permute-done.refs_0_) | copy-start | bytes 786436
  51.4 6.4 %copy-start.3 = (f32[2,32,1024]{2,1,0:T(8,128)}, f32[2,32,1024]{2,1,0:T(8,128)S(1)}, u32[]{:S(2)}) copy-start(f32[2,32,1024]{2,1,0:T(8,128)S(1)} %collective-permute-done.1.refs_1_) | copy-start | bytes 786436
  51.4 2.2 %collective-permute-start.4 = (f32[4,32,1024]{2,1,0:T(8,128)}, f32[4,32,1024]{2,1,0:T(8,128)S(1)}, u32[]{:S(2)}, u32[]{:S(2)}) collective-permute-start(f32[4,32,1024]{2,1,0:T(8,128)} %get-tuple-element.26), channel_id=1, source_target_pairs={{0,1},{1,0},{2,3},{3,2},{4,5},{5,4},{6,7},{7,6},{8,9},{9,8},{10,11... | collective-permute-start | bytes 1572872 | tf_op jit(solution)/shard_map/ppermute | solution.py:623
  51.5 6.3 %collective-permute-start.2 = (f32[2,32,1024]{2,1,0:T(8,128)S(1)}, f32[2,32,1024]{2,1,0:T(8,128)S(1)}, u32[]{:S(2)}, u32[]{:S(2)}) collective-permute-start(f32[2,32,1024]{2,1,0:T(8,128)S(1)} %collective-permute-done.refs_0_), channel_id=1, source_target_pairs={{0,1},{1,0},{2,3},{3,2},{4,5},{5,4},{6,7},{7,6},{8,9},{9,8},{10,11... | collective-permute-start | bytes 786440 | tf_op jit(solution)/shard_map/ppermute | solution.py:623
  52.0 5.8 %collective-permute-start.3 = (f32[2,32,1024]{2,1,0:T(8,128)S(1)}, f32[2,32,1024]{2,1,0:T(8,128)S(1)}, u32[]{:S(2)}, u32[]{:S(2)}) collective-permute-start(f32[2,32,1024]{2,1,0:T(8,128)S(1)} %collective-permute-done.1.refs_1_), channel_id=1, source_target_pairs={{0,1},{1,0},{2,3},{3,2},{4,5},{5,4},{6,7},{7,6},{8,9},{9,8},{10,11... | collective-permute-start | bytes 786440 | tf_op jit(solution)/shard_map/ppermute | solution.py:623
  55.5 22.3 %collective-permute-start.5 = (f32[2,32,1024]{2,1,0:T(8,128)}, f32[2,32,1024]{2,1,0:T(8,128)}, u32[]{:S(2)}, u32[]{:S(2)}) collective-permute-start(f32[2,32,1024]{2,1,0:T(8,128)} %get-tuple-element.28), channel_id=1, source_target_pairs={{0,4},{1,5},{2,6},{3,7},{4,8},{5,9},{6,10},{7,11},{8,12},{9,13},{1... | collective-permute-start | bytes 786440 | tf_op jit(solution)/shard_map/ppermute | solution.py:623
  57.3 20.6 %collective-permute-start.6 = (f32[2,32,1024]{2,1,0:T(8,128)}, f32[2,32,1024]{2,1,0:T(8,128)}, u32[]{:S(2)}, u32[]{:S(2)}) collective-permute-start(f32[2,32,1024]{2,1,0:T(8,128)} %get-tuple-element.27), channel_id=1, source_target_pairs={{0,6},{1,7},{2,4},{3,5},{4,10},{5,11},{6,8},{7,9},{8,14},{9,15},{1... | collective-permute-start | bytes 786440 | tf_op jit(solution)/shard_map/ppermute | solution.py:623
  57.8 0.7 copy-start.4
  57.8 0.8 copy-start.5

commit v4 on v3

--- a/solution.py
+++ b/solution.py
@@ -357,7 +357,7 @@
             out_specs=[whole_spec(shape) for shape in out_shapes],
             scratch_shapes=scratch,
         ),
-        compiler_params=pltpu.CompilerParams(dimension_semantics=("arbitrary",), vmem_limit_bytes=60 << 20),
+        compiler_params=pltpu.CompilerParams(dimension_semantics=("arbitrary",), vmem_limit_bytes=30 << 20),
         cost_estimate=cost(own.shape[0], breadth, terms, units),
         name=name,
     )(where, own, *extra, first, second_high, second_low, third)
@@ -608,7 +608,7 @@
         functools.partial(kernel, **settings),
         out_shape=jax.ShapeDtypeStruct(out_shape, F32),
         scratch_shapes=[pltpu.VMEM(shape, dtype) for shape, dtype in scratch],
-        compiler_params=pltpu.CompilerParams(vmem_limit_bytes=60 << 20),
+        compiler_params=pltpu.CompilerParams(vmem_limit_bytes=30 << 20),
         name=name,
         **extra,
     )
@@ -655,7 +655,7 @@
             jax.ShapeDtypeStruct((groups, 2 * LANES, 2 * per * hi_count), BF16),
             jax.ShapeDtypeStruct((groups, 2, LANES, 3 * per * hi_count), BF16),
         ],
-        compiler_params=pltpu.CompilerParams(vmem_limit_bytes=60 << 20),
+        compiler_params=pltpu.CompilerParams(vmem_limit_bytes=30 << 20),
         name="prepare",
     )(kernel_ops.reshape(terms * 9 * breadth, breadth))
     weights = (first, second_high, second_low)

time: 104 us -> 97 us (0.933)
  Pallas kernels: 55.4 us -> 43.1 us
  local copies, waits for them, and re-layouts: 5.57 us -> 14.8 us
  waiting for transfers between devices: 6.63 us -> 4.59 us
  other arithmetic: 2.48 us -> 0.91 us
    unnamed x13 -> x31, local copies, waits for them, and re-layouts: 3.26 us -> 12.1 us
    pallas_call x2, Pallas kernels: 38.2 us -> 33.5 us  [stage_call(): pl.pallas_call(kernel, out_shape=out_shapes, grid_spec=pltpu.PrefetchScal...]
    pallas_call x1, Pallas kernels: 5.22 us -> 2.37 us  [local(): pl.pallas_call(functools.partial(prepare_kernel, groups=groups), out_shap...]
    all_to_all x1, waiting for transfers between devices: 5.08 us -> 3.25 us  [local(): got = lax.all_to_all(sent, 'row', split_axis=0, concat_axis=0, tiled=True)]
    pallas_call x1, Pallas kernels: 3.71 us -> 1.97 us  [local(): vmem_call(filter_kernel, (count, breadth, width), [((2 * places, volume),...]
    add x1, other arithmetic: 1.94 us -> 0.88 us  [local(): terms_out.append(moved(keep[at:at + count] + came[at:at + count], 1, u))]
    pallas_call x1, Pallas kernels: 2.21 us -> 1.16 us  [local(): vmem_call(unpack_kernel, (held, volume), [((3 * places, volume), BF16)],...]
  transfers between devices with their start and end apart: 8 -> 8, of which waited for: 2 -> 2; matrix products, arithmetic and copies ran while one was open for 6% -> 6% of each run, Pallas kernels for 42% -> 37%
where the time goes in v4:
time: 97 us; the launch traced here: 96.5 us
  Pallas kernels  43.1 us (44%)
  blocking collectives  19.2 us (20%)
  local copies, waits for them, and re-layouts  14.8 us (15%)
  starting transfers between devices  13.8 us (14%)
  waiting for transfers between devices  4.59 us (5%)
    pallas_call x2, Pallas kernels, stage_call(): pl.pallas_call(kernel, out_shape=out_shapes, grid_spec=pltpu.PrefetchScal...  33.5 us
    all_to_all x1, blocking collectives, local(): lax.all_to_all(results, 'row', split_axis=0, concat_axis=0, tiled=True)  19.2 us
    unnamed x31, local copies, waits for them, and re-layouts  12.1 us
    all_to_all x1, starting transfers between devices, local(): got = lax.all_to_all(sent, 'row', split_axis=0, concat_axis=0, tiled=True)  7.28 us
    ppermute x7, starting transfers between devices, moved(): return lax.ppermute(array, ('row', 'col'), pairs)  6.49 us
    all_to_all x1, waiting for transfers between devices, local(): got = lax.all_to_all(sent, 'row', split_axis=0, concat_axis=0, tiled=True)  3.25 us
    pallas_call x1, Pallas kernels, local(): vmem_call(unfilter_kernel, (runs, capacity, volume), [((3 * count * bread...  2.91 us
    reshape x1, local copies, waits for them, and re-layouts, local(): kernel_ops.reshape(terms * 9 * breadth, breadth)  2.6 us
  transfers between devices with their start and end apart: 8, of which 2 were waited for; matrix products, arithmetic and copies ran while one was open for 6% of the time, Pallas kernels for 37%

profile of v4, /device:TPU:0, one launch (start us, length us, event | category | flops | bytes accessed | tf_op | source)
XLA Modules:
  0.0 96.5 jit_solution(17637171151564900557)
XLA Ops:
  0.0 0.0 copy-start
  0.0 0.0 copy-start.1
  0.0 1.0 copy-done.1
  1.0 0.0 copy-start.3
  1.0 0.7 copy-done.3
  1.6 1.2 %pack.1 = f32[8,4,4224]{2,1,0:T(4,128)} custom-call(s32[1,16]{1,0:T(1,128)S(1)} %bitcast.1, f32[16,4096]{1,0:T(8,128)S(1)} %copy-done.1), custom_call_target="tpu_custom_call" | custom-call | tf_op jit(solution)/shard_map/pack/pallas_call | solution.py:644
  2.8 7.3 %all-to-all-start = ((f32[8,4,4224]{2,1,0:T(4,128)}), f32[8,4,4224]{2,1,0:T(4,128)S(1)}, u32[]{:S(2)}, u32[]{:S(2)}) async-start(f32[8,4,4224]{2,1,0:T(4,128)} %pack.1), calls=%async_computation | async-start | bytes 1081344 | tf_op jit(solution)/shard_map/all_to_all | solution.py:647
  10.1 0.0 copy-done
  10.1 0.1 slice.15
  10.2 2.7 %copy.7 = f32[20,3,3,1024]{3,2,1,0:T(4,128)} copy(f32[20,3,3,1024]{3,0,2,1:T(8,128)} %param.9) | data formatting | bytes 1474560 | tf_op args[4]
  12.9 0.0 copy-start.2
  12.9 2.6 %reshape.7.ops = f32[5760,32]{1,0:T(8,128)S(1)} reshape(f32[20,3,3,1024]{3,2,1,0:T(4,128)} %copy.7) | data formatting | bytes 1474560 | tf_op jit(solution)/shard_map/reshape | solution.py:660
  15.5 2.4 %prepare.1 = (bf16[640,384]{1,0:T(8,128)(2,1)S(1)}, bf16[20,3,32,128]{3,2,1,0:T(8,128)(2,1)S(1)}, bf16[20,3,32,128]{3,2,1,0:T(8,128)(2,1)S(1)}, bf16[2,256,160]{...) custom-call(f32[5760,32]{1,0:T(8,128)S(1)} %reshape.7.ops), custom_call_target="tpu_custom_call" | custom-call | tf_op jit(solution)/shard_map/prepare/pallas_call | solution.py:649
  17.8 0.0 copy-start.5
  17.8 0.8 copy-done.5
  18.6 0.0 copy-start.7
  18.6 0.8 copy-done.7
  19.4 0.0 copy-start.9
  19.4 0.8 copy-done.9
  20.2 0.0 copy-start.11
  20.2 0.7 copy-done.11
  20.9 0.0 copy-start.13
  20.9 0.7 copy-done.13
  21.7 3.2 %all-to-all-done.got = f32[8,4,4224]{2,1,0:T(4,128)S(1)} async-done(((f32[8,4,4224]{2,1,0:T(4,128)}), f32[8,4,4224]{2,1,0:T(4,128)S(1)}, u32[]{:S(2)}, u32[]{:S(2)}) %all-to-all-start) | async-done | bytes 540704 | tf_op jit(solution)/shard_map/all_to_all | solution.py:647
  24.9 0.0 copy-done.2
  24.9 2.0 %filter.1.own = f32[2,32,1024]{2,1,0:T(8,128)S(1)} custom-call(f32[8,4,4224]{2,1,0:T(4,128)S(1)} %all-to-all-done.got, f32[32,32]{1,0:T(8,128)S(1)} %copy-done.2), custom_call_target="tpu_custom_call" | custom-call | tf_op jit(solution)/shard_map/filter/pallas_call | solution.py:670
  26.9 2.4 %collective-permute-start = (f32[2,32,1024]{2,1,0:T(8,128)S(1)}, f32[2,32,1024]{2,1,0:T(8,128)S(1)}, u32[]{:S(2)}, u32[]{:S(2)}) collective-permute-start(f32[2,32,1024]{2,1,0:T(8,128)S(1)} %filter.1.own), channel_id=1, source_target_pairs={{0,28},{1,29},{2,30},{3,31},{4,0},{5,1},{6,2},{7,3},{8,4},{9,5},{1... | collective-permute-start | bytes 786440 | tf_op jit(solution)/shard_map/ppermute | solution.py:623
  29.3 1.2 %collective-permute-start.1 = (f32[2,32,1024]{2,1,0:T(8,128)S(1)}, f32[2,32,1024]{2,1,0:T(8,128)S(1)}, u32[]{:S(2)}, u32[]{:S(2)}) collective-permute-start(f32[2,32,1024]{2,1,0:T(8,128)S(1)} %filter.1.own), channel_id=1, source_target_pairs={{0,30},{1,31},{2,28},{3,29},{4,2},{5,3},{6,0},{7,1},{8,6},{9,7},{1... | collective-permute-start | bytes 786440 | tf_op jit(solution)/shard_map/ppermute | solution.py:623
  30.6 0.0 copy-start.6
  30.6 1.0 %copy-done.6 = bf16[640,384]{1,0:T(8,128)(2,1)S(1)} copy-done((bf16[640,384]{1,0:T(8,128)(2,1)S(1)}, bf16[640,384]{1,0:T(8,128)(2,1)}, u32[]{:S(2)}) %copy-start.6) | copy-done | bytes 491544
  31.6 0.0 copy-start.8
  31.6 1.0 %copy-done.8 = bf16[20,3,32,128]{3,2,1,0:T(8,128)(2,1)S(1)} copy-done((bf16[20,3,32,128]{3,2,1,0:T(8,128)(2,1)S(1)}, bf16[20,3,32,128]{3,2,1,0:T(8,128)(2,1)}, u32[]{:S(2)}) %copy-start.8) | copy-done | bytes 491544
  32.6 0.0 copy-start.10
  32.6 1.0 %copy-done.10 = bf16[20,3,32,128]{3,2,1,0:T(8,128)(2,1)S(1)} copy-done((bf16[20,3,32,128]{3,2,1,0:T(8,128)(2,1)S(1)}, bf16[20,3,32,128]{3,2,1,0:T(8,128)(2,1)}, u32[]{:S(2)}) %copy-start.10) | copy-done | bytes 491544
  33.6 0.0 copy-start.14
  33.6 0.9 copy-done.14
  34.6 0.0 copy-start.12
  34.6 16.4 %spread.1 = (f32[4,32,1024]{2,1,0:T(8,128)S(1)}, f32[4,32,1024]{2,1,0:T(8,128)S(1)}) custom-call(s32[2,3]{1,0:T(2,128)S(1)} %compare_select_fusion.2.where, f32[2,32,1024]{2,1,0:T(8,128)S(1)} %filter.1.own, bf16[640,384]{1,0:T(8,128)(2,1)S(1)} %copy-done.6, bf16[20,3,32,128]{3,2,1,0:T(8,128)(2,1)S(1)} %copy-done.8, bf16[20,3,32,128]{3,2,1,0:T(8,128)(2,1)S(1)} %copy-done.10, ...), custom_call_target="tpu_custom_call" | custom-call | flops 134217728000 | bytes 4194304 | tf_op jit(solution)/shard_map/spread/pallas_call | solution.py:343
  51.0 0.0 collective-permute-done.refs_0_
  51.0 0.0 collective-permute-done.1.refs_1_
  51.0 0.1 collective-permute-start.4
  51.1 0.5 collective-permute-start.2
  51.6 0.1 collective-permute-start.3
  51.6 1.3 %collective-permute-done.4 = f32[4,32,1024]{2,1,0:T(8,128)S(1)} collective-permute-done((f32[4,32,1024]{2,1,0:T(8,128)S(1)}, f32[4,32,1024]{2,1,0:T(8,128)S(1)}, u32[]{:S(2)}, u32[]{:S(2)}) %collective-permute-start.4) | collective-permute-done | bytes 524320 | tf_op jit(solution)/shard_map/ppermute | solution.py:623
  53.0 0.9 slice_add_fusion
  53.8 1.7 %collective-permute-start.5 = (f32[2,32,1024]{2,1,0:T(8,128)}, f32[2,32,1024]{2,1,0:T(8,128)}, u32[]{:S(2)}, u32[]{:S(2)}) collective-permute-start(f32[2,32,1024]{2,1,0:T(8,128)} %get-tuple-element.28), channel_id=1, source_target_pairs={{0,4},{1,5},{2,6},{3,7},{4,8},{5,9},{6,10},{7,11},{8,12},{9,13},{1... | collective-permute-start | bytes 786440 | tf_op jit(solution)/shard_map/ppermute | solution.py:623
  55.6 0.5 collective-permute-start.6
  56.0 0.0 collective-permute-done.2.refs_2_
  56.0 0.0 collective-permute-done.3.refs_3_
  56.0 0.0 copy-done.12
  56.0 0.0 copy-start.4
  56.1 17.2 %merge.1.refs_0_ = f32[2,32,1024]{2,1,0:T(8,128)S(1)} custom-call(s32[2,3]{1,0:T(2,128)S(1)} %compare_select_fusion.2.where, f32[2,32,1024]{2,1,0:T(8,128)S(1)} %filter.1.own, f32[2,32,1024]{2,1,0:T(8,128)S(1)} %collective-permute-done.refs_0_, f32[2,32,1024]{2,1,0:T(8,128)S(1)} %collective-permute-done.1.refs_1_, ...), custom_call_target="tpu_custom_call" | custom-call | flops 150994944000 | bytes 4194304 | tf_op jit(solution)/shard_map/merge/pallas_call | solution.py:343
  73.2 0.0 collective-permute-done.5.refs_1_
  73.2 0.0 collective-permute-done.6.refs_2_
  73.2 2.9 %unfilter.1 = f32[8,4,4096]{2,1,0:T(4,128)S(1)} custom-call(f32[8,4,4224]{2,1,0:T(4,128)S(1)} %all-to-all-done.got, f32[32,32]{1,0:T(8,128)S(1)} %copy-done.2, f32[2,32,1024]{2,1,0:T(8,128)S(1)} %merge.1.refs_0_, f32[2,32,1024]{2,1,0:T(8,128)} %collective-permute-done.5.refs_1_, f32[2,32,1024]{2,1,0:T(8,128)} %collective-permute-done.6.refs_2_), custom_call_target="tpu_custom_call" | custom-call | tf_op jit(solution)/shard_map/unfilter/pallas_call | solution.py:695
  76.2 19.2 %all_to_all.10.back = f32[8,4,4096]{2,1,0:T(4,128)S(1)} all-to-all(f32[8,4,4096]{2,1,0:T(4,128)S(1)} %unfilter.1), channel_id=1, replica_groups=mesh['row'=8,'col'=4] {'row'}, dimensions={0} | all-to-all | bytes 1048576 | tf_op jit(solution)/shard_map/all_to_all | solution.py:712
  95.3 0.0 copy-done.4
  95.3 1.2 %unpack.1 = f32[16,4096]{1,0:T(8,128)} custom-call(s32[1,16]{1,0:T(1,128)S(1)} %bitcast.2, f32[8,4,4096]{2,1,0:T(4,128)S(1)} %all_to_all.10.back), custom_call_target="tpu_custom_call" | custom-call | tf_op jit(solution)/shard_map/unpack/pallas_call | solution.py:713
  (2 shorter events, 0.0 us)
Async XLA Ops:
  0.0 10.1 %copy-start = (s32[8,6]{1,0:T(8,128)S(1)}, s32[8,6]{1,0:T(8,128)}, u32[]{:S(2)}) copy-start(s32[8,6]{1,0:T(8,128)} %param.7) | copy-start | bytes 580
  0.0 1.0 copy-start.1
  1.0 0.7 copy-start.3
  2.8 22.1 %all-to-all-start = ((f32[8,4,4224]{2,1,0:T(4,128)}), f32[8,4,4224]{2,1,0:T(4,128)S(1)}, u32[]{:S(2)}, u32[]{:S(2)}) async-start(f32[8,4,4224]{2,1,0:T(4,128)} %pack.1), calls=%async_computation | async-start | bytes 1081344 | tf_op jit(solution)/shard_map/all_to_all | solution.py:647
  12.9 12.1 %copy-start.2 = (f32[32,32]{1,0:T(8,128)S(1)}, f32[32,32]{1,0:T(8,128)}, u32[]{:S(2)}) copy-start(f32[32,32]{1,0:T(8,128)} %filter_ref.3) | copy-start | bytes 12292
  17.8 0.8 copy-start.5
  18.6 0.8 copy-start.7
  19.4 0.8 copy-start.9
  20.2 0.7 copy-start.11
  20.9 0.7 copy-start.13
  26.9 24.1 %collective-permute-start = (f32[2,32,1024]{2,1,0:T(8,128)S(1)}, f32[2,32,1024]{2,1,0:T(8,128)S(1)}, u32[]{:S(2)}, u32[]{:S(2)}) collective-permute-start(f32[2,32,1024]{2,1,0:T(8,128)S(1)} %filter.1.own), channel_id=1, source_target_pairs={{0,28},{1,29},{2,30},{3,31},{4,0},{5,1},{6,2},{7,3},{8,4},{9,5},{1... | collective-permute-start | bytes 786440 | tf_op jit(solution)/shard_map/ppermute | solution.py:623
  29.3 21.7 %collective-permute-start.1 = (f32[2,32,1024]{2,1,0:T(8,128)S(1)}, f32[2,32,1024]{2,1,0:T(8,128)S(1)}, u32[]{:S(2)}, u32[]{:S(2)}) collective-permute-start(f32[2,32,1024]{2,1,0:T(8,128)S(1)} %filter.1.own), channel_id=1, source_target_pairs={{0,30},{1,31},{2,28},{3,29},{4,2},{5,3},{6,0},{7,1},{8,6},{9,7},{1... | collective-permute-start | bytes 786440 | tf_op jit(solution)/shard_map/ppermute | solution.py:623
  30.6 1.0 %copy-start.6 = (bf16[640,384]{1,0:T(8,128)(2,1)S(1)}, bf16[640,384]{1,0:T(8,128)(2,1)}, u32[]{:S(2)}) copy-start(bf16[640,384]{1,0:T(8,128)(2,1)} %copy-done.5) | copy-start | bytes 1474564
  31.6 1.0 %copy-start.8 = (bf16[20,3,32,128]{3,2,1,0:T(8,128)(2,1)S(1)}, bf16[20,3,32,128]{3,2,1,0:T(8,128)(2,1)}, u32[]{:S(2)}) copy-start(bf16[20,3,32,128]{3,2,1,0:T(8,128)(2,1)} %copy-done.7) | copy-start | bytes 1474564
  32.6 1.0 %copy-start.10 = (bf16[20,3,32,128]{3,2,1,0:T(8,128)(2,1)S(1)}, bf16[20,3,32,128]{3,2,1,0:T(8,128)(2,1)}, u32[]{:S(2)}) copy-start(bf16[20,3,32,128]{3,2,1,0:T(8,128)(2,1)} %copy-done.9) | copy-start | bytes 1474564
  33.6 0.9 copy-start.14
  34.6 21.4 %copy-start.12 = (bf16[2,256,160]{2,1,0:T(8,128)(2,1)S(1)}, bf16[2,256,160]{2,1,0:T(8,128)(2,1)}, u32[]{:S(2)}) copy-start(bf16[2,256,160]{2,1,0:T(8,128)(2,1)} %copy-done.11) | copy-start | bytes 491524
  51.0 2.0 %collective-permute-start.4 = (f32[4,32,1024]{2,1,0:T(8,128)S(1)}, f32[4,32,1024]{2,1,0:T(8,128)S(1)}, u32[]{:S(2)}, u32[]{:S(2)}) collective-permute-start(f32[4,32,1024]{2,1,0:T(8,128)S(1)} %get-tuple-element.26), channel_id=1, source_target_pairs={{0,1},{1,0},{2,3},{3,2},{4,5},{5,4},{6,7},{7,6},{8,9},{9,8},{10,11... | collective-permute-start | bytes 1572872 | tf_op jit(solution)/shard_map/ppermute | solution.py:623
  51.1 5.0 %collective-permute-start.2 = (f32[2,32,1024]{2,1,0:T(8,128)S(1)}, f32[2,32,1024]{2,1,0:T(8,128)S(1)}, u32[]{:S(2)}, u32[]{:S(2)}) collective-permute-start(f32[2,32,1024]{2,1,0:T(8,128)S(1)} %collective-permute-done.refs_0_), channel_id=1, source_target_pairs={{0,1},{1,0},{2,3},{3,2},{4,5},{5,4},{6,7},{7,6},{8,9},{9,8},{10,11... | collective-permute-start | bytes 786440 | tf_op jit(solution)/shard_map/ppermute | solution.py:623
  51.6 4.5 %collective-permute-start.3 = (f32[2,32,1024]{2,1,0:T(8,128)S(1)}, f32[2,32,1024]{2,1,0:T(8,128)S(1)}, u32[]{:S(2)}, u32[]{:S(2)}) collective-permute-start(f32[2,32,1024]{2,1,0:T(8,128)S(1)} %collective-permute-done.1.refs_1_), channel_id=1, source_target_pairs={{0,1},{1,0},{2,3},{3,2},{4,5},{5,4},{6,7},{7,6},{8,9},{9,8},{10,11... | collective-permute-start | bytes 786440 | tf_op jit(solution)/shard_map/ppermute | solution.py:623
  53.8 19.4 %collective-permute-start.5 = (f32[2,32,1024]{2,1,0:T(8,128)}, f32[2,32,1024]{2,1,0:T(8,128)}, u32[]{:S(2)}, u32[]{:S(2)}) collective-permute-start(f32[2,32,1024]{2,1,0:T(8,128)} %get-tuple-element.28), channel_id=1, source_target_pairs={{0,4},{1,5},{2,6},{3,7},{4,8},{5,9},{6,10},{7,11},{8,12},{9,13},{1... | collective-permute-start | bytes 786440 | tf_op jit(solution)/shard_map/ppermute | solution.py:623
  55.6 17.7 %collective-permute-start.6 = (f32[2,32,1024]{2,1,0:T(8,128)}, f32[2,32,1024]{2,1,0:T(8,128)}, u32[]{:S(2)}, u32[]{:S(2)}) collective-permute-start(f32[2,32,1024]{2,1,0:T(8,128)} %get-tuple-element.27), channel_id=1, source_target_pairs={{0,6},{1,7},{2,4},{3,5},{4,10},{5,11},{6,8},{7,9},{8,14},{9,15},{1... | collective-permute-start | bytes 786440 | tf_op jit(solution)/shard_map/ppermute | solution.py:623
  56.0 39.3 %copy-start.4 = (s32[16]{0:T(128)S(1)}, s32[16]{0:T(128)}, u32[]{:S(2)}) copy-start(s32[16]{0:T(128)} %param.6) | copy-start | bytes 196

commit v5 on v4

--- a/solution.py
+++ b/solution.py
@@ -78,6 +78,19 @@
                 spread[g, s, inner * breadth : (inner + 1) * breadth] = line.astype(BF16)
 
 
+class Loader:
+    def __init__(self, sources, targets, sems):
+        self.copies = [pltpu.make_async_copy(a, b, sems.at[i]) for i, (a, b) in enumerate(zip(sources, targets))]
+
+    def start(self):
+        for copy in self.copies:
+            copy.start()
+
+    def wait(self, chosen):
+        for i in chosen:
+            self.copies[i].wait()
+
+
 def fill(xbuf, slot, block):
     breadth = block.shape[0]
     high, low = split(block)
@@ -93,7 +106,7 @@
         ubuf[g, n, h, :rows] = result[:, h * LANES : (h + 1) * LANES]
 
 
-def second_stage(ubuf, lbuf, tbuf, second_high, second_low, per, breadth, offsets, recipes, emit):
+def second_stage(ubuf, lbuf, tbuf, second_high, second_low, group, per, breadth, offsets, recipes, emit):
     volumes, count, hi_count, stride = ubuf.shape[:4]
     lo_count = LANES // breadth
     flat = ubuf.reshape(volumes * count * hi_count * stride, LANES)
@@ -103,7 +116,7 @@
     def pair_body(pair, carry):
         for spot, k in enumerate(offsets):
             for half in range(2):
-                term = pair * 2 + half
+                term = group * per + pair * 2 + half
                 high = jnp.concatenate([second_high[term, k]] * lo_count, axis=0)
                 low = jnp.concatenate([second_low[term, k]] * lo_count, axis=0)
                 high = jnp.where(block_mask, high, zero_block)
@@ -173,10 +186,14 @@
 
 def merge_kernel(where, own, *refs, parts):
     sources = refs[:parts]
-    first, second_high, second_low, third, out = refs[parts : parts + 5]
-    vols, xbuf, ubuf, lbuf, tbuf, rbuf, obuf, sems = refs[parts + 5 :]
+    remote = refs[parts : parts + 4]
+    out = refs[parts + 4]
+    first, second_high, second_low, third, weight_sems = refs[parts + 5 : parts + 10]
+    vols, xbuf, ubuf, lbuf, tbuf, rbuf, obuf, sems = refs[parts + 10 :]
+    loader = Loader(remote, (first, second_high, second_low, third), weight_sems)
     count, breadth, width = own.shape
-    per = first.shape[0] // breadth
+    rows = first.shape[0] // third.shape[0]
+    per = rows // breadth
     kgroup = per * breadth * breadth // LANES
 
     def copies(action):
@@ -199,6 +216,7 @@
     @pl.when(group == 0)
     def _():
         copies(lambda c: c.start())
+        loader.start()
         for n in range(count):
             for axis in range(3):
 
@@ -210,14 +228,20 @@
         xbuf[...] = jnp.zeros(xbuf.shape, BF16)
         obuf[...] = jnp.zeros(obuf.shape, F32)
         copies(lambda c: c.wait())
-
+        loader.wait((0,))
+
+    top = pl.multiple_of(group * rows, 8)
     for n in range(count):
         fill(xbuf, 0, vols[n * 3])
         fill(xbuf, 1, own[n])
-        place(ubuf, 0, n, product(first[:, : 2 * LANES], xbuf[...]))
+        place(ubuf, 0, n, product(first[pl.ds(top, rows), : 2 * LANES], xbuf[...]))
         for g, axis in ((1, 2), (2, 1)):
             fill(xbuf, 0, vols[n * 3 + axis])
-            place(ubuf, g, n, product(first[:, LANES : 2 * LANES], xbuf[:LANES]))
+            place(ubuf, g, n, product(first[pl.ds(top, rows), LANES : 2 * LANES], xbuf[:LANES]))
+
+    @pl.when(group == 0)
+    def _():
+        loader.wait((1, 2, 3))
 
     def emit(q, pair, tile, lane, high, low):
         step = high.shape[0]
@@ -225,11 +249,13 @@
         rbuf[tile, pl.ds(row, step), lane : lane + LANES] = high
         rbuf[tile, pl.ds(row + 2 * kgroup, step), lane : lane + LANES] = low
 
-    second_stage(ubuf, lbuf, tbuf, second_high, second_low, per, breadth, (1, 0), (((0, 0), (1, 1)), ((2, 0),)), emit)
+    second_stage(
+        ubuf, lbuf, tbuf, second_high, second_low, group, per, breadth, (1, 0), (((0, 0), (1, 1)), ((2, 0),)), emit
+    )
 
     def tile_body(tile, carry):
-        wide = product(third[0], rbuf[tile, : 2 * kgroup])
-        wide = wide[:LANES] + wide[LANES:] + product(third[0, :LANES], rbuf[tile, 2 * kgroup :])
+        wide = product(third[group], rbuf[tile, : 2 * kgroup])
+        wide = wide[:LANES] + wide[LANES:] + product(third[group, :LANES], rbuf[tile, 2 * kgroup :])
         total = pick_diagonal(wide, breadth)
         for d in range(2):
             row = pl.multiple_of((tile * 2 + d) * breadth, breadth)
@@ -248,26 +274,37 @@
             turn_block(obuf, n * breadth * breadth, breadth, store)
 
 
-def spread_kernel(where, own, first, second_high, second_low, third, keep, send, *refs):
-    xbuf, ubuf, lbuf, tbuf, rbuf, obuf, block = refs
+def spread_kernel(where, own, *refs):
+    remote = refs[:4]
+    keep, send, first, second_high, second_low, third, weight_sems = refs[4:11]
+    xbuf, ubuf, lbuf, tbuf, rbuf, obuf, block = refs[11:]
+    loader = Loader(remote, (first, second_high, second_low, third), weight_sems)
     count, breadth, width = own.shape
-    per = first.shape[0] // breadth
+    rows = first.shape[0] // third.shape[0]
+    per = rows // breadth
     kgroup = per * breadth * breadth // LANES
     half_slots = keep.shape[0]
     group = pl.program_id(0)
 
     @pl.when(group == 0)
     def _():
+        loader.start()
         keep[...] = jnp.zeros(keep.shape, F32)
         send[...] = jnp.zeros(send.shape, F32)
         tbuf[...] = jnp.zeros(tbuf.shape, BF16)
         xbuf[...] = jnp.zeros(xbuf.shape, BF16)
         obuf[...] = jnp.zeros(obuf.shape, F32)
-
+        loader.wait((0,))
+
+    top = pl.multiple_of(group * rows, 8)
     for n in range(count):
         fill(xbuf, 0, own[n])
         for g in range(2):
-            place(ubuf, g, n, product(first[:, (1 + g) * LANES : (2 + g) * LANES], xbuf[...]))
+            place(ubuf, g, n, product(first[pl.ds(top, rows), (1 + g) * LANES : (2 + g) * LANES], xbuf[...]))
+
+    @pl.when(group == 0)
+    def _():
+        loader.wait((1, 2, 3))
 
     def emit(q, pair, tile, lane, high, low):
         step = high.shape[0]
@@ -277,11 +314,11 @@
         rbuf[tile, pl.ds(row + 2 * kgroup, step), lane : lane + LANES] = high
 
     recipes = (((1, 0),), ((0, 0),), ((0, 1),))
-    second_stage(ubuf, lbuf, tbuf, second_high, second_low, per, breadth, (1, 2), recipes, emit)
+    second_stage(ubuf, lbuf, tbuf, second_high, second_low, group, per, breadth, (1, 2), recipes, emit)
 
     def tile_body(tile, carry):
         for q in range(3):
-            wide = product(third[0, 1 if q == 1 else 0], rbuf[tile, q * 3 * kgroup : (q + 1) * 3 * kgroup])
+            wide = product(third[group, 1 if q == 1 else 0], rbuf[tile, q * 3 * kgroup : (q + 1) * 3 * kgroup])
             total = pick_diagonal(wide, breadth)
             for d in range(2):
                 row = pl.multiple_of((tile * 2 + d) * breadth, breadth)
@@ -314,11 +351,6 @@
 
 def whole_spec(array):
     return pl.BlockSpec(array.shape, lambda i, w, rank=len(array.shape): (0,) * rank)
-
-
-def group_spec(array, size):
-    rank = len(array.shape)
-    return pl.BlockSpec((size,) + array.shape[1:], lambda i, w: (i,) + (0,) * (rank - 1))
 
 
 def stage_scratch(volumes, recipes, thick, count, breadth, width, per):
@@ -348,19 +380,16 @@
             grid=(groups,),
             in_specs=[whole_spec(own)]
             + extra_specs
-            + [
-                group_spec(first, per * breadth),
-                group_spec(second_high, per),
-                group_spec(second_low, per),
-                group_spec(third, 1),
-            ],
+            + [pl.BlockSpec(memory_space=pltpu.HBM)] * 4,
             out_specs=[whole_spec(shape) for shape in out_shapes],
-            scratch_shapes=scratch,
+            scratch_shapes=[pltpu.VMEM(array.shape, BF16) for array in (first, second_high, second_low, third)]
+            + [pltpu.SemaphoreType.DMA((4,))]
+            + scratch,
         ),
         compiler_params=pltpu.CompilerParams(dimension_semantics=("arbitrary",), vmem_limit_bytes=30 << 20),
         cost_estimate=cost(own.shape[0], breadth, terms, units),
         name=name,
-    )(where, own, *extra, first, second_high, second_low, third)
+    )(where, own, *extra, *[pltpu.with_memory_space_constraint(w, pltpu.HBM) for w in (first, second_high, second_low, third)])
 
 
 def merge_call(where, own, parts, weights, third, groups):
@@ -599,7 +628,7 @@
         out[r] = packed[r * capacity : (r + 1) * capacity]
 
 
-def vmem_call(kernel, out_shape, scratch, name, in_specs=None, **settings):
+def vmem_call(kernel, out_shape, scratch, name, in_specs=None, room=14, **settings):
     extra = {} if in_specs is None else dict(grid=(1,), in_specs=in_specs)
     if in_specs is not None:
         rank = len(out_shape)
@@ -608,7 +637,7 @@
         functools.partial(kernel, **settings),
         out_shape=jax.ShapeDtypeStruct(out_shape, F32),
         scratch_shapes=[pltpu.VMEM(shape, dtype) for shape, dtype in scratch],
-        compiler_params=pltpu.CompilerParams(vmem_limit_bytes=30 << 20),
+        compiler_params=pltpu.CompilerParams(vmem_limit_bytes=room << 20),
         name=name,
         **extra,
     )
@@ -642,7 +671,7 @@
     slot_row = fine_slot.reshape(1, held)
     routing = dict(run_size=8 * par_row)
     sent = vmem_call(
-        pack_kernel, (runs, capacity, volume + LANES), [((3 * held, volume), BF16)], "pack", runs=runs, **routing
+        pack_kernel, (runs, capacity, volume + LANES), [((3 * held, volume), BF16)], "pack", room=60, runs=runs, **routing
     )(slot_row, fine_coeffs)
     got = lax.all_to_all(sent, "row", split_axis=0, concat_axis=0, tiled=True)
 
@@ -655,7 +684,7 @@
             jax.ShapeDtypeStruct((groups, 2 * LANES, 2 * per * hi_count), BF16),
             jax.ShapeDtypeStruct((groups, 2, LANES, 3 * per * hi_count), BF16),
         ],
-        compiler_params=pltpu.CompilerParams(vmem_limit_bytes=30 << 20),
+        compiler_params=pltpu.CompilerParams(vmem_limit_bytes=14 << 20),
         name="prepare",
     )(kernel_ops.reshape(terms * 9 * breadth, breadth))
     weights = (first, second_high, second_low)

time: 97 us -> 93.7 us (0.966)
  local copies, waits for them, and re-layouts: 14.8 us -> 9.13 us
  Pallas kernels: 43.1 us -> 45.4 us
    unnamed x31 -> x17, local copies, waits for them, and re-layouts: 12.1 us -> 6.43 us
    pallas_call x2, Pallas kernels: 33.5 us -> 34.9 us  [stage_call(): pl.pallas_call(kernel, out_shape=out_shapes, grid_spec=pltpu.PrefetchScal...]
    pallas_call x1, Pallas kernels: 1.18 us -> 2.16 us  [local(): vmem_call(pack_kernel, (runs, capacity, volume + LANES), [((3 * held, vol...]
  transfers between devices with their start and end apart: 8 -> 8, of which waited for: 2 -> 2; matrix products, arithmetic and copies ran while one was open for 6% -> 7% of each run, Pallas kernels for 37% -> 40%
where the time goes in v5:
time: 93.7 us; the launch traced here: 93.3 us
  Pallas kernels  45.4 us (48%)
  blocking collectives  19.3 us (21%)
  starting transfers between devices  13.8 us (15%)
  local copies, waits for them, and re-layouts  9.13 us (10%)
  waiting for transfers between devices  4.61 us (5%)
    pallas_call x2, Pallas kernels, stage_call(): pl.pallas_call(kernel, out_shape=out_shapes, grid_spec=pltpu.PrefetchScal...  34.9 us
    all_to_all x1, blocking collectives, local(): lax.all_to_all(results, 'row', split_axis=0, concat_axis=0, tiled=True)  19.3 us
    all_to_all x1, starting transfers between devices, local(): got = lax.all_to_all(sent, 'row', split_axis=0, concat_axis=0, tiled=True)  7.28 us
    ppermute x7, starting transfers between devices, moved(): return lax.ppermute(array, ('row', 'col'), pairs)  6.55 us
    unnamed x17, local copies, waits for them, and re-layouts  6.43 us
    all_to_all x1, waiting for transfers between devices, local(): got = lax.all_to_all(sent, 'row', split_axis=0, concat_axis=0, tiled=True)  3.28 us
    pallas_call x1, Pallas kernels, local(): vmem_call(unfilter_kernel, (runs, capacity, volume), [((3 * count * bread...  2.91 us
    reshape x1, local copies, waits for them, and re-layouts, local(): kernel_ops.reshape(terms * 9 * breadth, breadth)  2.6 us
  transfers between devices with their start and end apart: 8, of which 2 were waited for; matrix products, arithmetic and copies ran while one was open for 7% of the time, Pallas kernels for 40%

profile of v5, /device:TPU:0, one launch (start us, length us, event | category | flops | bytes accessed | tf_op | source)
XLA Modules:
  0.0 93.3 jit_solution(1244212172205676196)
XLA Ops:
  0.0 0.0 copy-start
  0.0 2.2 %pack.1 = f32[8,4,4224]{2,1,0:T(4,128)} custom-call(s32[1,16]{1,0:T(1,128)} %bitcast.1, f32[16,4096]{1,0:T(8,128)} %fine.1), custom_call_target="tpu_custom_call" | custom-call | tf_op jit(solution)/shard_map/pack/pallas_call | solution.py:673
  2.2 7.3 %all-to-all-start = ((f32[8,4,4224]{2,1,0:T(4,128)}), f32[8,4,4224]{2,1,0:T(4,128)S(1)}, u32[]{:S(2)}, u32[]{:S(2)}) async-start(f32[8,4,4224]{2,1,0:T(4,128)} %pack.1), calls=%async_computation | async-start | bytes 1081344 | tf_op jit(solution)/shard_map/all_to_all | solution.py:676
  9.4 0.0 copy-done
  9.5 0.1 slice.15
  9.6 2.6 %copy.7 = f32[20,3,3,1024]{3,2,1,0:T(4,128)} copy(f32[20,3,3,1024]{3,0,2,1:T(8,128)} %param.9) | data formatting | bytes 1474560 | tf_op args[4]
  12.2 0.0 copy-start.1
  12.2 2.6 %reshape.7.ops = f32[5760,32]{1,0:T(8,128)S(1)} reshape(f32[20,3,3,1024]{3,2,1,0:T(4,128)} %copy.7) | data formatting | bytes 1474560 | tf_op jit(solution)/shard_map/reshape | solution.py:689
  14.8 2.4 %prepare.1 = (bf16[640,384]{1,0:T(8,128)(2,1)S(1)}, bf16[20,3,32,128]{3,2,1,0:T(8,128)(2,1)S(1)}, bf16[20,3,32,128]{3,2,1,0:T(8,128)(2,1)S(1)}, bf16[2,256,160]{...) custom-call(f32[5760,32]{1,0:T(8,128)S(1)} %reshape.7.ops), custom_call_target="tpu_custom_call" | custom-call | tf_op jit(solution)/shard_map/prepare/pallas_call | solution.py:678
  17.2 0.0 copy-start.3
  17.2 0.8 copy-done.3
  18.0 0.0 copy-start.4
  18.0 0.8 copy-done.4
  18.7 0.0 copy-start.5
  18.7 0.8 copy-done.5
  19.6 0.0 copy-start.6
  19.6 0.7 copy-done.6
  20.3 0.0 copy-start.7
  20.3 0.7 copy-done.7
  21.0 3.3 %all-to-all-done.got = f32[8,4,4224]{2,1,0:T(4,128)S(1)} async-done(((f32[8,4,4224]{2,1,0:T(4,128)}), f32[8,4,4224]{2,1,0:T(4,128)S(1)}, u32[]{:S(2)}, u32[]{:S(2)}) %all-to-all-start) | async-done | bytes 540704 | tf_op jit(solution)/shard_map/all_to_all | solution.py:676
  24.3 0.0 copy-done.1
  24.3 2.0 %filter.1.own = f32[2,32,1024]{2,1,0:T(8,128)S(1)} custom-call(f32[8,4,4224]{2,1,0:T(4,128)S(1)} %all-to-all-done.got, f32[32,32]{1,0:T(8,128)S(1)} %copy-done.1), custom_call_target="tpu_custom_call" | custom-call | tf_op jit(solution)/shard_map/filter/pallas_call | solution.py:699
  26.2 2.4 %collective-permute-start = (f32[2,32,1024]{2,1,0:T(8,128)S(1)}, f32[2,32,1024]{2,1,0:T(8,128)S(1)}, u32[]{:S(2)}, u32[]{:S(2)}) collective-permute-start(f32[2,32,1024]{2,1,0:T(8,128)S(1)} %filter.1.own), channel_id=1, source_target_pairs={{0,28},{1,29},{2,30},{3,31},{4,0},{5,1},{6,2},{7,3},{8,4},{9,5},{1... | collective-permute-start | bytes 786440 | tf_op jit(solution)/shard_map/ppermute | solution.py:652
  28.7 1.2 %collective-permute-start.1 = (f32[2,32,1024]{2,1,0:T(8,128)S(1)}, f32[2,32,1024]{2,1,0:T(8,128)S(1)}, u32[]{:S(2)}, u32[]{:S(2)}) collective-permute-start(f32[2,32,1024]{2,1,0:T(8,128)S(1)} %filter.1.own), channel_id=1, source_target_pairs={{0,30},{1,31},{2,28},{3,29},{4,2},{5,3},{6,0},{7,1},{8,6},{9,7},{1... | collective-permute-start | bytes 786440 | tf_op jit(solution)/shard_map/ppermute | solution.py:652
  29.9 17.2 %spread.1 = (f32[4,32,1024]{2,1,0:T(8,128)S(1)}, f32[4,32,1024]{2,1,0:T(8,128)S(1)}) custom-call(s32[2,3]{1,0:T(2,128)S(1)} %compare_select_fusion.2.where, f32[2,32,1024]{2,1,0:T(8,128)S(1)} %filter.1.own, bf16[640,384]{1,0:T(8,128)(2,1)} %copy-done.3, bf16[20,3,32,128]{3,2,1,0:T(8,128)(2,1)} %copy-done.4, bf16[20,3,32,128]{3,2,1,0:T(8,128)(2,1)} %copy-done.5, ...), custom_call_target="tpu_custom_call" | custom-call | flops 134217728000 | bytes 4194304 | tf_op jit(solution)/shard_map/spread/pallas_call | solution.py:375
  47.1 0.0 collective-permute-done.refs_0_
  47.1 0.0 collective-permute-done.1.refs_1_
  47.1 0.1 collective-permute-start.4
  47.2 0.5 collective-permute-start.2
  47.7 0.1 collective-permute-start.3
  47.8 1.3 %collective-permute-done.4 = f32[4,32,1024]{2,1,0:T(8,128)S(1)} collective-permute-done((f32[4,32,1024]{2,1,0:T(8,128)S(1)}, f32[4,32,1024]{2,1,0:T(8,128)S(1)}, u32[]{:S(2)}, u32[]{:S(2)}) %collective-permute-start.4) | collective-permute-done | bytes 524320 | tf_op jit(solution)/shard_map/ppermute | solution.py:652
  49.1 0.9 slice_add_fusion
  50.0 1.8 %collective-permute-start.5 = (f32[2,32,1024]{2,1,0:T(8,128)}, f32[2,32,1024]{2,1,0:T(8,128)}, u32[]{:S(2)}, u32[]{:S(2)}) collective-permute-start(f32[2,32,1024]{2,1,0:T(8,128)} %get-tuple-element.28), channel_id=1, source_target_pairs={{0,4},{1,5},{2,6},{3,7},{4,8},{5,9},{6,10},{7,11},{8,12},{9,13},{1... | collective-permute-start | bytes 786440 | tf_op jit(solution)/shard_map/ppermute | solution.py:652
  51.7 0.5 collective-permute-start.6
  52.2 0.0 collective-permute-done.2.refs_2_
  52.2 0.0 collective-permute-done.3.refs_3_
  52.2 0.0 copy-start.2
  52.2 17.7 %merge.1.refs_0_ = f32[2,32,1024]{2,1,0:T(8,128)S(1)} custom-call(s32[2,3]{1,0:T(2,128)S(1)} %compare_select_fusion.2.where, f32[2,32,1024]{2,1,0:T(8,128)S(1)} %filter.1.own, f32[2,32,1024]{2,1,0:T(8,128)S(1)} %collective-permute-done.refs_0_, f32[2,32,1024]{2,1,0:T(8,128)S(1)} %collective-permute-done.1.refs_1_, ...), custom_call_target="tpu_custom_call" | custom-call | flops 150994944000 | bytes 4194304 | tf_op jit(solution)/shard_map/merge/pallas_call | solution.py:375
  69.9 0.0 collective-permute-done.5.refs_1_
  69.9 0.0 collective-permute-done.6.refs_2_
  69.9 2.9 %unfilter.1 = f32[8,4,4096]{2,1,0:T(4,128)S(1)} custom-call(f32[8,4,4224]{2,1,0:T(4,128)S(1)} %all-to-all-done.got, f32[32,32]{1,0:T(8,128)S(1)} %copy-done.1, f32[2,32,1024]{2,1,0:T(8,128)S(1)} %merge.1.refs_0_, f32[2,32,1024]{2,1,0:T(8,128)} %collective-permute-done.5.refs_1_, f32[2,32,1024]{2,1,0:T(8,128)} %collective-permute-done.6.refs_2_), custom_call_target="tpu_custom_call" | custom-call | tf_op jit(solution)/shard_map/unfilter/pallas_call | solution.py:724
  72.9 19.3 %all_to_all.10.back = f32[8,4,4096]{2,1,0:T(4,128)S(1)} all-to-all(f32[8,4,4096]{2,1,0:T(4,128)S(1)} %unfilter.1), channel_id=1, replica_groups=mesh['row'=8,'col'=4] {'row'}, dimensions={0} | all-to-all | bytes 1048576 | tf_op jit(solution)/shard_map/all_to_all | solution.py:741
  92.1 0.0 copy-done.2
  92.1 1.2 %unpack.1 = f32[16,4096]{1,0:T(8,128)} custom-call(s32[1,16]{1,0:T(1,128)S(1)} %bitcast.2, f32[8,4,4096]{2,1,0:T(4,128)S(1)} %all_to_all.10.back), custom_call_target="tpu_custom_call" | custom-call | tf_op jit(solution)/shard_map/unpack/pallas_call | solution.py:742
  (2 shorter events, 0.0 us)
Async XLA Ops:
  0.0 9.4 %copy-start = (s32[8,6]{1,0:T(8,128)S(1)}, s32[8,6]{1,0:T(8,128)}, u32[]{:S(2)}) copy-start(s32[8,6]{1,0:T(8,128)} %param.7) | copy-start | bytes 580
  2.2 22.1 %all-to-all-start = ((f32[8,4,4224]{2,1,0:T(4,128)}), f32[8,4,4224]{2,1,0:T(4,128)S(1)}, u32[]{:S(2)}, u32[]{:S(2)}) async-start(f32[8,4,4224]{2,1,0:T(4,128)} %pack.1), calls=%async_computation | async-start | bytes 1081344 | tf_op jit(solution)/shard_map/all_to_all | solution.py:676
  12.2 12.1 %copy-start.1 = (f32[32,32]{1,0:T(8,128)S(1)}, f32[32,32]{1,0:T(8,128)}, u32[]{:S(2)}) copy-start(f32[32,32]{1,0:T(8,128)} %filter_ref.3) | copy-start | bytes 12292
  17.2 0.8 copy-start.3
  18.0 0.8 copy-start.4
  18.7 0.8 copy-start.5
  19.6 0.7 copy-start.6
  20.3 0.7 copy-start.7
  26.2 20.9 %collective-permute-start = (f32[2,32,1024]{2,1,0:T(8,128)S(1)}, f32[2,32,1024]{2,1,0:T(8,128)S(1)}, u32[]{:S(2)}, u32[]{:S(2)}) collective-permute-start(f32[2,32,1024]{2,1,0:T(8,128)S(1)} %filter.1.own), channel_id=1, source_target_pairs={{0,28},{1,29},{2,30},{3,31},{4,0},{5,1},{6,2},{7,3},{8,4},{9,5},{1... | collective-permute-start | bytes 786440 | tf_op jit(solution)/shard_map/ppermute | solution.py:652
  28.7 18.5 %collective-permute-start.1 = (f32[2,32,1024]{2,1,0:T(8,128)S(1)}, f32[2,32,1024]{2,1,0:T(8,128)S(1)}, u32[]{:S(2)}, u32[]{:S(2)}) collective-permute-start(f32[2,32,1024]{2,1,0:T(8,128)S(1)} %filter.1.own), channel_id=1, source_target_pairs={{0,30},{1,31},{2,28},{3,29},{4,2},{5,3},{6,0},{7,1},{8,6},{9,7},{1... | collective-permute-start | bytes 786440 | tf_op jit(solution)/shard_map/ppermute | solution.py:652
  47.1 2.0 %collective-permute-start.4 = (f32[4,32,1024]{2,1,0:T(8,128)S(1)}, f32[4,32,1024]{2,1,0:T(8,128)S(1)}, u32[]{:S(2)}, u32[]{:S(2)}) collective-permute-start(f32[4,32,1024]{2,1,0:T(8,128)S(1)} %get-tuple-element.26), channel_id=1, source_target_pairs={{0,1},{1,0},{2,3},{3,2},{4,5},{5,4},{6,7},{7,6},{8,9},{9,8},{10,11... | collective-permute-start | bytes 1572872 | tf_op jit(solution)/shard_map/ppermute | solution.py:652
  47.2 5.0 %collective-permute-start.2 = (f32[2,32,1024]{2,1,0:T(8,128)S(1)}, f32[2,32,1024]{2,1,0:T(8,128)S(1)}, u32[]{:S(2)}, u32[]{:S(2)}) collective-permute-start(f32[2,32,1024]{2,1,0:T(8,128)S(1)} %collective-permute-done.refs_0_), channel_id=1, source_target_pairs={{0,1},{1,0},{2,3},{3,2},{4,5},{5,4},{6,7},{7,6},{8,9},{9,8},{10,11... | collective-permute-start | bytes 786440 | tf_op jit(solution)/shard_map/ppermute | solution.py:652
  47.7 4.5 %collective-permute-start.3 = (f32[2,32,1024]{2,1,0:T(8,128)S(1)}, f32[2,32,1024]{2,1,0:T(8,128)S(1)}, u32[]{:S(2)}, u32[]{:S(2)}) collective-permute-start(f32[2,32,1024]{2,1,0:T(8,128)S(1)} %collective-permute-done.1.refs_1_), channel_id=1, source_target_pairs={{0,1},{1,0},{2,3},{3,2},{4,5},{5,4},{6,7},{7,6},{8,9},{9,8},{10,11... | collective-permute-start | bytes 786440 | tf_op jit(solution)/shard_map/ppermute | solution.py:652
  50.0 19.9 %collective-permute-start.5 = (f32[2,32,1024]{2,1,0:T(8,128)}, f32[2,32,1024]{2,1,0:T(8,128)}, u32[]{:S(2)}, u32[]{:S(2)}) collective-permute-start(f32[2,32,1024]{2,1,0:T(8,128)} %get-tuple-element.28), channel_id=1, source_target_pairs={{0,4},{1,5},{2,6},{3,7},{4,8},{5,9},{6,10},{7,11},{8,12},{9,13},{1... | collective-permute-start | bytes 786440 | tf_op jit(solution)/shard_map/ppermute | solution.py:652
  51.7 18.2 %collective-permute-start.6 = (f32[2,32,1024]{2,1,0:T(8,128)}, f32[2,32,1024]{2,1,0:T(8,128)}, u32[]{:S(2)}, u32[]{:S(2)}) collective-permute-start(f32[2,32,1024]{2,1,0:T(8,128)} %get-tuple-element.27), channel_id=1, source_target_pairs={{0,6},{1,7},{2,4},{3,5},{4,10},{5,11},{6,8},{7,9},{8,14},{9,15},{1... | collective-permute-start | bytes 786440 | tf_op jit(solution)/shard_map/ppermute | solution.py:652
  52.2 39.9 %copy-start.2 = (s32[16]{0:T(128)S(1)}, s32[16]{0:T(128)}, u32[]{:S(2)}) copy-start(s32[16]{0:T(128)} %param.6) | copy-start | bytes 196

commit v6 on v5

--- a/solution.py
+++ b/solution.py
@@ -11,6 +11,7 @@
 F32, BF16 = jnp.float32, jnp.bfloat16
 LANES = 128
 PAD = 8
+UNROLL = True
 
 
 def iota(shape, axis):
@@ -69,9 +70,10 @@
                 )
                 for k in range(3)
             ]
-            high, low = split(jnp.concatenate([strip[1], strip[0]], axis=1))
-            merge[g, inner * breadth : (inner + 1) * breadth] = high
-            merge[g, LANES + inner * breadth : LANES + (inner + 1) * breadth] = low
+            value = jnp.concatenate([strip[1], strip[0]], axis=1)
+            high = value.astype(BF16).astype(F32)
+            line = jnp.concatenate([high, high, value - high], axis=1)
+            merge[g, inner * breadth : (inner + 1) * breadth] = line.astype(BF16)
             for s, k in enumerate((1, 2)):
                 high = strip[k].astype(BF16).astype(F32)
                 line = jnp.concatenate([high, high, strip[k] - high], axis=1)
@@ -106,55 +108,60 @@
         ubuf[g, n, h, :rows] = result[:, h * LANES : (h + 1) * LANES]
 
 
-def second_stage(ubuf, lbuf, tbuf, second_high, second_low, group, per, breadth, offsets, recipes, emit):
+def second_stage(ubuf, lbuf, tbuf, second_high, second_low, group, per, breadth, offsets, sides, recipes, emit):
     volumes, count, hi_count, stride = ubuf.shape[:4]
     lo_count = LANES // breadth
+    wide = 2 * LANES
     flat = ubuf.reshape(volumes * count * hi_count * stride, LANES)
     block_mask = iota((LANES, LANES), 0) // breadth == iota((LANES, LANES), 1) // breadth
     zero_block = jnp.zeros((LANES, LANES), BF16)
 
     def pair_body(pair, carry):
         for spot, k in enumerate(offsets):
+            row = spot * sides[0] * wide
+            lane = spot * sides[1] * wide
             for half in range(2):
                 term = group * per + pair * 2 + half
                 high = jnp.concatenate([second_high[term, k]] * lo_count, axis=0)
                 low = jnp.concatenate([second_low[term, k]] * lo_count, axis=0)
                 high = jnp.where(block_mask, high, zero_block)
                 low = jnp.where(block_mask, low, zero_block)
-                tbuf[half, spot, :LANES, :LANES] = high
-                tbuf[half, spot, LANES:, :LANES] = high
-                tbuf[half, spot, :LANES, LANES:] = low
-        for n in range(count):
-            for half in range(2):
-                term = pair * 2 + half
+                tbuf[half, row : row + LANES, lane : lane + LANES] = high
+                tbuf[half, row + LANES : row + wide, lane : lane + LANES] = high
+                tbuf[half, row : row + LANES, lane + LANES : lane + wide] = low
+        for half in range(2):
+            term = pair * 2 + half
+            for n in range(count):
                 for g in range(volumes):
                     base = (g * count + n) * hi_count * stride + term * breadth
                     for a in range(0, breadth, 2):
                         pieces = [flat[pl.ds(base + a + d, hi_count, stride=stride), :] for d in range(2)]
                         high, low = split(jnp.concatenate(pieces, axis=0))
-                        at = a * hi_count
-                        lbuf[half, g, at : at + 2 * hi_count, :LANES] = high
-                        lbuf[half, g, at : at + 2 * hi_count, LANES:] = low
-            results = []
-            for half in range(2):
-                line = []
-                for recipe in recipes:
-                    wide = None
-                    for g, spot in recipe:
-                        piece = product(lbuf[half, g], tbuf[half, spot])
-                        wide = piece if wide is None else wide + piece
-                    line.append(wide[:, :LANES] + wide[:, LANES:])
-                results.append(line)
-            for q in range(len(recipes)):
-                for a in range(breadth):
-                    both = jnp.concatenate(
-                        [results[half][q][a * hi_count : (a + 1) * hi_count] for half in range(2)], axis=0
-                    )
-                    high, low = split(both)
-                    emit(q, pair, (n * breadth + a) // 2, (a % 2) * LANES, high, low)
+                        at = (n * breadth + a) * hi_count
+                        lane = g * wide
+                        lbuf[half, at : at + 2 * hi_count, lane : lane + LANES] = high
+                        lbuf[half, at : at + 2 * hi_count, lane + LANES : lane + wide] = low
+        results = []
+        for half in range(2):
+            line = []
+            for (start, size), (row, rows), (lane, lanes) in recipes:
+                full = product(
+                    lbuf[half, :, start * wide : (start + size) * wide],
+                    tbuf[half, row * wide : (row + rows) * wide, lane * wide : (lane + lanes) * wide],
+                )
+                for out in range(lanes):
+                    line.append(full[:, out * wide : out * wide + LANES] + full[:, out * wide + LANES : (out + 1) * wide])
+            results.append(line)
+        for q in range(len(results[0])):
+            for at in range(count * breadth):
+                both = jnp.concatenate(
+                    [results[half][q][at * hi_count : (at + 1) * hi_count] for half in range(2)], axis=0
+                )
+                high, low = split(both)
+                emit(q, pair, at // 2, (at % 2) * LANES, high, low)
         return carry
 
-    lax.fori_loop(0, per // 2, pair_body, 0)
+    lax.fori_loop(0, per // 2, pair_body, 0, unroll=UNROLL)
 
 
 def pick_diagonal(wide, breadth):
@@ -166,12 +173,13 @@
 
 
 def turn_block(obuf, base, breadth, store):
+    stride = breadth + PAD
     lo_count = LANES // breadth
     lane_of = iota((8, LANES), 1) // breadth
     for a in range(0, breadth, 8):
         for high in range(breadth // lo_count):
             level = [
-                obuf[pl.ds(base + a * breadth + high * lo_count + low, 8, stride=breadth), :] for low in range(lo_count)
+                obuf[pl.ds(base + a * stride + high * lo_count + low, 8, stride=stride), :] for low in range(lo_count)
             ]
             step = 1
             while step < lo_count:
@@ -211,67 +219,61 @@
 
                     start += size
 
-    group = pl.program_id(0)
-
-    @pl.when(group == 0)
-    def _():
-        copies(lambda c: c.start())
-        loader.start()
+    copies(lambda c: c.start())
+    loader.start()
+    for n in range(count):
+        for axis in range(3):
+
+            @pl.when(where[n, axis] < 0)
+            def _(slot=n * 3 + axis):
+                vols[slot] = jnp.zeros((breadth, width), F32)
+
+    tbuf[...] = jnp.zeros(tbuf.shape, BF16)
+    xbuf[...] = jnp.zeros(xbuf.shape, BF16)
+    copies(lambda c: c.wait())
+    loader.wait((0,))
+    stride = breadth + PAD
+
+    def group_body(group, carry):
+        top = pl.multiple_of(group * rows, 8)
         for n in range(count):
-            for axis in range(3):
-
-                @pl.when(where[n, axis] < 0)
-                def _(slot=n * 3 + axis):
-                    vols[slot] = jnp.zeros((breadth, width), F32)
-
-        tbuf[...] = jnp.zeros(tbuf.shape, BF16)
-        xbuf[...] = jnp.zeros(xbuf.shape, BF16)
-        obuf[...] = jnp.zeros(obuf.shape, F32)
-        copies(lambda c: c.wait())
-        loader.wait((0,))
-
-    top = pl.multiple_of(group * rows, 8)
+            fill(xbuf, 0, vols[n * 3])
+            fill(xbuf, 1, own[n])
+            place(ubuf, 0, n, product(first[pl.ds(top, rows), : 2 * LANES], xbuf[...]))
+            for g, axis in ((1, 2), (2, 1)):
+                fill(xbuf, 0, vols[n * 3 + axis])
+                place(ubuf, g, n, product(first[pl.ds(top, rows), LANES : 2 * LANES], xbuf[:LANES]))
+
+        @pl.when(group == 0)
+        def _():
+            loader.wait((1, 2, 3))
+
+        def emit(q, pair, tile, lane, high, low):
+            step = high.shape[0]
+            row = pl.multiple_of(q * kgroup + pair * step, step)
+            rbuf[tile, pl.ds(row, step), lane : lane + LANES] = high
+            rbuf[tile, pl.ds(row + 2 * kgroup, step), lane : lane + LANES] = low
+            rbuf[tile, pl.ds(row + 4 * kgroup, step), lane : lane + LANES] = high
+
+        recipes = (((0, 2), (0, 2), (0, 1)), ((2, 1), (0, 1), (0, 1)))
+        second_stage(
+            ubuf, lbuf, tbuf, second_high, second_low, group, per, breadth, (1, 0), (1, 0), recipes, emit
+        )
+        for tile in range(count * breadth // 2):
+            total = pick_diagonal(product(third[group], rbuf[tile]), breadth)
+            for d in range(2):
+                row = (tile * 2 + d) * stride
+                old = jnp.where(group == 0, 0.0, obuf[row : row + breadth])
+                obuf[row : row + breadth] = old + total[:, d * LANES : (d + 1) * LANES]
+        return carry
+
+    lax.fori_loop(0, third.shape[0], group_body, 0)
     for n in range(count):
-        fill(xbuf, 0, vols[n * 3])
-        fill(xbuf, 1, own[n])
-        place(ubuf, 0, n, product(first[pl.ds(top, rows), : 2 * LANES], xbuf[...]))
-        for g, axis in ((1, 2), (2, 1)):
-            fill(xbuf, 0, vols[n * 3 + axis])
-            place(ubuf, g, n, product(first[pl.ds(top, rows), LANES : 2 * LANES], xbuf[:LANES]))
-
-    @pl.when(group == 0)
-    def _():
-        loader.wait((1, 2, 3))
-
-    def emit(q, pair, tile, lane, high, low):
-        step = high.shape[0]
-        row = pl.multiple_of(q * kgroup + pair * step, step)
-        rbuf[tile, pl.ds(row, step), lane : lane + LANES] = high
-        rbuf[tile, pl.ds(row + 2 * kgroup, step), lane : lane + LANES] = low
-
-    second_stage(
-        ubuf, lbuf, tbuf, second_high, second_low, group, per, breadth, (1, 0), (((0, 0), (1, 1)), ((2, 0),)), emit
-    )
-
-    def tile_body(tile, carry):
-        wide = product(third[group], rbuf[tile, : 2 * kgroup])
-        wide = wide[:LANES] + wide[LANES:] + product(third[group, :LANES], rbuf[tile, 2 * kgroup :])
-        total = pick_diagonal(wide, breadth)
-        for d in range(2):
-            row = pl.multiple_of((tile * 2 + d) * breadth, breadth)
-            obuf[pl.ds(row, breadth), :] = obuf[pl.ds(row, breadth), :] + total[:, d * LANES : (d + 1) * LANES]
-        return carry
-
-    lax.fori_loop(0, count * breadth // 2, tile_body, 0, unroll=True)
-
-    @pl.when(group == pl.num_programs(0) - 1)
-    def _():
-        for n in range(count):
-
-            def store(a, lane, value, n=n):
-                out[n, a : a + 8, lane : lane + LANES] = value
-
-            turn_block(obuf, n * breadth * breadth, breadth, store)
+
+        def store(a, lane, value, n=n):
+            out[n, a : a + 8, lane : lane + LANES] = value
+
+        turn_block(obuf, n * breadth * stride, breadth, store)
 
 
 def spread_kernel(where, own, *refs):
@@ -284,82 +286,72 @@
     per = rows // breadth
     kgroup = per * breadth * breadth // LANES
     half_slots = keep.shape[0]
-    group = pl.program_id(0)
-
-    @pl.when(group == 0)
-    def _():
-        loader.start()
-        keep[...] = jnp.zeros(keep.shape, F32)
-        send[...] = jnp.zeros(send.shape, F32)
-        tbuf[...] = jnp.zeros(tbuf.shape, BF16)
-        xbuf[...] = jnp.zeros(xbuf.shape, BF16)
-        obuf[...] = jnp.zeros(obuf.shape, F32)
-        loader.wait((0,))
-
-    top = pl.multiple_of(group * rows, 8)
+    loader.start()
+    keep[...] = jnp.zeros(keep.shape, F32)
+    send[...] = jnp.zeros(send.shape, F32)
+    tbuf[...] = jnp.zeros(tbuf.shape, BF16)
+    xbuf[...] = jnp.zeros(xbuf.shape, BF16)
+    loader.wait((0,))
+    stride = breadth + PAD
+
+    def group_body(group, carry):
+        top = pl.multiple_of(group * rows, 8)
+        for n in range(count):
+            fill(xbuf, 0, own[n])
+            for g in range(2):
+                place(ubuf, g, n, product(first[pl.ds(top, rows), (1 + g) * LANES : (2 + g) * LANES], xbuf[...]))
+
+        @pl.when(group == 0)
+        def _():
+            loader.wait((1, 2, 3))
+
+        def emit(q, pair, tile, lane, high, low):
+            step = high.shape[0]
+            row = pl.multiple_of(q * 3 * kgroup + pair * step, step)
+            rbuf[tile, pl.ds(row, step), lane : lane + LANES] = high
+            rbuf[tile, pl.ds(row + kgroup, step), lane : lane + LANES] = low
+            rbuf[tile, pl.ds(row + 2 * kgroup, step), lane : lane + LANES] = high
+
+        recipes = (((1, 1), (0, 1), (0, 1)), ((0, 1), (0, 1), (0, 2)))
+        second_stage(
+            ubuf, lbuf, tbuf, second_high, second_low, group, per, breadth, (1, 2), (0, 1), recipes, emit
+        )
+        for tile in range(count * breadth // 2):
+            for q in range(3):
+                wide = product(third[group, 1 if q == 1 else 0], rbuf[tile, q * 3 * kgroup : (q + 1) * 3 * kgroup])
+                total = pick_diagonal(wide, breadth)
+                for d in range(2):
+                    row = (tile * 2 + d) * stride
+                    old = jnp.where(group == 0, 0.0, obuf[q, row : row + breadth])
+                    obuf[q, row : row + breadth] = old + total[:, d * LANES : (d + 1) * LANES]
+        return carry
+
+    lax.fori_loop(0, third.shape[0], group_body, 0)
     for n in range(count):
-        fill(xbuf, 0, own[n])
-        for g in range(2):
-            place(ubuf, g, n, product(first[pl.ds(top, rows), (1 + g) * LANES : (2 + g) * LANES], xbuf[...]))
-
-    @pl.when(group == 0)
-    def _():
-        loader.wait((1, 2, 3))
-
-    def emit(q, pair, tile, lane, high, low):
-        step = high.shape[0]
-        row = pl.multiple_of(q * 3 * kgroup + pair * step, step)
-        rbuf[tile, pl.ds(row, step), lane : lane + LANES] = high
-        rbuf[tile, pl.ds(row + kgroup, step), lane : lane + LANES] = low
-        rbuf[tile, pl.ds(row + 2 * kgroup, step), lane : lane + LANES] = high
-
-    recipes = (((1, 0),), ((0, 0),), ((0, 1),))
-    second_stage(ubuf, lbuf, tbuf, second_high, second_low, group, per, breadth, (1, 2), recipes, emit)
-
-    def tile_body(tile, carry):
         for q in range(3):
-            wide = product(third[group, 1 if q == 1 else 0], rbuf[tile, q * 3 * kgroup : (q + 1) * 3 * kgroup])
-            total = pick_diagonal(wide, breadth)
-            for d in range(2):
-                row = pl.multiple_of((tile * 2 + d) * breadth, breadth)
-                obuf[q, pl.ds(row, breadth), :] = (
-                    obuf[q, pl.ds(row, breadth), :] + total[:, d * LANES : (d + 1) * LANES]
-                )
-        return carry
-
-    lax.fori_loop(0, count * breadth // 2, tile_body, 0, unroll=True)
-
-    @pl.when(group == pl.num_programs(0) - 1)
-    def _():
-        for n in range(count):
-            for q in range(3):
-
-                def store(a, lane, value):
-                    block[a : a + 8, lane : lane + LANES] = value
-
-                turn_block(obuf.at[q], n * breadth * breadth, breadth, store)
-                slot = where[n, q]
-
-                @pl.when((slot >= 0) & (slot < half_slots))
-                def _(slot=slot):
-                    keep[slot] = keep[slot] + block[...]
-
-                @pl.when(slot >= half_slots)
-                def _(slot=slot):
-                    send[slot - half_slots] = send[slot - half_slots] + block[...]
-
-
-def whole_spec(array):
-    return pl.BlockSpec(array.shape, lambda i, w, rank=len(array.shape): (0,) * rank)
-
-
-def stage_scratch(volumes, recipes, thick, count, breadth, width, per):
+
+            def store(a, lane, value):
+                block[a : a + 8, lane : lane + LANES] = value
+
+            turn_block(obuf.at[q], n * breadth * stride, breadth, store)
+            slot = where[n, q]
+
+            @pl.when((slot >= 0) & (slot < half_slots))
+            def _(slot=slot):
+                keep[slot] = keep[slot] + block[...]
+
+            @pl.when(slot >= half_slots)
+            def _(slot=slot):
+                send[slot - half_slots] = send[slot - half_slots] + block[...]
+
+
+def stage_scratch(volumes, spots, recipes, count, breadth, per):
     hi_count = breadth * breadth // LANES
     return [
         pltpu.VMEM((volumes, count, hi_count, per * breadth + PAD, LANES), F32),
-        pltpu.VMEM((2, volumes, breadth * hi_count, 2 * LANES), BF16),
-        pltpu.VMEM((2, 2, 2 * LANES, 2 * LANES), BF16),
-        pltpu.VMEM((count * breadth // 2, recipes * thick * per * hi_count, 2 * LANES), BF16),
+        pltpu.VMEM((2, count * breadth * hi_count, volumes * 2 * LANES), BF16),
+        pltpu.VMEM((2, spots[0] * 2 * LANES, spots[1] * 2 * LANES), BF16),
+        pltpu.VMEM((count * breadth // 2, recipes * 3 * per * hi_count, 2 * LANES), BF16),
     ]
 
 
@@ -367,7 +359,7 @@
     return pl.CostEstimate(flops=units * per * 2 * count * breadth**4 * 200, transcendentals=0, bytes_accessed=1 << 22)
 
 
-def stage_call(kernel, name, where, own, extra, extra_specs, weights, third, groups, out_shapes, scratch, units):
+def stage_call(kernel, name, where, own, extra, weights, third, groups, out_shapes, scratch, units):
     first, second_high, second_low = weights
     breadth = own.shape[1]
     terms = second_high.shape[0]
@@ -375,18 +367,14 @@
     return pl.pallas_call(
         kernel,
         out_shape=out_shapes,
-        grid_spec=pltpu.PrefetchScalarGridSpec(
-            num_scalar_prefetch=1,
-            grid=(groups,),
-            in_specs=[whole_spec(own)]
-            + extra_specs
-            + [pl.BlockSpec(memory_space=pltpu.HBM)] * 4,
-            out_specs=[whole_spec(shape) for shape in out_shapes],
-            scratch_shapes=[pltpu.VMEM(array.shape, BF16) for array in (first, second_high, second_low, third)]
-            + [pltpu.SemaphoreType.DMA((4,))]
-            + scratch,
-        ),
-        compiler_params=pltpu.CompilerParams(dimension_semantics=("arbitrary",), vmem_limit_bytes=30 << 20),
+        in_specs=[pl.BlockSpec(memory_space=pltpu.SMEM), pl.BlockSpec(memory_space=pltpu.VMEM)]
+        + [pl.BlockSpec(memory_space=pl.ANY)] * len(extra)
+        + [pl.BlockSpec(memory_space=pltpu.HBM)] * 4,
+        out_specs=[pl.BlockSpec(memory_space=pltpu.VMEM)] * len(out_shapes),
+        scratch_shapes=[pltpu.VMEM(array.shape, BF16) for array in (first, second_high, second_low, third)]
+        + [pltpu.SemaphoreType.DMA((4,))]
+        + scratch,
+        compiler_params=pltpu.CompilerParams(vmem_limit_bytes=36 << 20),
         cost_estimate=cost(own.shape[0], breadth, terms, units),
         name=name,
     )(where, own, *extra, *[pltpu.with_memory_space_constraint(w, pltpu.HBM) for w in (first, second_high, second_low, third)])
@@ -395,11 +383,11 @@
 def merge_call(where, own, parts, weights, third, groups):
     count, breadth, width = own.shape
     per = weights[1].shape[0] // groups
-    scratch = stage_scratch(3, 2, 2, count, breadth, width, per)
+    scratch = stage_scratch(3, (2, 1), 2, count, breadth, per)
     scratch = (
         [pltpu.VMEM((count * 3, breadth, width), F32), pltpu.VMEM((2 * LANES, width), BF16)]
         + scratch
-        + [pltpu.VMEM((count * breadth * breadth, LANES), F32), pltpu.SemaphoreType.DMA((count * 3,))]
+        + [pltpu.VMEM((count * breadth * (breadth + PAD), LANES), F32), pltpu.SemaphoreType.DMA((count * 3,))]
     )
     return stage_call(
         functools.partial(merge_kernel, parts=len(parts)),
@@ -407,7 +395,6 @@
         where,
         own,
         list(parts),
-        [pl.BlockSpec(memory_space=pl.ANY)] * len(parts),
         weights,
         third,
         groups,
@@ -420,11 +407,11 @@
 def spread_call(where, own, slots, weights, third, groups):
     count, breadth, width = own.shape
     per = weights[1].shape[0] // groups
-    scratch = stage_scratch(2, 3, 3, count, breadth, width, per)
+    scratch = stage_scratch(2, (1, 2), 3, count, breadth, per)
     scratch = (
         [pltpu.VMEM((LANES, width), BF16)]
         + scratch
-        + [pltpu.VMEM((3, count * breadth * breadth, LANES), F32), pltpu.VMEM((breadth, width), F32)]
+        + [pltpu.VMEM((3, count * breadth * (breadth + PAD), LANES), F32), pltpu.VMEM((breadth, width), F32)]
     )
     shape = jax.ShapeDtypeStruct((slots // 2, breadth, width), F32)
     return stage_call(
@@ -432,7 +419,6 @@
         "spread",
         where,
         own,
-        [],
         [],
         weights,
         third,
@@ -681,7 +667,7 @@
             jax.ShapeDtypeStruct((terms * breadth, 3 * LANES), BF16),
             jax.ShapeDtypeStruct((terms, 3, breadth, LANES), BF16),
             jax.ShapeDtypeStruct((terms, 3, breadth, LANES), BF16),
-            jax.ShapeDtypeStruct((groups, 2 * LANES, 2 * per * hi_count), BF16),
+            jax.ShapeDtypeStruct((groups, LANES, 6 * per * hi_count), BF16),
             jax.ShapeDtypeStruct((groups, 2, LANES, 3 * per * hi_count), BF16),
         ],
         compiler_params=pltpu.CompilerParams(vmem_limit_bytes=14 << 20),

time: 93.7 us -> 88.2 us (0.941)
  Pallas kernels: 45.4 us -> 39.8 us
    pallas_call x2, Pallas kernels: 34.9 us -> 29.1 us  [stage_call(): pl.pallas_call(kernel, out_shape=out_shapes, in_specs=[pl.BlockSpec(memor...]
  transfers between devices with their start and end apart: 8 -> 8, of which waited for: 2 -> 3; matrix products, arithmetic and copies ran while one was open for 7% -> 7% of each run, Pallas kernels for 40% -> 36%
where the time goes in v6:
time: 88.2 us; the launch traced here: 87.7 us
  Pallas kernels  39.8 us (45%)
  blocking collectives  19.5 us (22%)
  starting transfers between devices  13.8 us (16%)
  local copies, waits for them, and re-layouts  9.13 us (10%)
  waiting for transfers between devices  4.55 us (5%)
  other arithmetic  0.9 us (1%)
    pallas_call x2, Pallas kernels, stage_call(): pl.pallas_call(kernel, out_shape=out_shapes, in_specs=[pl.BlockSpec(memor...  29.1 us
    all_to_all x1, blocking collectives, local(): lax.all_to_all(results, 'row', split_axis=0, concat_axis=0, tiled=True)  19.5 us
    all_to_all x1, starting transfers between devices, local(): got = lax.all_to_all(sent, 'row', split_axis=0, concat_axis=0, tiled=True)  7.28 us
    ppermute x7, starting transfers between devices, moved(): return lax.ppermute(array, ('row', 'col'), pairs)  6.52 us
    unnamed x17, local copies, waits for them, and re-layouts  6.43 us
    all_to_all x1, waiting for transfers between devices, local(): got = lax.all_to_all(sent, 'row', split_axis=0, concat_axis=0, tiled=True)  3.16 us
    pallas_call x1, Pallas kernels, local(): vmem_call(unfilter_kernel, (runs, capacity, volume), [((3 * count * bread...  2.91 us
    reshape x1, local copies, waits for them, and re-layouts, local(): kernel_ops.reshape(terms * 9 * breadth, breadth)  2.6 us
  transfers between devices with their start and end apart: 8, of which 3 were waited for; matrix products, arithmetic and copies ran while one was open for 7% of the time, Pallas kernels for 36%

profile of v6, /device:TPU:0, one launch (start us, length us, event | category | flops | bytes accessed | tf_op | source)
XLA Modules:
  0.0 87.7 jit_solution(1518420645002981480)
XLA Ops:
  0.0 0.0 copy-start
  0.0 2.2 %pack.1 = f32[8,4,4224]{2,1,0:T(4,128)} custom-call(s32[1,16]{1,0:T(1,128)} %bitcast.1, f32[16,4096]{1,0:T(8,128)} %fine.1), custom_call_target="tpu_custom_call" | custom-call | tf_op jit(solution)/shard_map/pack/pallas_call | solution.py:659
  2.2 7.3 %all-to-all-start = ((f32[8,4,4224]{2,1,0:T(4,128)}), f32[8,4,4224]{2,1,0:T(4,128)S(1)}, u32[]{:S(2)}, u32[]{:S(2)}) async-start(f32[8,4,4224]{2,1,0:T(4,128)} %pack.1), calls=%async_computation | async-start | bytes 1081344 | tf_op jit(solution)/shard_map/all_to_all | solution.py:662
  9.4 0.0 copy-done
  9.5 0.1 slice.15
  9.6 2.6 %copy.7 = f32[20,3,3,1024]{3,2,1,0:T(4,128)} copy(f32[20,3,3,1024]{3,0,2,1:T(8,128)} %param.9) | data formatting | bytes 1474560 | tf_op args[4]
  12.2 0.0 copy-start.1
  12.2 2.6 %reshape.7.ops = f32[5760,32]{1,0:T(8,128)S(1)} reshape(f32[20,3,3,1024]{3,2,1,0:T(4,128)} %copy.7) | data formatting | bytes 1474560 | tf_op jit(solution)/shard_map/reshape | solution.py:675
  14.8 2.5 %prepare.1 = (bf16[640,384]{1,0:T(8,128)(2,1)S(1)}, bf16[20,3,32,128]{3,2,1,0:T(8,128)(2,1)S(1)}, bf16[20,3,32,128]{3,2,1,0:T(8,128)(2,1)S(1)}, bf16[2,128,480]{...) custom-call(f32[5760,32]{1,0:T(8,128)S(1)} %reshape.7.ops), custom_call_target="tpu_custom_call" | custom-call | tf_op jit(solution)/shard_map/prepare/pallas_call | solution.py:664
  17.3 0.0 copy-start.3
  17.3 0.8 copy-done.3
  18.1 0.0 copy-start.4
  18.1 0.8 copy-done.4
  18.9 0.0 copy-start.5
  18.9 0.8 copy-done.5
  19.7 0.0 copy-start.6
  19.7 0.7 copy-done.6
  20.4 0.0 copy-start.7
  20.4 0.7 copy-done.7
  21.1 3.2 %all-to-all-done.got = f32[8,4,4224]{2,1,0:T(4,128)S(1)} async-done(((f32[8,4,4224]{2,1,0:T(4,128)}), f32[8,4,4224]{2,1,0:T(4,128)S(1)}, u32[]{:S(2)}, u32[]{:S(2)}) %all-to-all-start) | async-done | bytes 540704 | tf_op jit(solution)/shard_map/all_to_all | solution.py:662
  24.3 0.0 copy-done.1
  24.3 2.0 %filter.1.own = f32[2,32,1024]{2,1,0:T(8,128)S(1)} custom-call(f32[8,4,4224]{2,1,0:T(4,128)S(1)} %all-to-all-done.got, f32[32,32]{1,0:T(8,128)S(1)} %copy-done.1), custom_call_target="tpu_custom_call" | custom-call | tf_op jit(solution)/shard_map/filter/pallas_call | solution.py:685
  26.2 2.4 %collective-permute-start = (f32[2,32,1024]{2,1,0:T(8,128)S(1)}, f32[2,32,1024]{2,1,0:T(8,128)S(1)}, u32[]{:S(2)}, u32[]{:S(2)}) collective-permute-start(f32[2,32,1024]{2,1,0:T(8,128)S(1)} %filter.1.own), channel_id=1, source_target_pairs={{0,28},{1,29},{2,30},{3,31},{4,0},{5,1},{6,2},{7,3},{8,4},{9,5},{1... | collective-permute-start | bytes 786440 | tf_op jit(solution)/shard_map/ppermute | solution.py:638
  28.7 1.2 %collective-permute-start.1 = (f32[2,32,1024]{2,1,0:T(8,128)S(1)}, f32[2,32,1024]{2,1,0:T(8,128)S(1)}, u32[]{:S(2)}, u32[]{:S(2)}) collective-permute-start(f32[2,32,1024]{2,1,0:T(8,128)S(1)} %filter.1.own), channel_id=1, source_target_pairs={{0,30},{1,31},{2,28},{3,29},{4,2},{5,3},{6,0},{7,1},{8,6},{9,7},{1... | collective-permute-start | bytes 786440 | tf_op jit(solution)/shard_map/ppermute | solution.py:638
  29.9 14.5 %spread.1 = (f32[4,32,1024]{2,1,0:T(8,128)S(1)}, f32[4,32,1024]{2,1,0:T(8,128)S(1)}) custom-call(s32[2,3]{1,0:T(2,128)S(1)} %compare_select_fusion.2.where, f32[2,32,1024]{2,1,0:T(8,128)S(1)} %filter.1.own, bf16[640,384]{1,0:T(8,128)(2,1)} %copy-done.3, bf16[20,3,32,128]{3,2,1,0:T(8,128)(2,1)} %copy-done.4, bf16[20,3,32,128]{3,2,1,0:T(8,128)(2,1)} %copy-done.5, ...), custom_call_target="tpu_custom_call" | custom-call | flops 134217728000 | bytes 4194304 | tf_op jit(solution)/shard_map/spread/pallas_call | solution.py:367
  44.5 0.0 collective-permute-done.refs_0_
  44.5 0.0 collective-permute-done.1.refs_1_
  44.5 0.1 collective-permute-start.4
  44.6 0.5 collective-permute-start.2
  45.1 0.1 collective-permute-start.3
  45.1 1.3 %collective-permute-done.4 = f32[4,32,1024]{2,1,0:T(8,128)S(1)} collective-permute-done((f32[4,32,1024]{2,1,0:T(8,128)S(1)}, f32[4,32,1024]{2,1,0:T(8,128)S(1)}, u32[]{:S(2)}, u32[]{:S(2)}) %collective-permute-start.4) | collective-permute-done | bytes 524320 | tf_op jit(solution)/shard_map/ppermute | solution.py:638
  46.5 0.9 slice_add_fusion
  47.3 1.7 %collective-permute-start.5 = (f32[2,32,1024]{2,1,0:T(8,128)}, f32[2,32,1024]{2,1,0:T(8,128)}, u32[]{:S(2)}, u32[]{:S(2)}) collective-permute-start(f32[2,32,1024]{2,1,0:T(8,128)} %get-tuple-element.28), channel_id=1, source_target_pairs={{0,4},{1,5},{2,6},{3,7},{4,8},{5,9},{6,10},{7,11},{8,12},{9,13},{1... | collective-permute-start | bytes 786440 | tf_op jit(solution)/shard_map/ppermute | solution.py:638
  49.0 0.5 collective-permute-start.6
  49.5 0.0 collective-permute-done.2.refs_2_
  49.5 0.0 collective-permute-done.3.refs_3_
  49.5 0.0 copy-start.2
  49.5 14.6 %merge.1.refs_0_ = f32[2,32,1024]{2,1,0:T(8,128)S(1)} custom-call(s32[2,3]{1,0:T(2,128)S(1)} %compare_select_fusion.2.where, f32[2,32,1024]{2,1,0:T(8,128)S(1)} %filter.1.own, f32[2,32,1024]{2,1,0:T(8,128)S(1)} %collective-permute-done.refs_0_, f32[2,32,1024]{2,1,0:T(8,128)S(1)} %collective-permute-done.1.refs_1_, ...), custom_call_target="tpu_custom_call" | custom-call | flops 150994944000 | bytes 4194304 | tf_op jit(solution)/shard_map/merge/pallas_call | solution.py:367
  64.1 0.0 collective-permute-done.5.refs_1_
  64.1 0.1 collective-permute-done.6.refs_2_
  64.2 2.9 %unfilter.1 = f32[8,4,4096]{2,1,0:T(4,128)S(1)} custom-call(f32[8,4,4224]{2,1,0:T(4,128)S(1)} %all-to-all-done.got, f32[32,32]{1,0:T(8,128)S(1)} %copy-done.1, f32[2,32,1024]{2,1,0:T(8,128)S(1)} %merge.1.refs_0_, f32[2,32,1024]{2,1,0:T(8,128)} %collective-permute-done.5.refs_1_, f32[2,32,1024]{2,1,0:T(8,128)} %collective-permute-done.6.refs_2_), custom_call_target="tpu_custom_call" | custom-call | tf_op jit(solution)/shard_map/unfilter/pallas_call | solution.py:710
  67.1 19.5 %all_to_all.10.back = f32[8,4,4096]{2,1,0:T(4,128)S(1)} all-to-all(f32[8,4,4096]{2,1,0:T(4,128)S(1)} %unfilter.1), channel_id=1, replica_groups=mesh['row'=8,'col'=4] {'row'}, dimensions={0} | all-to-all | bytes 1048576 | tf_op jit(solution)/shard_map/all_to_all | solution.py:727
  86.6 0.0 copy-done.2
  86.6 1.2 %unpack.1 = f32[16,4096]{1,0:T(8,128)} custom-call(s32[1,16]{1,0:T(1,128)S(1)} %bitcast.2, f32[8,4,4096]{2,1,0:T(4,128)S(1)} %all_to_all.10.back), custom_call_target="tpu_custom_call" | custom-call | tf_op jit(solution)/shard_map/unpack/pallas_call | solution.py:728
  (2 shorter events, 0.0 us)
Async XLA Ops:
  0.0 9.4 %copy-start = (s32[8,6]{1,0:T(8,128)S(1)}, s32[8,6]{1,0:T(8,128)}, u32[]{:S(2)}) copy-start(s32[8,6]{1,0:T(8,128)} %param.7) | copy-start | bytes 580
  2.2 22.1 %all-to-all-start = ((f32[8,4,4224]{2,1,0:T(4,128)}), f32[8,4,4224]{2,1,0:T(4,128)S(1)}, u32[]{:S(2)}, u32[]{:S(2)}) async-start(f32[8,4,4224]{2,1,0:T(4,128)} %pack.1), calls=%async_computation | async-start | bytes 1081344 | tf_op jit(solution)/shard_map/all_to_all | solution.py:662
  12.2 12.1 %copy-start.1 = (f32[32,32]{1,0:T(8,128)S(1)}, f32[32,32]{1,0:T(8,128)}, u32[]{:S(2)}) copy-start(f32[32,32]{1,0:T(8,128)} %filter_ref.3) | copy-start | bytes 12292
  17.3 0.8 copy-start.3
  18.1 0.8 copy-start.4
  18.9 0.8 copy-start.5
  19.7 0.7 copy-start.6
  20.4 0.7 copy-start.7
  26.2 18.2 %collective-permute-start = (f32[2,32,1024]{2,1,0:T(8,128)S(1)}, f32[2,32,1024]{2,1,0:T(8,128)S(1)}, u32[]{:S(2)}, u32[]{:S(2)}) collective-permute-start(f32[2,32,1024]{2,1,0:T(8,128)S(1)} %filter.1.own), channel_id=1, source_target_pairs={{0,28},{1,29},{2,30},{3,31},{4,0},{5,1},{6,2},{7,3},{8,4},{9,5},{1... | collective-permute-start | bytes 786440 | tf_op jit(solution)/shard_map/ppermute | solution.py:638
  28.7 15.8 %collective-permute-start.1 = (f32[2,32,1024]{2,1,0:T(8,128)S(1)}, f32[2,32,1024]{2,1,0:T(8,128)S(1)}, u32[]{:S(2)}, u32[]{:S(2)}) collective-permute-start(f32[2,32,1024]{2,1,0:T(8,128)S(1)} %filter.1.own), channel_id=1, source_target_pairs={{0,30},{1,31},{2,28},{3,29},{4,2},{5,3},{6,0},{7,1},{8,6},{9,7},{1... | collective-permute-start | bytes 786440 | tf_op jit(solution)/shard_map/ppermute | solution.py:638
  44.5 2.0 %collective-permute-start.4 = (f32[4,32,1024]{2,1,0:T(8,128)S(1)}, f32[4,32,1024]{2,1,0:T(8,128)S(1)}, u32[]{:S(2)}, u32[]{:S(2)}) collective-permute-start(f32[4,32,1024]{2,1,0:T(8,128)S(1)} %get-tuple-element.26), channel_id=1, source_target_pairs={{0,1},{1,0},{2,3},{3,2},{4,5},{5,4},{6,7},{7,6},{8,9},{9,8},{10,11... | collective-permute-start | bytes 1572872 | tf_op jit(solution)/shard_map/ppermute | solution.py:638
  44.6 5.0 %collective-permute-start.2 = (f32[2,32,1024]{2,1,0:T(8,128)S(1)}, f32[2,32,1024]{2,1,0:T(8,128)S(1)}, u32[]{:S(2)}, u32[]{:S(2)}) collective-permute-start(f32[2,32,1024]{2,1,0:T(8,128)S(1)} %collective-permute-done.refs_0_), channel_id=1, source_target_pairs={{0,1},{1,0},{2,3},{3,2},{4,5},{5,4},{6,7},{7,6},{8,9},{9,8},{10,11... | collective-permute-start | bytes 786440 | tf_op jit(solution)/shard_map/ppermute | solution.py:638
  45.1 4.5 %collective-permute-start.3 = (f32[2,32,1024]{2,1,0:T(8,128)S(1)}, f32[2,32,1024]{2,1,0:T(8,128)S(1)}, u32[]{:S(2)}, u32[]{:S(2)}) collective-permute-start(f32[2,32,1024]{2,1,0:T(8,128)S(1)} %collective-permute-done.1.refs_1_), channel_id=1, source_target_pairs={{0,1},{1,0},{2,3},{3,2},{4,5},{5,4},{6,7},{7,6},{8,9},{9,8},{10,11... | collective-permute-start | bytes 786440 | tf_op jit(solution)/shard_map/ppermute | solution.py:638
  47.3 16.8 %collective-permute-start.5 = (f32[2,32,1024]{2,1,0:T(8,128)}, f32[2,32,1024]{2,1,0:T(8,128)}, u32[]{:S(2)}, u32[]{:S(2)}) collective-permute-start(f32[2,32,1024]{2,1,0:T(8,128)} %get-tuple-element.28), channel_id=1, source_target_pairs={{0,4},{1,5},{2,6},{3,7},{4,8},{5,9},{6,10},{7,11},{8,12},{9,13},{1... | collective-permute-start | bytes 786440 | tf_op jit(solution)/shard_map/ppermute | solution.py:638
  49.0 15.2 %collective-permute-start.6 = (f32[2,32,1024]{2,1,0:T(8,128)}, f32[2,32,1024]{2,1,0:T(8,128)}, u32[]{:S(2)}, u32[]{:S(2)}) collective-permute-start(f32[2,32,1024]{2,1,0:T(8,128)} %get-tuple-element.27), channel_id=1, source_target_pairs={{0,6},{1,7},{2,4},{3,5},{4,10},{5,11},{6,8},{7,9},{8,14},{9,15},{1... | collective-permute-start | bytes 786440 | tf_op jit(solution)/shard_map/ppermute | solution.py:638
  49.5 37.0 %copy-start.2 = (s32[16]{0:T(128)S(1)}, s32[16]{0:T(128)}, u32[]{:S(2)}) copy-start(s32[16]{0:T(128)} %param.6) | copy-start | bytes 196

commit v7 on v6

--- a/solution.py
+++ b/solution.py
@@ -441,7 +441,7 @@
     return jnp.sum(jnp.where(diagonal, row, 0.0), axis=1, keepdims=True)
 
 
-def place_row(slot_row, runs, run_size, capacity):
+def place_row(slot_row, runs, run_size, capacity, row=None):
     held = slot_row.shape[1]
     run_row = jnp.zeros(slot_row.shape, F32)
     for r in range(1, runs):
@@ -449,6 +449,9 @@
     same = to_column(run_row) == run_row
     earlier = iota((held, held), 0) < iota((held, held), 1)
     before = jnp.sum(jnp.where(same & earlier, 1.0, 0.0), axis=0, keepdims=True)
+    if row is not None:
+        run_row = row.astype(F32) - run_row
+        run_row = jnp.where(run_row < 0.0, run_row + runs, run_row)
     return run_row * capacity + before
 
 
@@ -473,14 +476,17 @@
         out[r, :, volume:] = ids[r * capacity : (r + 1) * capacity]
 
 
-def unpack_kernel(slot_row, back, out, stack, *, run_size):
+def unpack_kernel(row, slot_row, *refs, run_size):
+    backs = refs[:-2]
+    out, stack = refs[-2:]
     held, volume = out.shape
-    runs, capacity = back.shape[:2]
+    runs = len(backs)
+    capacity = backs[0].shape[0]
     places = runs * capacity
-    place = to_column(place_row(slot_row[...], runs, run_size, capacity))
+    place = to_column(place_row(slot_row[...], runs, run_size, capacity, row[0]))
     hit = iota((held, places), 1).astype(F32) == place
     one = jnp.where(hit, 1.0, 0.0).astype(BF16)
-    rest = jnp.concatenate([back[r] for r in range(runs)], axis=0)
+    rest = jnp.concatenate([back[...] for back in backs], axis=0)
     for part in range(3):
         head = rest.astype(BF16)
         stack[part * places : (part + 1) * places] = head
@@ -566,10 +572,12 @@
         out[n] = result[n * breadth : (n + 1) * breadth]
 
 
-def unfilter_kernel(got, filter_ref, *refs, count, pieces):
+def unfilter_kernel(row, got, filter_ref, *refs, count, pieces):
     applied = refs[:pieces]
-    out, weave, cross, stack = refs[pieces:]
-    runs, capacity, volume = out.shape
+    runs = got.shape[0]
+    outs = refs[pieces : pieces + runs]
+    weave, cross, stack = refs[pieces + runs :]
+    capacity, volume = outs[0].shape
     places = runs * capacity
     breadth = filter_ref.shape[0]
     half = breadth // 2
@@ -605,23 +613,23 @@
             high, low = split(both)
             stack[g * 8 : g * 8 + 16, i * face : (i + 1) * face] = high
             stack[32 + g * 8 : 32 + g * 8 + 16, i * face : (i + 1) * face] = low
-    ids = jnp.concatenate([got[r] for r in range(runs)], axis=0)
+    ids = jnp.concatenate([got[(row[0] + k) % runs] for k in range(runs)], axis=0)
     code = child_code(ids[:, :1], 8 * count)
     hit = row_code(iota((places, 32), 1), count) == code
     one = jnp.where(hit, 1.0, 0.0).astype(BF16)
     packed = product(jnp.concatenate([one, one], axis=1), stack[...])
-    for r in range(runs):
-        out[r] = packed[r * capacity : (r + 1) * capacity]
-
-
-def vmem_call(kernel, out_shape, scratch, name, in_specs=None, room=14, **settings):
-    extra = {} if in_specs is None else dict(grid=(1,), in_specs=in_specs)
-    if in_specs is not None:
-        rank = len(out_shape)
-        extra["out_specs"] = pl.BlockSpec(out_shape, lambda i: (0,) * rank)
+    for k in range(runs):
+        outs[k][...] = packed[k * capacity : (k + 1) * capacity]
+
+
+def vmem_call(kernel, out_shape, scratch, name, in_specs=None, room=14, outputs=1, **settings):
+    extra = {} if in_specs is None else dict(in_specs=in_specs)
+    shapes = jax.ShapeDtypeStruct(out_shape, F32)
+    if outputs > 1:
+        shapes = [shapes] * outputs
     return pl.pallas_call(
         functools.partial(kernel, **settings),
-        out_shape=jax.ShapeDtypeStruct(out_shape, F32),
+        out_shape=shapes,
         scratch_shapes=[pltpu.VMEM(shape, dtype) for shape, dtype in scratch],
         compiler_params=pltpu.CompilerParams(vmem_limit_bytes=room << 20),
         name=name,
@@ -706,26 +714,32 @@
         at = u // 2 * count
         terms_out.append(moved(keep[at : at + count] + came[at : at + count], 1, u))
     pieces = [merge_call(where, filtered, parts, weights, merge_third, groups)] + terms_out
-    tail = volume // LANES
+    row = jnp.full((1,), lax.axis_index("row"), jnp.int32)
+    scalar = pl.BlockSpec(memory_space=pltpu.SMEM)
+    plain = pl.BlockSpec(memory_space=pltpu.VMEM)
     results = vmem_call(
         unfilter_kernel,
-        (runs, capacity, volume),
+        (capacity, volume),
         [
             ((3 * count * breadth, width), BF16),
             ((2, width, width), BF16),
             ((64, volume), BF16),
         ],
         "unfilter",
-        in_specs=[
-            pl.BlockSpec((runs, capacity, LANES), lambda i: (0, 0, tail)),
-            pl.BlockSpec((breadth, breadth), lambda i: (0, 0)),
-        ]
-        + [pl.BlockSpec((count, breadth, width), lambda i: (0, 0, 0))] * len(pieces),
+        in_specs=[scalar] + [plain] * (2 + len(pieces)),
+        outputs=runs,
         count=count,
         pieces=len(pieces),
-    )(got, filter_matrix, *pieces)
-    back = lax.all_to_all(results, "row", split_axis=0, concat_axis=0, tiled=True)
-    return vmem_call(unpack_kernel, (held, volume), [((3 * places, volume), BF16)], "unpack", **routing)(slot_row, back)
+    )(row, got[:, :, volume:], filter_matrix, *pieces)
+    backs = [results[0]] + [moved(results[k], k, 0) for k in range(1, runs)]
+    return vmem_call(
+        unpack_kernel,
+        (held, volume),
+        [((3 * places, volume), BF16)],
+        "unpack",
+        in_specs=[scalar, plain] + [plain] * runs,
+        **routing,
+    )(row, slot_row, *backs)
 
 
 def solution(mesh):

time: 88.2 us -> 85.6 us (0.971)
  blocking collectives: 19.5 us -> 0 us
  starting transfers between devices: 13.8 us -> 25 us
  waiting for transfers between devices: 4.55 us -> 10.4 us
    all_to_all x1 -> x0, blocking collectives: 19.5 us -> none  [local(): lax.all_to_all(results, 'row', split_axis=0, concat_axis=0, tiled=True)]
    ppermute x7 -> x14, starting transfers between devices: 6.52 us -> 17.7 us  [moved(): return lax.ppermute(array, ('row', 'col'), pairs)]
    ppermute x7 -> x14, waiting for transfers between devices: 1.39 us -> 7.28 us  [moved(): return lax.ppermute(array, ('row', 'col'), pairs)]
  transfers between devices with their start and end apart: 8 -> 15, of which waited for: 3 -> 7; matrix products, arithmetic and copies ran while one was open for 7% -> 7% of each run, Pallas kernels for 36% -> 37%
where the time goes in v7:
time: 85.6 us; the launch traced here: 85.2 us
  Pallas kernels  39.6 us (46%)
  starting transfers between devices  25 us (29%)
  waiting for transfers between devices  10.4 us (12%)
  local copies, waits for them, and re-layouts  9.15 us (11%)
  other arithmetic  0.89 us (1%)
    pallas_call x2, Pallas kernels, stage_call(): pl.pallas_call(kernel, out_shape=out_shapes, in_specs=[pl.BlockSpec(memor...  28.9 us
    ppermute x14, starting transfers between devices, moved(): return lax.ppermute(array, ('row', 'col'), pairs)  17.7 us
    all_to_all x1, starting transfers between devices, local(): got = lax.all_to_all(sent, 'row', split_axis=0, concat_axis=0, tiled=True)  7.28 us
    ppermute x14, waiting for transfers between devices, moved(): return lax.ppermute(array, ('row', 'col'), pairs)  7.28 us
    unnamed x17, local copies, waits for them, and re-layouts  6.44 us
    all_to_all x1, waiting for transfers between devices, local(): got = lax.all_to_all(sent, 'row', split_axis=0, concat_axis=0, tiled=True)  3.14 us
    pallas_call x1, Pallas kernels, local(): vmem_call(unfilter_kernel, (capacity, volume), [((3 * count * breadth, wi...  2.92 us
    reshape x1, local copies, waits for them, and re-layouts, local(): kernel_ops.reshape(terms * 9 * breadth, breadth)  2.6 us
  transfers between devices with their start and end apart: 15, of which 7 were waited for; matrix products, arithmetic and copies ran while one was open for 7% of the time, Pallas kernels for 37%

profile of v7, /device:TPU:0, one launch (start us, length us, event | category | flops | bytes accessed | tf_op | source)
XLA Modules:
  0.0 85.2 jit_solution(1665817638281851075)
XLA Ops:
  0.0 0.0 copy-start
  0.0 2.2 %pack.1 = f32[8,4,4224]{2,1,0:T(4,128)} custom-call(s32[1,16]{1,0:T(1,128)} %bitcast.2, f32[16,4096]{1,0:T(8,128)} %fine.1), custom_call_target="tpu_custom_call" | custom-call | tf_op jit(solution)/shard_map/pack/pallas_call | solution.py:667
  2.2 7.3 %all-to-all-start = ((f32[8,4,4224]{2,1,0:T(4,128)}), f32[8,4,4224]{2,1,0:T(4,128)S(1)}, u32[]{:S(2)}, u32[]{:S(2)}) async-start(f32[8,4,4224]{2,1,0:T(4,128)} %pack.1), calls=%async_computation | async-start | bytes 1081344 | tf_op jit(solution)/shard_map/all_to_all | solution.py:670
  9.4 0.0 copy-done
  9.5 0.1 slice.19
  9.6 2.7 %copy.7 = f32[20,3,3,1024]{3,2,1,0:T(4,128)} copy(f32[20,3,3,1024]{3,0,2,1:T(8,128)} %param.9) | data formatting | bytes 1474560 | tf_op args[4]
  12.2 0.0 copy-start.1
  12.2 2.6 %reshape.7.ops = f32[5760,32]{1,0:T(8,128)S(1)} reshape(f32[20,3,3,1024]{3,2,1,0:T(4,128)} %copy.7) | data formatting | bytes 1474560 | tf_op jit(solution)/shard_map/reshape | solution.py:683
  14.8 2.5 %prepare.1 = (bf16[640,384]{1,0:T(8,128)(2,1)S(1)}, bf16[20,3,32,128]{3,2,1,0:T(8,128)(2,1)S(1)}, bf16[20,3,32,128]{3,2,1,0:T(8,128)(2,1)S(1)}, bf16[2,128,480]{...) custom-call(f32[5760,32]{1,0:T(8,128)S(1)} %reshape.7.ops), custom_call_target="tpu_custom_call" | custom-call | tf_op jit(solution)/shard_map/prepare/pallas_call | solution.py:672
  17.3 0.0 copy-start.3
  17.3 0.8 copy-done.3
  18.1 0.0 copy-start.4
  18.1 0.8 copy-done.4
  18.9 0.0 copy-start.5
  18.9 0.8 copy-done.5
  19.7 0.0 copy-start.6
  19.7 0.7 copy-done.6
  20.4 0.0 copy-start.7
  20.4 0.7 copy-done.7
  21.1 3.1 %all-to-all-done.got = f32[8,4,4224]{2,1,0:T(4,128)S(1)} async-done(((f32[8,4,4224]{2,1,0:T(4,128)}), f32[8,4,4224]{2,1,0:T(4,128)S(1)}, u32[]{:S(2)}, u32[]{:S(2)}) %all-to-all-start) | async-done | bytes 540704 | tf_op jit(solution)/shard_map/all_to_all | solution.py:670
  24.3 0.0 copy-done.1
  24.3 2.0 %filter.1.own = f32[2,32,1024]{2,1,0:T(8,128)S(1)} custom-call(f32[8,4,4224]{2,1,0:T(4,128)S(1)} %all-to-all-done.got, f32[32,32]{1,0:T(8,128)S(1)} %copy-done.1), custom_call_target="tpu_custom_call" | custom-call | tf_op jit(solution)/shard_map/filter/pallas_call | solution.py:693
  26.3 2.4 %collective-permute-start = (f32[2,32,1024]{2,1,0:T(8,128)S(1)}, f32[2,32,1024]{2,1,0:T(8,128)S(1)}, u32[]{:S(2)}, u32[]{:S(2)}) collective-permute-start(f32[2,32,1024]{2,1,0:T(8,128)S(1)} %filter.1.own), channel_id=1, source_target_pairs={{0,28},{1,29},{2,30},{3,31},{4,0},{5,1},{6,2},{7,3},{8,4},{9,5},{1... | collective-permute-start | bytes 786440 | tf_op jit(solution)/shard_map/ppermute | solution.py:646
  28.7 1.2 %collective-permute-start.1 = (f32[2,32,1024]{2,1,0:T(8,128)S(1)}, f32[2,32,1024]{2,1,0:T(8,128)S(1)}, u32[]{:S(2)}, u32[]{:S(2)}) collective-permute-start(f32[2,32,1024]{2,1,0:T(8,128)S(1)} %filter.1.own), channel_id=1, source_target_pairs={{0,30},{1,31},{2,28},{3,29},{4,2},{5,3},{6,0},{7,1},{8,6},{9,7},{1... | collective-permute-start | bytes 786440 | tf_op jit(solution)/shard_map/ppermute | solution.py:646
  29.9 14.5 %spread.1 = (f32[4,32,1024]{2,1,0:T(8,128)S(1)}, f32[4,32,1024]{2,1,0:T(8,128)S(1)}) custom-call(s32[2,3]{1,0:T(2,128)S(1)} %compare_select_fusion.2.where, f32[2,32,1024]{2,1,0:T(8,128)S(1)} %filter.1.own, bf16[640,384]{1,0:T(8,128)(2,1)} %copy-done.3, bf16[20,3,32,128]{3,2,1,0:T(8,128)(2,1)} %copy-done.4, bf16[20,3,32,128]{3,2,1,0:T(8,128)(2,1)} %copy-done.5, ...), custom_call_target="tpu_custom_call" | custom-call | flops 134217728000 | bytes 4194304 | tf_op jit(solution)/shard_map/spread/pallas_call | solution.py:367
  44.4 0.0 collective-permute-done.refs_0_
  44.4 0.0 collective-permute-done.1.refs_1_
  44.4 0.1 collective-permute-start.4
  44.5 0.5 collective-permute-start.2
  45.0 0.1 collective-permute-start.3
  45.1 1.3 %collective-permute-done.4 = f32[4,32,1024]{2,1,0:T(8,128)S(1)} collective-permute-done((f32[4,32,1024]{2,1,0:T(8,128)S(1)}, f32[4,32,1024]{2,1,0:T(8,128)S(1)}, u32[]{:S(2)}, u32[]{:S(2)}) %collective-permute-start.4) | collective-permute-done | bytes 524320 | tf_op jit(solution)/shard_map/ppermute | solution.py:646
  46.4 0.9 %slice_add_fusion = (f32[2,32,1024]{2,1,0:T(8,128)}, f32[2,32,1024]{2,1,0:T(8,128)}) fusion(f32[4,32,1024]{2,1,0:T(8,128)S(1)} %collective-permute-done.4, f32[4,32,1024]{2,1,0:T(8,128)S(1)} %get-tuple-element.33), kind=kLoop, calls=%fused_computation | loop fusion | flops 131072 | bytes 1572864 | tf_op jit(solution)/shard_map/add | solution.py:715
  47.3 1.8 %collective-permute-start.5 = (f32[2,32,1024]{2,1,0:T(8,128)}, f32[2,32,1024]{2,1,0:T(8,128)}, u32[]{:S(2)}, u32[]{:S(2)}) collective-permute-start(f32[2,32,1024]{2,1,0:T(8,128)} %get-tuple-element.44), channel_id=1, source_target_pairs={{0,4},{1,5},{2,6},{3,7},{4,8},{5,9},{6,10},{7,11},{8,12},{9,13},{1... | collective-permute-start | bytes 786440 | tf_op jit(solution)/shard_map/ppermute | solution.py:646
  49.0 0.5 collective-permute-start.6
  49.5 0.0 collective-permute-done.2.refs_2_
  49.5 0.0 collective-permute-done.3.refs_3_
  49.5 0.0 copy-start.2
  49.5 14.4 %merge.1.refs_0_ = f32[2,32,1024]{2,1,0:T(8,128)S(1)} custom-call(s32[2,3]{1,0:T(2,128)S(1)} %compare_select_fusion.2.where, f32[2,32,1024]{2,1,0:T(8,128)S(1)} %filter.1.own, f32[2,32,1024]{2,1,0:T(8,128)S(1)} %collective-permute-done.refs_0_, f32[2,32,1024]{2,1,0:T(8,128)S(1)} %collective-permute-done.1.refs_1_, ...), custom_call_target="tpu_custom_call" | custom-call | flops 150994944000 | bytes 4194304 | tf_op jit(solution)/shard_map/merge/pallas_call | solution.py:367
  64.0 0.0 collective-permute-done.5.refs_1_
  64.0 0.2 collective-permute-done.6.refs_2_
  64.2 2.9 %unfilter.1 = (f32[4,4096]{1,0:T(4,128)S(1)}, f32[4,4096]{1,0:T(4,128)S(1)}, f32[4,4096]{1,0:T(4,128)S(1)}, f32[4,4096]{1,0:T(4,128)S(1)}, f32[4,4096]{1,0:T(4,1...) custom-call(s32[1]{0:T(128)} %bitcast.row, f32[8,4,128]{2,1,0:T(4,128)S(1)} %slice.24.got, ...), custom_call_target="tpu_custom_call" | custom-call | tf_op jit(solution)/shard_map/unfilter/pallas_call | solution.py:720
  67.1 0.1 collective-permute-start.10
  67.2 3.7 %collective-permute-start.11 = (f32[4,4096]{1,0:T(4,128)S(1)}, f32[4,4096]{1,0:T(4,128)S(1)}, u32[]{:S(2)}, u32[]{:S(2)}) collective-permute-start(f32[4,4096]{1,0:T(4,128)S(1)} %get-tuple-element.40), channel_id=1, source_target_pairs={{0,20},{1,21},{2,22},{3,23},{4,24},{5,25},{6,26},{7,27},{8,28},{9,... | collective-permute-start | bytes 196616 | tf_op jit(solution)/shard_map/ppermute | solution.py:646
  71.0 3.4 %collective-permute-start.12 = (f32[4,4096]{1,0:T(4,128)S(1)}, f32[4,4096]{1,0:T(4,128)S(1)}, u32[]{:S(2)}, u32[]{:S(2)}) collective-permute-start(f32[4,4096]{1,0:T(4,128)S(1)} %get-tuple-element.41), channel_id=1, source_target_pairs={{0,24},{1,25},{2,26},{3,27},{4,28},{5,29},{6,30},{7,31},{8,0},{9,1... | collective-permute-start | bytes 196616 | tf_op jit(solution)/shard_map/ppermute | solution.py:646
  74.4 0.3 collective-permute-start.13
  74.7 1.7 %collective-permute-start.7 = (f32[4,4096]{1,0:T(4,128)S(1)}, f32[4,4096]{1,0:T(4,128)S(1)}, u32[]{:S(2)}, u32[]{:S(2)}) collective-permute-start(f32[4,4096]{1,0:T(4,128)S(1)} %get-tuple-element.36), channel_id=1, source_target_pairs={{0,4},{1,5},{2,6},{3,7},{4,8},{5,9},{6,10},{7,11},{8,12},{9,13},{1... | collective-permute-start | bytes 196616 | tf_op jit(solution)/shard_map/ppermute | solution.py:646
  76.4 0.0 collective-permute-done.10.refs_4_
  76.4 0.0 collective-permute-start.8
  76.4 0.0 collective-permute-done.11.refs_5_
  76.4 1.9 %collective-permute-start.9 = (f32[4,4096]{1,0:T(4,128)S(1)}, f32[4,4096]{1,0:T(4,128)S(1)}, u32[]{:S(2)}, u32[]{:S(2)}) collective-permute-start(f32[4,4096]{1,0:T(4,128)S(1)} %get-tuple-element.38), channel_id=1, source_target_pairs={{0,12},{1,13},{2,14},{3,15},{4,16},{5,17},{6,18},{7,19},{8,20},{9,... | collective-permute-start | bytes 196616 | tf_op jit(solution)/shard_map/ppermute | solution.py:646
  78.3 0.0 collective-permute-done.12.refs_6_
  78.3 1.1 %collective-permute-done.13.refs_7_ = f32[4,4096]{1,0:T(4,128)S(1)} collective-permute-done((f32[4,4096]{1,0:T(4,128)S(1)}, f32[4,4096]{1,0:T(4,128)S(1)}, u32[]{:S(2)}, u32[]{:S(2)}) %collective-permute-start.13) | collective-permute-done | bytes 65568 | tf_op jit(solution)/shard_map/ppermute | solution.py:646
  79.4 2.2 %collective-permute-done.7.refs_1_ = f32[4,4096]{1,0:T(4,128)S(1)} collective-permute-done((f32[4,4096]{1,0:T(4,128)S(1)}, f32[4,4096]{1,0:T(4,128)S(1)}, u32[]{:S(2)}, u32[]{:S(2)}) %collective-permute-start.7) | collective-permute-done | bytes 65568 | tf_op jit(solution)/shard_map/ppermute | solution.py:646
  81.7 0.8 collective-permute-done.8.refs_2_
  82.5 1.5 %collective-permute-done.9.refs_3_ = f32[4,4096]{1,0:T(4,128)S(1)} collective-permute-done((f32[4,4096]{1,0:T(4,128)S(1)}, f32[4,4096]{1,0:T(4,128)S(1)}, u32[]{:S(2)}, u32[]{:S(2)}) %collective-permute-start.9) | collective-permute-done | bytes 65568 | tf_op jit(solution)/shard_map/ppermute | solution.py:646
  84.1 0.0 copy-done.2
  84.1 1.2 %unpack.1 = f32[16,4096]{1,0:T(8,128)} custom-call(s32[1]{0:T(128)} %bitcast.row, s32[1,16]{1,0:T(1,128)S(1)} %bitcast.3, f32[4,4096]{1,0:T(4,128)S(1)} %get-tuple-element.35.refs_0_, f32[4,4096]{1,0:T(4,128)S(1)} %collective-permute-done.7.refs_1_, f32[4,4096]{1,0:T(4,128)S(1)} %collective-permute-done.8.refs_2_, ...), custom_call_target="tpu_custom_call" | custom-call | tf_op jit(solution)/shard_map/unpack/pallas_call | solution.py:735
  (3 shorter events, 0.0 us)
Async XLA Ops:
  0.0 9.4 %copy-start = (s32[8,6]{1,0:T(8,128)S(1)}, s32[8,6]{1,0:T(8,128)}, u32[]{:S(2)}) copy-start(s32[8,6]{1,0:T(8,128)} %param.7) | copy-start | bytes 580
  2.2 22.1 %all-to-all-start = ((f32[8,4,4224]{2,1,0:T(4,128)}), f32[8,4,4224]{2,1,0:T(4,128)S(1)}, u32[]{:S(2)}, u32[]{:S(2)}) async-start(f32[8,4,4224]{2,1,0:T(4,128)} %pack.1), calls=%async_computation | async-start | bytes 1081344 | tf_op jit(solution)/shard_map/all_to_all | solution.py:670
  12.2 12.1 %copy-start.1 = (f32[32,32]{1,0:T(8,128)S(1)}, f32[32,32]{1,0:T(8,128)}, u32[]{:S(2)}) copy-start(f32[32,32]{1,0:T(8,128)} %filter_ref.3) | copy-start | bytes 12292
  17.3 0.8 copy-start.3
  18.1 0.8 copy-start.4
  18.9 0.8 copy-start.5
  19.7 0.7 copy-start.6
  20.4 0.7 copy-start.7
  26.3 18.2 %collective-permute-start = (f32[2,32,1024]{2,1,0:T(8,128)S(1)}, f32[2,32,1024]{2,1,0:T(8,128)S(1)}, u32[]{:S(2)}, u32[]{:S(2)}) collective-permute-start(f32[2,32,1024]{2,1,0:T(8,128)S(1)} %filter.1.own), channel_id=1, source_target_pairs={{0,28},{1,29},{2,30},{3,31},{4,0},{5,1},{6,2},{7,3},{8,4},{9,5},{1... | collective-permute-start | bytes 786440 | tf_op jit(solution)/shard_map/ppermute | solution.py:646
  28.7 15.8 %collective-permute-start.1 = (f32[2,32,1024]{2,1,0:T(8,128)S(1)}, f32[2,32,1024]{2,1,0:T(8,128)S(1)}, u32[]{:S(2)}, u32[]{:S(2)}) collective-permute-start(f32[2,32,1024]{2,1,0:T(8,128)S(1)} %filter.1.own), channel_id=1, source_target_pairs={{0,30},{1,31},{2,28},{3,29},{4,2},{5,3},{6,0},{7,1},{8,6},{9,7},{1... | collective-permute-start | bytes 786440 | tf_op jit(solution)/shard_map/ppermute | solution.py:646
  44.4 2.0 %collective-permute-start.4 = (f32[4,32,1024]{2,1,0:T(8,128)S(1)}, f32[4,32,1024]{2,1,0:T(8,128)S(1)}, u32[]{:S(2)}, u32[]{:S(2)}) collective-permute-start(f32[4,32,1024]{2,1,0:T(8,128)S(1)} %get-tuple-element.34), channel_id=1, source_target_pairs={{0,1},{1,0},{2,3},{3,2},{4,5},{5,4},{6,7},{7,6},{8,9},{9,8},{10,11... | collective-permute-start | bytes 1572872 | tf_op jit(solution)/shard_map/ppermute | solution.py:646
  44.5 5.0 %collective-permute-start.2 = (f32[2,32,1024]{2,1,0:T(8,128)S(1)}, f32[2,32,1024]{2,1,0:T(8,128)S(1)}, u32[]{:S(2)}, u32[]{:S(2)}) collective-permute-start(f32[2,32,1024]{2,1,0:T(8,128)S(1)} %collective-permute-done.refs_0_), channel_id=1, source_target_pairs={{0,1},{1,0},{2,3},{3,2},{4,5},{5,4},{6,7},{7,6},{8,9},{9,8},{10,11... | collective-permute-start | bytes 786440 | tf_op jit(solution)/shard_map/ppermute | solution.py:646
  45.0 4.5 %collective-permute-start.3 = (f32[2,32,1024]{2,1,0:T(8,128)S(1)}, f32[2,32,1024]{2,1,0:T(8,128)S(1)}, u32[]{:S(2)}, u32[]{:S(2)}) collective-permute-start(f32[2,32,1024]{2,1,0:T(8,128)S(1)} %collective-permute-done.1.refs_1_), channel_id=1, source_target_pairs={{0,1},{1,0},{2,3},{3,2},{4,5},{5,4},{6,7},{7,6},{8,9},{9,8},{10,11... | collective-permute-start | bytes 786440 | tf_op jit(solution)/shard_map/ppermute | solution.py:646
  47.3 16.7 %collective-permute-start.5 = (f32[2,32,1024]{2,1,0:T(8,128)}, f32[2,32,1024]{2,1,0:T(8,128)}, u32[]{:S(2)}, u32[]{:S(2)}) collective-permute-start(f32[2,32,1024]{2,1,0:T(8,128)} %get-tuple-element.44), channel_id=1, source_target_pairs={{0,4},{1,5},{2,6},{3,7},{4,8},{5,9},{6,10},{7,11},{8,12},{9,13},{1... | collective-permute-start | bytes 786440 | tf_op jit(solution)/shard_map/ppermute | solution.py:646
  49.0 15.2 %collective-permute-start.6 = (f32[2,32,1024]{2,1,0:T(8,128)}, f32[2,32,1024]{2,1,0:T(8,128)}, u32[]{:S(2)}, u32[]{:S(2)}) collective-permute-start(f32[2,32,1024]{2,1,0:T(8,128)} %get-tuple-element.43), channel_id=1, source_target_pairs={{0,6},{1,7},{2,4},{3,5},{4,10},{5,11},{6,8},{7,9},{8,14},{9,15},{1... | collective-permute-start | bytes 786440 | tf_op jit(solution)/shard_map/ppermute | solution.py:646
  49.5 34.5 %copy-start.2 = (s32[16]{0:T(128)S(1)}, s32[16]{0:T(128)}, u32[]{:S(2)}) copy-start(s32[16]{0:T(128)} %param.6) | copy-start | bytes 196
  67.1 9.3 %collective-permute-start.10 = (f32[4,4096]{1,0:T(4,128)S(1)}, f32[4,4096]{1,0:T(4,128)S(1)}, u32[]{:S(2)}, u32[]{:S(2)}) collective-permute-start(f32[4,4096]{1,0:T(4,128)S(1)} %get-tuple-element.39), channel_id=1, source_target_pairs={{0,16},{1,17},{2,18},{3,19},{4,20},{5,21},{6,22},{7,23},{8,24},{9,... | collective-permute-start | bytes 196616 | tf_op jit(solution)/shard_map/ppermute | solution.py:646
  67.2 9.2 %collective-permute-start.11 = (f32[4,4096]{1,0:T(4,128)S(1)}, f32[4,4096]{1,0:T(4,128)S(1)}, u32[]{:S(2)}, u32[]{:S(2)}) collective-permute-start(f32[4,4096]{1,0:T(4,128)S(1)} %get-tuple-element.40), channel_id=1, source_target_pairs={{0,20},{1,21},{2,22},{3,23},{4,24},{5,25},{6,26},{7,27},{8,28},{9,... | collective-permute-start | bytes 196616 | tf_op jit(solution)/shard_map/ppermute | solution.py:646
  71.0 7.4 %collective-permute-start.12 = (f32[4,4096]{1,0:T(4,128)S(1)}, f32[4,4096]{1,0:T(4,128)S(1)}, u32[]{:S(2)}, u32[]{:S(2)}) collective-permute-start(f32[4,4096]{1,0:T(4,128)S(1)} %get-tuple-element.41), channel_id=1, source_target_pairs={{0,24},{1,25},{2,26},{3,27},{4,28},{5,29},{6,30},{7,31},{8,0},{9,1... | collective-permute-start | bytes 196616 | tf_op jit(solution)/shard_map/ppermute | solution.py:646
  74.4 5.0 %collective-permute-start.13 = (f32[4,4096]{1,0:T(4,128)S(1)}, f32[4,4096]{1,0:T(4,128)S(1)}, u32[]{:S(2)}, u32[]{:S(2)}) collective-permute-start(f32[4,4096]{1,0:T(4,128)S(1)} %get-tuple-element.42), channel_id=1, source_target_pairs={{0,28},{1,29},{2,30},{3,31},{4,0},{5,1},{6,2},{7,3},{8,4},{9,5},{1... | collective-permute-start | bytes 196616 | tf_op jit(solution)/shard_map/ppermute | solution.py:646
  74.7 7.0 %collective-permute-start.7 = (f32[4,4096]{1,0:T(4,128)S(1)}, f32[4,4096]{1,0:T(4,128)S(1)}, u32[]{:S(2)}, u32[]{:S(2)}) collective-permute-start(f32[4,4096]{1,0:T(4,128)S(1)} %get-tuple-element.36), channel_id=1, source_target_pairs={{0,4},{1,5},{2,6},{3,7},{4,8},{5,9},{6,10},{7,11},{8,12},{9,13},{1... | collective-permute-start | bytes 196616 | tf_op jit(solution)/shard_map/ppermute | solution.py:646
  76.4 6.1 %collective-permute-start.8 = (f32[4,4096]{1,0:T(4,128)S(1)}, f32[4,4096]{1,0:T(4,128)S(1)}, u32[]{:S(2)}, u32[]{:S(2)}) collective-permute-start(f32[4,4096]{1,0:T(4,128)S(1)} %get-tuple-element.37), channel_id=1, source_target_pairs={{0,8},{1,9},{2,10},{3,11},{4,12},{5,13},{6,14},{7,15},{8,16},{9,17... | collective-permute-start | bytes 196616 | tf_op jit(solution)/shard_map/ppermute | solution.py:646
  76.4 7.6 %collective-permute-start.9 = (f32[4,4096]{1,0:T(4,128)S(1)}, f32[4,4096]{1,0:T(4,128)S(1)}, u32[]{:S(2)}, u32[]{:S(2)}) collective-permute-start(f32[4,4096]{1,0:T(4,128)S(1)} %get-tuple-element.38), channel_id=1, source_target_pairs={{0,12},{1,13},{2,14},{3,15},{4,16},{5,17},{6,18},{7,19},{8,20},{9,... | collective-permute-start | bytes 196616 | tf_op jit(solution)/shard_map/ppermute | solution.py:646
